TPU v7x, 512 devices: a whole 4x8x8 slice. The times are simulated.
512 devices in a mesh: grp: 8 (over y), dev: 64 (over z, x, core).
Axes of the slice: x: 4, y: 8, z: 8, core: 2. Of those that a mesh axis runs over, the one named last changes fastest.
Arguments:
- leaf_right: float32 [32, 131072], P(None, ('grp', 'dev')), may hold values from -6 to 6
- leaf_inverse: float32 [1024, 128, 128], P(('grp', 'dev')), may hold values from -1 to 2, as said below
- leaf_link: float32 [1024, 128, 128], P(('grp', 'dev')), may hold values from -0.25 to 0.25
- leaf_front: float32 [1024, 128, 128], P(('grp', 'dev')), may hold values from -0.1875 to 0.1875
- parents: int32 [1024], P(('grp', 'dev')), may hold values from 1 to 2, as said below
- front_rows: int32 [1024], P(('grp', 'dev')), may hold values from 0 to 15
- live_blocks: int32 [512], P(('grp', 'dev')), may hold values from 1 to 2, 896 in all
- front_right: float32 [32, 16384], P(None, ('grp', 'dev')), may hold values from -6 to 6
- front_inverse: float32 [16384, 2048], P(('grp', 'dev')), may hold values from -1 to 2, as said below
- front_couple: float32 [16384, 4096], P(('grp', 'dev')), may hold values from -0.046875 to 0.046875
- root_right: float32 [32, 2, 2048], P(None, None, 'dev'), may hold values from -6 to 6
- root_inverse: float32 [2, 2048, 2048], P(None, 'dev', 'grp'), may hold values from -1 to 2, as said below
- root_couple: float32 [1, 2048, 2048], P(None, 'dev', 'grp'), may hold values from -0.09375 to 0.09375
Outputs:
- leaf_solution: float32 [32, 131072], P(None, ('grp', 'dev'))
- front_solution: float32 [32, 16384], P(None, 'grp')
- root_solution: float32 [32, 2, 2048], P(None, None, 'dev')
Inputs may be any that keep to these rules, and one draw needn't show every extreme that they name: For local block k = b mod 2, parents[b] lies in k + 1 .. 2; the value 2 means no parent among the piece's blocks. A piece's live blocks are its first live_blocks[p]; some piece has all 2. `leaf_inverse`: each block is lower triangular with a positive diagonal. `front_inverse`: each front's block is lower triangular with a positive diagonal. `root_inverse`: each level's block is lower triangular with a positive diagonal.
All inputs are finite; a program needn't handle non-finite values.
Results may differ from a plain program's by a relative error of at most 0.0003.
Values sent between devices are 32-bit elements; how exact they have to be, the bound alone decides.
No kernel may reach another device: no remote copies, remote signals or barrier semaphores. Data moves between devices by JAX's collectives and lax.ppermute only.
A program may use at most 64 MiB of HBM per device.

v0:
```python
import jax
import jax.numpy as jnp
from jax import lax
from jax.sharding import PartitionSpec as P

EXACT_ARITHMETIC = lax.Precision.HIGHEST


def front_table(targets, blocks_front):
    return (targets[:, None] == jnp.arange(blocks_front, dtype=jnp.int32)[None, :]).astype(
        jnp.float32
    )


def piece_forward(right_side, inverse, linked, parents, live_count, upper_bound):
    total_blocks = inverse.shape[0]

    def advance(member, loop_state):
        pending, solved = loop_state
        is_alive = member < live_count
        residual = lax.dynamic_index_in_dim(
            right_side, member, 1, False
        ) - lax.dynamic_index_in_dim(pending, member, 1, False)
        solved_block = jnp.where(
            is_alive, jnp.dot(residual, inverse[member], precision=EXACT_ARITHMETIC), 0.0
        )
        solved = lax.dynamic_update_index_in_dim(solved, solved_block, member, 1)
        target = parents[member]
        target_slot = jnp.minimum(target, total_blocks - 1)
        update = jnp.where(
            target < live_count,
            jnp.dot(solved_block, linked[member], precision=EXACT_ARITHMETIC),
            0.0,
        )
        current = lax.dynamic_index_in_dim(pending, target_slot, 1, False)
        pending = lax.dynamic_update_index_in_dim(pending, current + update, target_slot, 1)
        return (pending, solved)

    empty_state = jnp.zeros_like(right_side)
    return lax.fori_loop(0, upper_bound, advance, (empty_state, empty_state))[1]


def piece_backward(base_terms, inverse, linked, parents, live_count, upper_bound):
    total_blocks = inverse.shape[0]

    def retreat(turn_index, solved):
        member = upper_bound - 1 - turn_index
        is_alive = member < live_count
        target = parents[member]
        target_slot = jnp.minimum(target, total_blocks - 1)
        parent_value = lax.dynamic_index_in_dim(solved, target_slot, 1, False)
        carried = jnp.where(
            target < live_count,
            jnp.einsum("rn,mn->rm", parent_value, linked[member], precision=EXACT_ARITHMETIC),
            0.0,
        )
        residual = lax.dynamic_index_in_dim(base_terms, member, 1, False) - carried
        solved_block = jnp.where(
            is_alive,
            jnp.einsum("rn,mn->rm", residual, inverse[member], precision=EXACT_ARITHMETIC),
            0.0,
        )
        return lax.dynamic_update_index_in_dim(solved, solved_block, member, 1)

    return lax.fori_loop(0, upper_bound, retreat, jnp.zeros_like(base_terms))


def front_update(solved, coupled, targets, blocks_front):
    contrib = jnp.einsum("rkn,knm->rkm", solved, coupled, precision=EXACT_ARITHMETIC)
    table = front_table(targets, blocks_front)
    placed = jnp.einsum("rkm,kf->rfm", contrib, table, precision=EXACT_ARITHMETIC)
    return placed.reshape(solved.shape[0], -1)


def front_back(front_values, coupled, targets, blocks_front):
    table = front_table(targets, blocks_front)
    grouped = front_values.reshape(front_values.shape[0], blocks_front, -1)
    picked = jnp.einsum("rfn,kf->rkn", grouped, table, precision=EXACT_ARITHMETIC)
    return jnp.einsum("rkn,kmn->rkm", picked, coupled, precision=EXACT_ARITHMETIC)


def body(
    leaf_right,
    leaf_inverse,
    leaf_link,
    leaf_front,
    parents,
    front_rows,
    live_blocks,
    front_right,
    front_inverse,
    front_couple,
    root_right,
    root_inverse,
    root_couple,
):
    columns = leaf_right.shape[0]
    blocks_here = leaf_inverse.shape[0]
    block_width = leaf_inverse.shape[1]
    front_order = front_inverse.shape[1]
    blocks_front = front_order // block_width
    levels = root_right.shape[1]
    share_width = root_right.shape[2]
    live_count = live_blocks[0]
    right_side = leaf_right.reshape(columns, blocks_here, block_width)
    solved = piece_forward(right_side, leaf_inverse, leaf_link, parents, live_count, live_count)
    partial_front = front_update(solved, leaf_front, front_rows, blocks_front)
    front_share = lax.psum_scatter(partial_front, "dev", scatter_dimension=1, tiled=True)
    front_terms = jnp.dot(front_right - front_share, front_inverse, precision=EXACT_ARITHMETIC)
    forward_front_sweep = lax.psum_scatter(front_terms, "dev", scatter_dimension=1, tiled=True)
    raised_values = jnp.dot(forward_front_sweep, front_couple, precision=EXACT_ARITHMETIC).reshape(
        columns, levels, -1
    )
    summed = lax.psum(raised_values, ("grp", "dev"))
    pending = lax.dynamic_slice_in_dim(summed, lax.axis_index("dev") * share_width, share_width, 2)
    pending_levels = [pending[:, height] for height in range(levels)]
    forward_values = [None] * levels
    for height in reversed(range(levels)):
        residual = root_right[:, height] - pending_levels[height]
        solved_level = lax.psum(
            jnp.dot(residual, root_inverse[height], precision=EXACT_ARITHMETIC), "dev"
        )
        forward_values[height] = solved_level
        if height > 0:
            outgoing = jnp.einsum(
                "rj,mij->rmi", solved_level, root_couple, precision=EXACT_ARITHMETIC
            )
            pushed = lax.psum(outgoing, "grp")
            pending_levels[0] = pending_levels[0] + pushed[:, 0]
    back_values = [None] * levels
    corrections = [jnp.zeros_like(forward_values[0]) for height in range(levels)]
    for height in range(levels):
        residual = forward_values[height] - corrections[height]
        solved_level = lax.psum(
            jnp.einsum("rj,ij->ri", residual, root_inverse[height], precision=EXACT_ARITHMETIC),
            "grp",
        )
        back_values[height] = solved_level
        if height < levels - 1:
            later_levels = list(range(height + 1, levels))
            stacked_blocks = jnp.stack(
                [
                    root_couple[upper_level * (upper_level - 1) // 2 + height]
                    for upper_level in later_levels
                ],
                0,
            )
            outgoing = jnp.einsum(
                "ri,kij->rkj", solved_level, stacked_blocks, precision=EXACT_ARITHMETIC
            )
            pushed = lax.psum(outgoing, "dev")
            for offset, upper_level in enumerate(later_levels):
                corrections[upper_level] = pushed[:, offset]
    root_solution = jnp.stack(back_values, 1)
    grouped_couple = front_couple.reshape(front_couple.shape[0], levels, -1)
    lifted_back = jnp.einsum(
        "rlj,flj->rf",
        lax.all_gather(root_solution, "dev", axis=2, tiled=True),
        grouped_couple,
        precision=EXACT_ARITHMETIC,
    )
    backward_remainder = forward_front_sweep - lifted_back
    front_rows_solved = jnp.einsum(
        "rj,ij->ri",
        lax.all_gather(backward_remainder, "dev", axis=1, tiled=True),
        front_inverse,
        precision=EXACT_ARITHMETIC,
    )
    front_solution = lax.all_gather(front_rows_solved, "dev", axis=1, tiled=True)
    base_terms = solved - front_back(front_solution, leaf_front, front_rows, blocks_front)
    leaf_blocks = piece_backward(
        base_terms, leaf_inverse, leaf_link, parents, live_count, live_count
    )
    return (leaf_blocks.reshape(columns, -1), front_solution, root_solution)


def solution(mesh):
    in_specs = (
        P(None, ("grp", "dev")),
        P(("grp", "dev"), None, None),
        P(("grp", "dev"), None, None),
        P(("grp", "dev"), None, None),
        P(("grp", "dev")),
        P(("grp", "dev")),
        P(("grp", "dev")),
        P(None, ("grp", "dev")),
        P(("grp", "dev"), None),
        P(("grp", "dev"), None),
        P(None, None, "dev"),
        P(None, "dev", "grp"),
        P(None, "dev", "grp"),
    )
    out_specs = (P(None, ("grp", "dev")), P(None, "grp"), P(None, None, "dev"))
    return jax.shard_map(body, mesh=mesh, in_specs=in_specs, out_specs=out_specs, check_vma=False)
```

profile of v0, /device:TPU:1, one launch (start us, length us, event | category | flops | bytes accessed | tf_op | source)
XLA Modules:
  0.0 1600.9 jit_solution(14024327891004830132)
XLA Ops:
  7.2 0.8 reshape.34
  8.1 7.2 while.24
  9.5 1.0 bitcast_dynamic-update-slice_fusion.2
  10.5 1.2 dynamic_slice.93
  13.7 1.0 fusion.87
  15.4 0.2 convolution_bitcast_fusion.4
  15.6 0.4 convolution_bitcast_fusion.1
  16.1 1.3 copy.48
  17.4 0.0 reduce-scatter.9.cloned.1.call-start
  17.5 156.0 %reduce-scatter.7.cloned.1.call-done = f32[32,32]{1,0:T(8,128)} async-done(((f32[2048,32]{1,0:T(8,128)}), f32[32,32]{1,0:T(8,128)}) %reduce-scatter.7.cloned.1.call-update) | async-done | bytes 4112
  173.5 0.8 copy.45
  174.3 2.8 convolution_bitcast_fusion
  177.1 0.0 all-reduce.2.cloned.1.call-start
  177.2 147.9 %reduce-scatter.9.cloned.1.call-done = f32[32,32]{1,0:T(8,128)} async-done(((f32[2048,32]{1,0:T(8,128)}), f32[32,32]{1,0:T(8,128)}) %reduce-scatter.9.cloned.1.call-update) | async-done | bytes 4112
  325.1 1.4 fusion.59
  326.5 0.8 copy.74
  328.1 0.1 copy.47
  328.1 277.8 %all-reduce.2.cloned.1.call-done = f32[32,2,2048]{2,0,1:T(8,128)} async-done(((f32[32,2,2048]{2,0,1:T(8,128)}), f32[32,2,2048]{2,0,1:T(8,128)}) %all-reduce.2.cloned.1.call-update) | async-done | bytes 524304 | tf_op jit(solution)/shard_map/psum | solution.py:114
  605.9 0.9 fusion.38
  606.8 243.2 %psum.50 = f32[32,256]{1,0:T(8,128)S(1)} all-reduce(f32[32,256]{1,0:T(8,128)S(1)} %fusion.38), channel_id=1, replica_groups=mesh['grp'=8,'dev'=64] {'dev'}, use_global_device_ids=true, to_apply=%region_5.6 | all-reduce | flops 8192 | bytes 65536 | tf_op jit(solution)/shard_map/psum | solution.py:120
  850.1 0.2 convolution_bitcast_fusion.6
  850.2 23.5 %psum.51 = f32[32,1,32]{2,0,1:T(8,128)S(1)} all-reduce(f32[32,1,32]{2,0,1:T(8,128)S(1)} %convolution_bitcast_fusion.6), channel_id=1, replica_groups=mesh['grp'=8,'dev'=64] {'grp'}, use_global_device_ids=true, to_apply=%region_6.7 | all-reduce | flops 1024 | bytes 8192 | tf_op jit(solution)/shard_map/psum | solution.py:128
  873.7 0.9 fusion.32
  874.6 253.2 %psum.52 = f32[32,256]{1,0:T(8,128)S(1)} all-reduce(f32[32,256]{1,0:T(8,128)S(1)} %fusion.32), channel_id=1, replica_groups=mesh['grp'=8,'dev'=64] {'dev'}, use_global_device_ids=true, to_apply=%region_7.8 | all-reduce | flops 8192 | bytes 65536 | tf_op jit(solution)/shard_map/psum | solution.py:120
  1127.9 0.2 fusion.30
  1128.0 21.0 %psum.53 = f32[32,32]{1,0:T(8,128)S(1)} all-reduce(f32[32,32]{1,0:T(8,128)S(1)} %fusion.30), channel_id=1, replica_groups=mesh['grp'=8,'dev'=64] {'grp'}, use_global_device_ids=true, to_apply=%region_8.9 | all-reduce | flops 1024 | bytes 8192 | tf_op jit(solution)/shard_map/psum | solution.py:134
  1149.0 0.2 fusion.34
  1149.2 252.2 %psum.54 = f32[32,256]{1,0:T(8,128)S(1)} all-reduce(f32[32,256]{1,0:T(8,128)S(1)} %fusion.34), channel_id=1, replica_groups=mesh['grp'=8,'dev'=64] {'dev'}, use_global_device_ids=true, to_apply=%region_9.10 | all-reduce | flops 8192 | bytes 65536 | tf_op jit(solution)/shard_map/psum | solution.py:151
  1401.4 0.2 convolution_bitcast_fusion.5
  1401.6 21.7 %psum.55 = f32[32,1,32]{2,0,1:T(8,128)S(1)} all-reduce(f32[32,1,32]{2,0,1:T(8,128)S(1)} %convolution_bitcast_fusion.5), channel_id=1, replica_groups=mesh['grp'=8,'dev'=64] {'grp'}, use_global_device_ids=true, to_apply=%region_10.11 | all-reduce | flops 1024 | bytes 8192 | tf_op jit(solution)/shard_map/psum | solution.py:134
  1423.2 0.1 copy.32
  1423.3 0.6 copy.41
  1424.0 60.2 %all_gather.9 = f32[32,2,2048]{0,1,2:T(2,128)S(1)} all-gather(f32[32,2,32]{0,1,2:T(2,128)S(1)} %copy.32), channel_id=1, replica_groups=mesh['grp'=8,'dev'=64] {'dev'}, dimensions={2}, use_global_device_ids=true | all-gather | bytes 532480 | tf_op jit(solution)/shard_map/all_gather | solution.py:158
  1484.1 3.4 fusion.25
  1487.5 0.1 copy.35
  1487.6 50.5 %all_gather.10 = f32[32,2048]{0,1:T(8,128)S(1)} all-gather(f32[32,32]{0,1:T(8,128)S(1)} %copy.35), channel_id=1, replica_groups=mesh['grp'=8,'dev'=64] {'dev'}, dimensions={1}, use_global_device_ids=true | all-gather | bytes 266240 | tf_op jit(solution)/shard_map/all_gather | solution.py:165
  1538.1 0.7 fusion.62
  1538.8 47.7 %all_gather.11 = f32[32,2048]{0,1:T(8,128)S(1)} all-gather(f32[32,32]{0,1:T(8,128)S(1)} %fusion.62), channel_id=1, replica_groups=mesh['grp'=8,'dev'=64] {'dev'}, dimensions={1}, use_global_device_ids=true | all-gather | bytes 266240 | tf_op jit(solution)/shard_map/all_gather | solution.py:169
  1586.5 1.0 copy.40
  1587.5 0.3 copy.43
  1587.8 0.3 convolution_bitcast_fusion.3
  1588.1 0.3 fusion.21
  1588.5 5.3 while.25
  1589.2 0.7 dynamic_slice.98
  1591.9 0.2 fusion.92
  1592.8 0.2 convolution_select_fusion.5
  1593.0 0.1 dynamic_update_slice.20
  1593.7 0.6 copy.75
  (36 shorter events, 0.3 us)
Async XLA Ops:
  7.2 167.1 %copy-start = (f32[32,2048]{1,0:T(8,128)S(1)}, f32[32,2048]{1,0:T(8,128)}, u32[]{:S(2)}) copy-start(f32[32,2048]{1,0:T(8,128)} %param.25) | copy-start | bytes 786436
  7.2 8.2 copy-start.4
  7.2 8.4 copy-start.10
  7.2 166.3 %reduce-scatter.7.cloned.1.call-start = ((), (), s32[]{:S(2)}) async-start(), calls=%async_computation.3 | async-start | bytes 1064960
  8.1 166.2 %copy-start.9 = (f32[32,32]{1,0:T(8,128)S(1)}, f32[32,32]{1,0:T(8,128)}, u32[]{:S(2)}) copy-start(f32[32,32]{1,0:T(8,128)} %param.24) | copy-start | bytes 12292
  16.0 309.0 %copy-start.3 = (f32[32,4096]{1,0:T(8,128)S(1)}, f32[32,4096]{1,0:T(8,128)}, u32[]{:S(2)}) copy-start(f32[32,4096]{1,0:T(8,128)} %param.26) | copy-start | bytes 1572868
  17.4 307.6 %reduce-scatter.9.cloned.1.call-start = ((), (), s32[]{:S(2)}) async-start(), calls=%async_computation.4 | async-start | bytes 1064960
  177.1 150.9 %copy-start.8 = (f32[32,2,32]{2,1,0:T(2,128)S(1)}, f32[32,2,32]{2,1,0:T(2,128)}, u32[]{:S(2)}) copy-start(f32[32,2,32]{2,1,0:T(2,128)} %param.27) | copy-start | bytes 24580
  177.1 428.8 %copy-start.5 = (f32[2,32,256]{2,1,0:T(8,128)S(1)}, f32[2,32,256]{2,1,0:T(8,128)}, u32[]{:S(2)}) copy-start(f32[2,32,256]{2,1,0:T(8,128)} %param.28) | copy-start | bytes 196612
  177.1 673.0 %copy-start.6 = (f32[1,32,256]{2,1,0:T(8,128)S(1)}, f32[1,32,256]{2,1,0:T(8,128)}, u32[]{:S(2)}) copy-start(f32[1,32,256]{2,1,0:T(8,128)} %param.29) | copy-start | bytes 98308
  177.1 428.7 %all-reduce.2.cloned.1.call-start = ((), (), s32[]{:S(2)}) async-start(), calls=%async_computation.2 | async-start | bytes 1048576 | tf_op jit(solution)/shard_map/psum | solution.py:114
  325.1 3.0 copy-start.7
  1538.8 49.7 %copy-start.1 = (f32[2,128,128]{2,1,0:T(8,128)S(1)}, f32[2,128,128]{2,1,0:T(8,128)}, u32[]{:S(2)}) copy-start(f32[2,128,128]{2,1,0:T(8,128)} %get-tuple-element.377) | copy-start | bytes 393220
  1538.8 49.7 %copy-start.2 = (f32[2,128,128]{2,1,0:T(8,128)S(1)}, f32[2,128,128]{2,1,0:T(8,128)}, u32[]{:S(2)}) copy-start(f32[2,128,128]{2,1,0:T(8,128)} %get-tuple-element.378) | copy-start | bytes 393220
  1538.8 49.7 %copy-start.11 = (s32[2]{0:T(128)S(1)}, s32[2]{0:T(128)}, u32[]{:S(2)}) copy-start(s32[2]{0:T(128)} %get-tuple-element.384) | copy-start | bytes 28
Sparse Core Ops, SparseCore 0:
  17.5 155.9 reduce-scatter.6
  178.1 146.9 reduce-scatter.8
  330.1 275.7 all-reduce.1
where the time goes:
time: 1610 us; the launch traced here: 1600 us
  blocking collectives  973 us (60%)
  waiting for transfers between devices  582 us (36%)
    psum x2, blocking collectives, body(): lax.psum(jnp.dot(residual, root_inverse[height], precision=EXACT_ARITHMET...  496 us
    unnamed x5, waiting for transfers between devices  304 us
    psum x1, waiting for transfers between devices, body(): summed = lax.psum(raised_values, ('grp', 'dev'))  278 us
    psum x1, blocking collectives, body(): pushed = lax.psum(outgoing, 'dev')  252 us
    all_gather x1, blocking collectives, body(): lax.all_gather(root_solution, 'dev', axis=2, tiled=True)  60.2 us
    all_gather x1, blocking collectives, body(): lax.all_gather(backward_remainder, 'dev', axis=1, tiled=True)  50.5 us
    all_gather x1, blocking collectives, body(): lax.all_gather(front_rows_solved, 'dev', axis=1, tiled=True)  47.7 us
    psum x2, blocking collectives, body(): lax.psum(jnp.einsum('rj,ij->ri', residual, root_inverse[height], precisio...  42.6 us
  transfers between devices with their start and end apart: 3, of which 3 were waited for; matrix products, arithmetic and copies ran while one was open for 0% of the time, Pallas kernels for 0%

commit v1 on v0

v1 whole, which is shorter than its diff:
```python
import jax
import jax.numpy as jnp
from jax import lax
from jax.sharding import Mesh
from jax.sharding import PartitionSpec as P

EXACT = lax.Precision.HIGHEST
NEAR = ("x", "core")
DEV = ("z", "x", "core")


def mm(left, right):
    return jnp.dot(left, right, precision=EXACT)


def mmt(left, right):
    return jnp.einsum("rn,mn->rm", left, right, precision=EXACT)


def swap(chunks, axes):
    return lax.all_to_all(chunks, axes, 0, 0, tiled=True)


def spread(values, axes, count):
    return swap(jnp.broadcast_to(values[None], (count,) + values.shape), axes)


def reduce_over(values, axes, count):
    return jnp.sum(spread(values, axes, count), 0)


def scatter_sum(values, axes, count):
    rows, width = values.shape
    chunks = values.reshape(rows, count, width // count).transpose(1, 0, 2)
    return jnp.sum(swap(chunks, axes), 0)


def gather_columns(values, axes, count):
    rows, width = values.shape
    return spread(values, axes, count).transpose(1, 0, 2).reshape(rows, count * width)


def make_body(sizes):
    n_grp, n_z = sizes["grp"], sizes["z"]
    n_near = sizes["x"] * sizes["core"]
    n_dev = n_z * n_near

    def reduce_dev(values):
        return reduce_over(reduce_over(values, NEAR, n_near), "z", n_z)

    def body(
        leaf_right,
        leaf_inverse,
        leaf_link,
        leaf_front,
        parents,
        front_rows,
        live_blocks,
        front_right,
        front_inverse,
        front_couple,
        root_right,
        root_inverse,
        root_couple,
    ):
        rows = leaf_right.shape[0]
        width = leaf_inverse.shape[1]
        front_order = front_inverse.shape[1]
        n_front = front_order // width
        share = root_right.shape[2]
        live = live_blocks[0]
        has_parent = parents[0] < live
        right0, right1 = leaf_right[:, :width], leaf_right[:, width:]
        solved0 = jnp.where(live > 0, mm(right0, leaf_inverse[0]), 0.0)
        lifted = jnp.where(has_parent, mm(solved0, leaf_link[0]), 0.0)
        solved1 = jnp.where(live > 1, mm(right1 - lifted, leaf_inverse[1]), 0.0)
        given0, given1 = mm(solved0, leaf_front[0]), mm(solved1, leaf_front[1])
        slots = jnp.arange(n_front, dtype=jnp.int32)[None, :, None]
        placed = jnp.where(slots == front_rows[0], given0[:, None, :], 0.0) + jnp.where(
            slots == front_rows[1], given1[:, None, :], 0.0
        )
        update = scatter_sum(placed.reshape(rows, front_order), DEV, n_dev)
        terms = mm(front_right - update, front_inverse)
        y_front = scatter_sum(terms, DEV, n_dev)

        raised = mm(y_front, front_couple).reshape(rows, 2, n_dev, share)
        raised = jnp.sum(swap(raised.transpose(2, 0, 1, 3).reshape(n_dev, rows, 2 * share), DEV), 0)
        raised = reduce_over(raised, "grp", n_grp)
        low = root_right[:, 0] - raised[:, :share]
        high = root_right[:, 1] - raised[:, share:]
        w_low, w_high, link = root_inverse[0], root_inverse[1], root_couple[0]
        y_high = reduce_dev(mm(high, w_high))
        low = low - reduce_over(mmt(y_high, link), "grp", n_grp)
        y_low = reduce_dev(mm(low, w_low))
        x_low = reduce_over(mmt(y_low, w_low), "grp", n_grp)
        y_high = y_high - reduce_dev(mm(x_low, link))
        x_high = reduce_over(mmt(y_high, w_high), "grp", n_grp)

        both = jnp.concatenate([x_low, x_high], 1)
        whole = spread(both, DEV, n_dev).reshape(n_dev, rows, 2, share)
        whole = whole.transpose(1, 2, 0, 3).reshape(rows, 2 * n_dev * share)
        rest = y_front - mmt(whole, front_couple)
        rest = gather_columns(rest, DEV, n_dev)
        front_solution = gather_columns(mmt(rest, front_inverse), DEV, n_dev)

        def back(solved, block):
            start = front_rows[block] * width
            picked = lax.dynamic_slice(front_solution, (0, start), (rows, width))
            return solved - mmt(picked, leaf_front[block])

        base0, base1 = back(solved0, 0), back(solved1, 1)
        leaf1 = jnp.where(live > 1, mmt(base1, leaf_inverse[1]), 0.0)
        carried = jnp.where(has_parent, mmt(leaf1, leaf_link[0]), 0.0)
        leaf0 = jnp.where(live > 0, mmt(base0 - carried, leaf_inverse[0]), 0.0)
        leaf_solution = jnp.concatenate([leaf0, leaf1], 1)
        return leaf_solution, front_solution, jnp.stack([x_low, x_high], 1)

    return body


def solution(mesh):
    n_grp, n_dev = mesh.shape["grp"], mesh.shape["dev"]
    fine = Mesh(mesh.devices.reshape(n_grp, n_dev // 8, 4, 2), ("grp", "z", "x", "core"))
    every = ("grp",) + DEV
    in_specs = (
        P(None, every),
        P(every, None, None),
        P(every, None, None),
        P(every, None, None),
        P(every),
        P(every),
        P(every),
        P(None, every),
        P(every, None),
        P(every, None),
        P(None, None, DEV),
        P(None, DEV, "grp"),
        P(None, DEV, "grp"),
    )
    out_specs = (P(None, every), P(None, "grp"), P(None, None, DEV))
    body = make_body(dict(fine.shape))
    return jax.shard_map(body, mesh=fine, in_specs=in_specs, out_specs=out_specs, check_vma=False)
```

time: 1610 us -> 295 us (0.18)
  blocking collectives: 973 us -> 197 us
  waiting for transfers between devices: 582 us -> 29.7 us
  starting transfers between devices: 0.12 us -> 16.8 us
    psum x6 -> x0, blocking collectives: 815 us -> none  [the longest x2 496 us: body(): lax.psum(jnp.dot(residual, root_inverse[height], precision=EXACT_ARITHMET...]
    unnamed x5 -> x0, waiting for transfers between devices: 304 us -> none
    psum x1 -> x0, waiting for transfers between devices: 278 us -> none  [body(): summed = lax.psum(raised_values, ('grp', 'dev'))]
    all_to_all x0 -> x13, blocking collectives: none -> 197 us  [swap(): return lax.all_to_all(chunks, axes, 0, 0, tiled=True)]
    all_gather x3 -> x0, blocking collectives: 158 us -> none  [the longest x1 60.2 us: body(): lax.all_gather(root_solution, 'dev', axis=2, tiled=True)]
    all_to_all x0 -> x3, waiting for transfers between devices: none -> 29.7 us  [swap(): return lax.all_to_all(chunks, axes, 0, 0, tiled=True)]
    all_to_all x0 -> x3, starting transfers between devices: none -> 16.8 us  [swap(): return lax.all_to_all(chunks, axes, 0, 0, tiled=True)]
  transfers between devices with their start and end apart: 3 -> 3, of which waited for: 3 -> 3; matrix products, arithmetic and copies ran while one was open for 0% -> 1% of each run, Pallas kernels for 0% -> 0%
where the time goes in v1:
time: 295 us; the launch traced here: 293 us
  blocking collectives  197 us (67%)
  waiting for transfers between devices  29.7 us (10%)
  local copies, waits for them, and re-layouts  21 us (7%)
  starting transfers between devices  16.8 us (6%)
  other arithmetic  15.8 us (5%)
  matrix products  9.27 us (3%)
  between operations  4.01 us (1%)
    all_to_all x13, blocking collectives, swap(): return lax.all_to_all(chunks, axes, 0, 0, tiled=True)  197 us
    all_to_all x3, waiting for transfers between devices, swap(): return lax.all_to_all(chunks, axes, 0, 0, tiled=True)  29.7 us
    all_to_all x3, starting transfers between devices, swap(): return lax.all_to_all(chunks, axes, 0, 0, tiled=True)  16.8 us
    all_to_all x10, other arithmetic, swap(): return lax.all_to_all(chunks, axes, 0, 0, tiled=True)  13.1 us
    unnamed x43, local copies, waits for them, and re-layouts  9 us
    dot_general x10, matrix products, mm(): return jnp.dot(left, right, precision=EXACT)  6.94 us
  transfers between devices with their start and end apart: 3, of which 3 were waited for; matrix products, arithmetic and copies ran while one was open for 1% of the time, Pallas kernels for 0%

profile of v1, /device:TPU:1, one launch (start us, length us, event | category | flops | bytes accessed | tf_op | source)
XLA Modules:
  0.0 293.4 jit_solution(8495664913417354445)
XLA Ops:
  2.0 1.3 fusion.53
  3.3 0.6 iota_compare_fusion.1
  4.8 1.0 convolution_select_fusion.5
  5.9 1.0 fusion.10
  6.9 1.0 fusion.1
  7.9 1.0 convolution_select_fusion.3
  8.9 1.0 fusion.3
  11.9 27.7 %all_to_all.80 = f32[64,1,1024]{2,1,0:T(1,128)S(1)} all-to-all(f32[64,1,1024]{2,1,0:T(1,128)S(1)} %reshape.67), channel_id=1, replica_groups=mesh['grp'=8,'z'=8,'x'=4,'core'=2] {'z','x','core'}, dimensions={0} | all-to-all | bytes 524288 | tf_op jit(solution)/shard_map/all_to_all | solution.py:21
  40.1 1.3 reduce
  43.3 1.2 reshape.69
  44.4 5.2 %all-to-all-start.1 = ((f32[64,1,1024]{2,1,0:T(1,128)}), f32[64,1,1024]{2,1,0:T(1,128)}, u32[]{:S(2)}, u32[]{:S(2)}) async-start(f32[64,1,1024]{2,1,0:T(1,128)} %reshape.69), calls=%async_computation.1 | async-start | bytes 524288 | tf_op jit(solution)/shard_map/all_to_all | solution.py:21
  49.7 0.7 dot_general.71
  50.3 0.9 copy.50
  51.3 11.3 %all-to-all-done.1 = f32[64,1,1024]{2,1,0:T(1,128)} async-done(((f32[64,1,1024]{2,1,0:T(1,128)}), f32[64,1,1024]{2,1,0:T(1,128)}, u32[]{:S(2)}, u32[]{:S(2)}) %all-to-all-start.1) | async-done | bytes 262176 | tf_op jit(solution)/shard_map/all_to_all | solution.py:21
  62.6 2.3 reduce.1
  65.3 1.0 fusion.43
  66.3 1.1 copy.51
  67.4 0.7 reshape.71
  68.1 22.3 %all_to_all.81 = f32[64,1,2048]{2,1,0:T(1,128)S(1)} all-to-all(f32[64,1,2048]{2,1,0:T(1,128)S(1)} %reshape.71), channel_id=1, replica_groups=mesh['grp'=8,'z'=8,'x'=4,'core'=2] {'z','x','core'}, dimensions={0} | all-to-all | bytes 1048576 | tf_op jit(solution)/shard_map/all_to_all | solution.py:21
  90.4 2.0 reduce.2
  92.9 0.8 reshape.73
  93.7 6.8 %all-to-all-start.3 = ((f32[8,1,2048]{2,1,0:T(1,128)}), f32[8,1,2048]{2,1,0:T(1,128)S(1)}, u32[]{:S(2)}, u32[]{:S(2)}) async-start(f32[8,1,2048]{2,1,0:T(1,128)} %reshape.73), calls=%async_computation.3 | async-start | bytes 131072 | tf_op jit(solution)/shard_map/all_to_all | solution.py:21
  100.5 7.2 %all-to-all-done.3 = f32[8,1,2048]{2,1,0:T(1,128)S(1)} async-done(((f32[8,1,2048]{2,1,0:T(1,128)}), f32[8,1,2048]{2,1,0:T(1,128)S(1)}, u32[]{:S(2)}, u32[]{:S(2)}) %all-to-all-start.3) | async-done | bytes 65568 | tf_op jit(solution)/shard_map/all_to_all | solution.py:21
  107.7 0.8 reduce.3
  108.9 12.3 %all_to_all.82 = f32[8,32,256]{2,1,0:T(8,128)S(1)} all-to-all(f32[8,32,256]{2,1,0:T(8,128)S(1)} %broadcast_in_dim.146), channel_id=1, replica_groups=mesh['grp'=8,'z'=8,'x'=4,'core'=2] {'x','core'}, dimensions={0} | all-to-all | bytes 524288 | tf_op jit(solution)/shard_map/all_to_all | solution.py:21
  121.3 12.7 %all_to_all.83 = f32[8,32,256]{2,1,0:T(8,128)S(1)} all-to-all(f32[8,32,256]{2,1,0:T(8,128)S(1)} %broadcast_in_dim.147), channel_id=1, replica_groups=mesh['grp'=8,'z'=8,'x'=4,'core'=2] {'z'}, dimensions={0} | all-to-all | bytes 524288 | tf_op jit(solution)/shard_map/all_to_all | solution.py:21
  134.4 9.3 %all_to_all.84 = f32[8,1,1024]{2,1,0:T(1,128)S(1)} all-to-all(f32[8,1,1024]{2,1,0:T(1,128)S(1)} %reshape.75), channel_id=1, replica_groups=mesh['grp'=8,'z'=8,'x'=4,'core'=2] {'grp'}, dimensions={0} | all-to-all | bytes 65536 | tf_op jit(solution)/shard_map/all_to_all | solution.py:21
  143.7 0.8 reduce.4
  144.8 12.4 %all_to_all.85 = f32[8,32,256]{2,1,0:T(8,128)S(1)} all-to-all(f32[8,32,256]{2,1,0:T(8,128)S(1)} %broadcast_in_dim.149), channel_id=1, replica_groups=mesh['grp'=8,'z'=8,'x'=4,'core'=2] {'x','core'}, dimensions={0} | all-to-all | bytes 524288 | tf_op jit(solution)/shard_map/all_to_all | solution.py:21
  157.3 12.7 %all_to_all.86 = f32[8,32,256]{2,1,0:T(8,128)S(1)} all-to-all(f32[8,32,256]{2,1,0:T(8,128)S(1)} %broadcast_in_dim.150), channel_id=1, replica_groups=mesh['grp'=8,'z'=8,'x'=4,'core'=2] {'z'}, dimensions={0} | all-to-all | bytes 524288 | tf_op jit(solution)/shard_map/all_to_all | solution.py:21
  170.3 9.3 %all_to_all.87 = f32[8,1,1024]{2,1,0:T(1,128)S(1)} all-to-all(f32[8,1,1024]{2,1,0:T(1,128)S(1)} %reshape.77), channel_id=1, replica_groups=mesh['grp'=8,'z'=8,'x'=4,'core'=2] {'grp'}, dimensions={0} | all-to-all | bytes 65536 | tf_op jit(solution)/shard_map/all_to_all | solution.py:21
  179.7 0.8 reduce.5
  180.8 12.4 %all_to_all.88 = f32[8,32,256]{2,1,0:T(8,128)S(1)} all-to-all(f32[8,32,256]{2,1,0:T(8,128)S(1)} %broadcast_in_dim.152), channel_id=1, replica_groups=mesh['grp'=8,'z'=8,'x'=4,'core'=2] {'x','core'}, dimensions={0} | all-to-all | bytes 524288 | tf_op jit(solution)/shard_map/all_to_all | solution.py:21
  193.3 12.7 %all_to_all.89 = f32[8,32,256]{2,1,0:T(8,128)S(1)} all-to-all(f32[8,32,256]{2,1,0:T(8,128)S(1)} %broadcast_in_dim.153), channel_id=1, replica_groups=mesh['grp'=8,'z'=8,'x'=4,'core'=2] {'z'}, dimensions={0} | all-to-all | bytes 524288 | tf_op jit(solution)/shard_map/all_to_all | solution.py:21
  206.3 9.3 %all_to_all.90 = f32[8,1,1024]{2,1,0:T(1,128)S(1)} all-to-all(f32[8,1,1024]{2,1,0:T(1,128)S(1)} %reshape.79), channel_id=1, replica_groups=mesh['grp'=8,'z'=8,'x'=4,'core'=2] {'grp'}, dimensions={0} | all-to-all | bytes 65536 | tf_op jit(solution)/shard_map/all_to_all | solution.py:21
  215.6 0.8 reduce.6
  216.7 0.7 reshape.81
  217.4 24.8 %all_to_all.91 = f32[64,1,2048]{2,1,0:T(1,128)S(1)} all-to-all(f32[64,1,2048]{2,1,0:T(1,128)S(1)} %reshape.81), channel_id=1, replica_groups=mesh['grp'=8,'z'=8,'x'=4,'core'=2] {'z','x','core'}, dimensions={0} | all-to-all | bytes 1048576 | tf_op jit(solution)/shard_map/all_to_all | solution.py:21
  242.2 1.9 reduce.7
  245.9 1.0 reshape.63
  248.0 18.6 %all_to_all.92 = f32[64,1,1024]{2,1,0:T(1,128)S(1)} all-to-all(f32[64,1,1024]{2,1,0:T(1,128)S(1)} %reshape.83), channel_id=1, replica_groups=mesh['grp'=8,'z'=8,'x'=4,'core'=2] {'z','x','core'}, dimensions={0} | all-to-all | bytes 524288 | tf_op jit(solution)/shard_map/all_to_all | solution.py:21
  266.6 1.3 reduce.8
  269.8 1.2 reshape.85
  271.0 4.8 %all-to-all-start.15 = ((f32[64,1,1024]{2,1,0:T(1,128)}), f32[64,1,1024]{2,1,0:T(1,128)S(1)}, u32[]{:S(2)}, u32[]{:S(2)}) async-start(f32[64,1,1024]{2,1,0:T(1,128)} %reshape.85), calls=%async_computation.15 | async-start | bytes 524288 | tf_op jit(solution)/shard_map/all_to_all | solution.py:21
  277.0 0.6 copy.59
  277.7 11.2 %all-to-all-done.15 = f32[64,1,1024]{2,1,0:T(1,128)S(1)} async-done(((f32[64,1,1024]{2,1,0:T(1,128)}), f32[64,1,1024]{2,1,0:T(1,128)S(1)}, u32[]{:S(2)}, u32[]{:S(2)}) %all-to-all-start.15) | async-done | bytes 262176 | tf_op jit(solution)/shard_map/all_to_all | solution.py:21
  288.9 1.3 reduce.9
  292.8 0.6 pad_maximum_fusion
  (100 shorter events, 15.6 us)
Async XLA Ops:
  0.6 41.3 %copy-start = (f32[32,2048]{1,0:T(8,128)S(1)}, f32[32,2048]{1,0:T(8,128)}, u32[]{:S(2)}) copy-start(f32[32,2048]{1,0:T(8,128)} %param.21) | copy-start | bytes 786436
  11.4 30.5 %copy-start.10 = (f32[32,32]{1,0:T(8,128)S(1)}, f32[32,32]{1,0:T(8,128)}, u32[]{:S(2)}) copy-start(f32[32,32]{1,0:T(8,128)} %param.20) | copy-start | bytes 12292
  42.6 7.0 %copy-start.1 = (f32[32,4096]{1,0:T(8,128)S(1)}, f32[32,4096]{1,0:T(8,128)}, u32[]{:S(2)}) copy-start(f32[32,4096]{1,0:T(8,128)} %param.22) | copy-start | bytes 1572868
  44.4 18.2 %all-to-all-start.1 = ((f32[64,1,1024]{2,1,0:T(1,128)}), f32[64,1,1024]{2,1,0:T(1,128)}, u32[]{:S(2)}, u32[]{:S(2)}) async-start(f32[64,1,1024]{2,1,0:T(1,128)} %reshape.69), calls=%async_computation.1 | async-start | bytes 524288 | tf_op jit(solution)/shard_map/all_to_all | solution.py:21
  90.4 10.1 %copy-start.9 = (f32[32,2,32]{2,1,0:T(2,128)S(1)}, f32[32,2,32]{2,1,0:T(2,128)}, u32[]{:S(2)}) copy-start(f32[32,2,32]{2,1,0:T(2,128)} %param.23) | copy-start | bytes 24580
  90.4 18.3 %copy-start.6 = (f32[2,32,256]{2,1,0:T(8,128)S(1)}, f32[2,32,256]{2,1,0:T(8,128)}, u32[]{:S(2)}) copy-start(f32[2,32,256]{2,1,0:T(8,128)} %param.24) | copy-start | bytes 196612
  92.8 41.3 %copy-start.8 = (f32[1,32,256]{2,1,0:T(8,128)S(1)}, f32[1,32,256]{2,1,0:T(8,128)}, u32[]{:S(2)}) copy-start(f32[1,32,256]{2,1,0:T(8,128)} %param.25) | copy-start | bytes 98308
  93.7 14.0 %all-to-all-start.3 = ((f32[8,1,2048]{2,1,0:T(1,128)}), f32[8,1,2048]{2,1,0:T(1,128)S(1)}, u32[]{:S(2)}, u32[]{:S(2)}) async-start(f32[8,1,2048]{2,1,0:T(1,128)} %reshape.73), calls=%async_computation.3 | async-start | bytes 131072 | tf_op jit(solution)/shard_map/all_to_all | solution.py:21
  245.8 1.0 copy-start.2
  271.0 17.9 %all-to-all-start.15 = ((f32[64,1,1024]{2,1,0:T(1,128)}), f32[64,1,1024]{2,1,0:T(1,128)S(1)}, u32[]{:S(2)}, u32[]{:S(2)}) async-start(f32[64,1,1024]{2,1,0:T(1,128)} %reshape.85), calls=%async_computation.15 | async-start | bytes 524288 | tf_op jit(solution)/shard_map/all_to_all | solution.py:21
  290.2 1.5 copy-start.3
  290.2 1.7 copy-start.4
  290.5 1.8 copy-start.7
  291.7 1.8 copy-start.5

commit v2 on v1

v2 whole, which is shorter than its diff:
```python
import jax
import jax.numpy as jnp
from jax import lax
from jax.sharding import Mesh
from jax.sharding import PartitionSpec as P

EXACT = lax.Precision.HIGH
NEAR = ("x", "core")
DEV = ("z", "x", "core")


def mm(left, right):
    return jnp.dot(left, right, precision=EXACT)


def mmt(left, right):
    return jnp.einsum("rn,mn->rm", left, right, precision=EXACT)


def swap(chunks, axes):
    return lax.all_to_all(chunks, axes, 0, 0, tiled=True)


def spread(values, axes, count):
    return swap(jnp.broadcast_to(values[None], (count,) + values.shape), axes)


def reduce_over(values, axes, count):
    return jnp.sum(spread(values, axes, count), 0)


def make_body(sizes):
    n_grp, n_z = sizes["grp"], sizes["z"]
    n_near = sizes["x"] * sizes["core"]
    n_dev = n_z * n_near

    def body(
        leaf_right,
        leaf_inverse,
        leaf_link,
        leaf_front,
        parents,
        front_rows,
        live_blocks,
        front_right,
        front_inverse,
        front_couple,
        root_right,
        root_inverse,
        root_couple,
    ):
        rows = leaf_right.shape[0]
        width = leaf_inverse.shape[1]
        front_order = front_inverse.shape[1]
        n_front = front_order // width
        share = front_inverse.shape[0]
        slab = share * n_z
        part = root_inverse.shape[2]
        live = live_blocks[0]
        my_z = lax.axis_index("z")

        def near_sum(natural):
            chunks = natural.reshape(rows, n_z, n_near, share).transpose(2, 0, 1, 3)
            return jnp.sum(swap(chunks.reshape(n_near, rows, slab), NEAR), 0)

        def own(values):
            return lax.dynamic_slice_in_dim(values, my_z * share, share, 1)

        blocks = front_inverse.reshape(share, n_z, part).transpose(1, 0, 2)
        wide = jnp.concatenate([blocks, root_inverse, root_couple], 0)
        wide = lax.all_gather(wide, "z", axis=1, tiled=True)
        front_slab, w_low, w_high, link = wide[:n_z], wide[n_z], wide[n_z + 1], wide[n_z + 2]

        has_parent = parents[0] < live
        right0, right1 = leaf_right[:, :width], leaf_right[:, width:]
        solved0 = jnp.where(live > 0, mm(right0, leaf_inverse[0]), 0.0)
        lifted = jnp.where(has_parent, mm(solved0, leaf_link[0]), 0.0)
        solved1 = jnp.where(live > 1, mm(right1 - lifted, leaf_inverse[1]), 0.0)
        given0, given1 = mm(solved0, leaf_front[0]), mm(solved1, leaf_front[1])
        slots = jnp.arange(n_front, dtype=jnp.int32)[None, :, None]
        placed = jnp.where(slots == front_rows[0], given0[:, None, :], 0.0) + jnp.where(
            slots == front_rows[1], given1[:, None, :], 0.0
        )
        update = near_sum(placed.reshape(rows, front_order))
        here = (jnp.arange(slab, dtype=jnp.int32) // share == my_z)[None, :]
        start = jnp.where(here, jnp.tile(front_right, (1, n_z)), 0.0) - update
        start = jnp.broadcast_to(reduce_over(start, "z", n_z)[None], (n_z, rows, slab))
        terms = jnp.einsum("zrk,zkn->zrn", start, front_slab, precision=EXACT)
        terms = lax.optimization_barrier(terms).reshape(n_z, rows, n_near, share)
        terms = terms.transpose(2, 1, 0, 3).reshape(n_near, rows, slab)
        y_slab = jnp.sum(swap(terms, NEAR), 0)
        y_own = own(y_slab)

        raised = mm(y_own, front_couple)
        half = rows // 2
        chunks = raised.reshape(2, half, 2, n_dev, share).transpose(3, 1, 0, 2, 4)
        raised = jnp.sum(swap(chunks.reshape(n_dev, half, 4 * share), DEV), 0)
        given = root_right.reshape(2, half, 2, share).transpose(1, 0, 2, 3).reshape(half, 4 * share)
        given = jnp.where(lax.axis_index("grp") == 0, given, 0.0) - raised
        given = jnp.sum(spread(given, ("grp", "z"), n_grp * n_z).reshape(n_grp, n_z, half, 4 * share), 0)
        given = given.reshape(n_z, half, 2, 2, share).transpose(3, 2, 1, 0, 4).reshape(2, rows, slab)
        low, high = given[0], given[1]
        y_high = reduce_over(mm(high, w_high), NEAR, n_near)
        low = low - reduce_over(mmt(y_high, link), "grp", n_grp)
        y_low = reduce_over(mm(low, w_low), NEAR, n_near)
        x_low = reduce_over(mmt(y_low, w_low), "grp", n_grp)
        y_high = y_high - reduce_over(mm(x_low, link), NEAR, n_near)
        x_high = reduce_over(mmt(y_high, w_high), "grp", n_grp)

        both = jnp.concatenate([x_low, x_high], 1)
        whole = spread(both, NEAR, n_near).reshape(n_near, rows, 2, n_z, share)
        whole = whole.transpose(1, 2, 3, 0, 4).reshape(rows, 2 * front_order)
        rest = y_own - mmt(whole, front_couple)
        rest = rest.reshape(4, rows // 4, share).transpose(1, 0, 2).reshape(rows // 4, 4 * share)
        rest = spread(rest, DEV, n_dev).reshape(n_dev, rows // 4, 4, share)
        rest = rest.reshape(n_z, n_near, rows // 4, 4, share)
        rest = rest.transpose(0, 3, 2, 1, 4).reshape(n_z, rows, part)
        solved = jnp.einsum("zrn,zkn->zrk", rest, front_slab, precision=EXACT)
        front_solution = spread(jnp.sum(solved, 0), NEAR, n_near)
        front_solution = front_solution.reshape(n_near, rows, n_z, share)
        front_solution = front_solution.transpose(1, 2, 0, 3).reshape(rows, front_order)

        def back(solved, block):
            picked = lax.dynamic_slice(front_solution, (0, front_rows[block] * width), (rows, width))
            return solved - mmt(picked, leaf_front[block])

        base0, base1 = back(solved0, 0), back(solved1, 1)
        leaf1 = jnp.where(live > 1, mmt(base1, leaf_inverse[1]), 0.0)
        carried = jnp.where(has_parent, mmt(leaf1, leaf_link[0]), 0.0)
        leaf0 = jnp.where(live > 0, mmt(base0 - carried, leaf_inverse[0]), 0.0)
        leaf_solution = jnp.concatenate([leaf0, leaf1], 1)
        return leaf_solution, front_solution, jnp.stack([own(x_low), own(x_high)], 1)

    return body


def solution(mesh):
    n_grp, n_dev = mesh.shape["grp"], mesh.shape["dev"]
    fine = Mesh(mesh.devices.reshape(n_grp, n_dev // 8, 4, 2), ("grp", "z", "x", "core"))
    every = ("grp",) + DEV
    in_specs = (
        P(None, every),
        P(every, None, None),
        P(every, None, None),
        P(every, None, None),
        P(every),
        P(every),
        P(every),
        P(None, every),
        P(every, None),
        P(every, None),
        P(None, None, DEV),
        P(None, DEV, "grp"),
        P(None, DEV, "grp"),
    )
    out_specs = (P(None, every), P(None, "grp"), P(None, None, DEV))
    body = make_body(dict(fine.shape))
    return jax.shard_map(body, mesh=fine, in_specs=in_specs, out_specs=out_specs, check_vma=False)
```

time: 295 us -> 313 us (1.061)
  blocking collectives: 197 us -> 139 us
  waiting for transfers between devices: 29.7 us -> 56.3 us
  local copies, waits for them, and re-layouts: 21 us -> 37.6 us
  starting transfers between devices: 16.8 us -> 33.2 us
  between operations: 4.01 us -> 17.3 us
  matrix products: 9.27 us -> 13 us
    all_to_all x13 -> x9, blocking collectives: 197 us -> 139 us  [swap(): return lax.all_to_all(chunks, axes, 0, 0, tiled=True)]
    all_to_all x3 -> x5, waiting for transfers between devices: 29.7 us -> 47.7 us  [swap(): return lax.all_to_all(chunks, axes, 0, 0, tiled=True)]
    all_to_all x3 -> x5, starting transfers between devices: 16.8 us -> 33.1 us  [swap(): return lax.all_to_all(chunks, axes, 0, 0, tiled=True)]
    reshape x5 -> x15, local copies, waits for them, and re-layouts: 3.35 us -> 18.2 us  [the longest x1 3.33 us: body(): whole = whole.transpose(1, 2, 3, 0, 4).reshape(rows, 2 * front_order)]
    all_to_all x10 -> x0, other arithmetic: 13.1 us -> none  [swap(): return lax.all_to_all(chunks, axes, 0, 0, tiled=True)]
    all_gather x0 -> x1, waiting for transfers between devices: none -> 8.64 us  [body(): wide = lax.all_gather(wide, 'z', axis=1, tiled=True)]
    unnamed x43 -> x32, local copies, waits for them, and re-layouts: 9 us -> 0.86 us
    transpose x5, local copies, waits for them, and re-layouts: 3.07 us -> 9.35 us  [the longest x1 4.11 us: body(): whole = whole.transpose(1, 2, 3, 0, 4).reshape(rows, 2 * front_order)]
  transfers between devices with their start and end apart: 3 -> 6, of which waited for: 3 -> 6; matrix products, arithmetic and copies ran while one was open for 1% -> 3% of each run, Pallas kernels for 0% -> 0%
where the time goes in v2:
time: 313 us; the launch traced here: 311 us
  blocking collectives  139 us (44%)
  waiting for transfers between devices  56.3 us (18%)
  local copies, waits for them, and re-layouts  37.6 us (12%)
  starting transfers between devices  33.2 us (11%)
  between operations  17.3 us (6%)
  other arithmetic  14.9 us (5%)
  matrix products  13 us (4%)
    all_to_all x9, blocking collectives, swap(): return lax.all_to_all(chunks, axes, 0, 0, tiled=True)  139 us
    all_to_all x5, waiting for transfers between devices, swap(): return lax.all_to_all(chunks, axes, 0, 0, tiled=True)  47.7 us
    all_to_all x5, starting transfers between devices, swap(): return lax.all_to_all(chunks, axes, 0, 0, tiled=True)  33.1 us
    all_gather x1, waiting for transfers between devices, body(): wide = lax.all_gather(wide, 'z', axis=1, tiled=True)  8.64 us
    reduce_sum x7, other arithmetic, reduce_over(): return jnp.sum(spread(values, axes, count), 0)  6.46 us
  transfers between devices with their start and end apart: 6, of which 6 were waited for; matrix products, arithmetic and copies ran while one was open for 3% of the time, Pallas kernels for 0%

profile of v2, /device:TPU:1, one launch (start us, length us, event | category | flops | bytes accessed | tf_op | source)
XLA Modules:
  0.0 311.3 jit_solution(14920914953933961020)
XLA Ops:
  7.2 1.0 copy.88
  8.3 1.6 pad_maximum_fusion
  11.2 1.4 fusion.51
  14.2 1.0 convolution_select_fusion.5
  15.2 1.0 fusion.9
  16.2 1.0 convolution_select_fusion.3
  17.2 1.0 fusion.18
  19.5 1.0 reshape.150
  20.5 10.2 %all-to-all-start = ((f32[8,32,256]{2,1,0:T(8,128)}), f32[8,32,256]{2,1,0:T(8,128)S(1)}, u32[]{:S(2)}, u32[]{:S(2)}) async-start(f32[8,32,256]{2,1,0:T(8,128)} %reshape.150), calls=%async_computation | async-start | bytes 524288 | tf_op jit(solution)/shard_map/all_to_all | solution.py:21
  30.7 6.4 %all-to-all-done = f32[8,32,256]{2,1,0:T(8,128)S(1)} async-done(((f32[8,32,256]{2,1,0:T(8,128)}), f32[8,32,256]{2,1,0:T(8,128)S(1)}, u32[]{:S(2)}, u32[]{:S(2)}) %all-to-all-start) | async-done | bytes 262176 | tf_op jit(solution)/shard_map/all_to_all | solution.py:21
  37.2 20.2 %all_to_all.70 = f32[8,32,256]{2,1,0:T(8,128)S(1)} all-to-all(f32[8,32,256]{2,1,0:T(8,128)S(1)} %broadcast_in_dim.159), channel_id=1, replica_groups=mesh['grp'=8,'z'=8,'x'=4,'core'=2] {'z'}, dimensions={0} | all-to-all | bytes 524288 | tf_op jit(solution)/shard_map/all_to_all | solution.py:21
  57.5 8.6 %all-gather.2.cloned.1.call-done = f32[11,256,256]{2,1,0:T(8,128)} async-done(((f32[11,32,256]{2,1,0:T(8,128)}), f32[11,256,256]{2,1,0:T(8,128)}) %all-gather.2.cloned.1.call-update) | async-done | bytes 2883600 | tf_op jit(solution)/shard_map/all_gather | solution.py:71
  66.1 2.3 fusion.2
  69.3 1.0 reshape.153
  70.3 6.6 %all-to-all-start.2 = ((f32[8,32,256]{2,1,0:T(8,128)}), f32[8,32,256]{2,1,0:T(8,128)S(1)}, u32[]{:S(2)}, u32[]{:S(2)}) async-start(f32[8,32,256]{2,1,0:T(8,128)} %reshape.153), calls=%async_computation.2 | async-start | bytes 524288 | tf_op jit(solution)/shard_map/all_to_all | solution.py:21
  76.9 6.5 %all-to-all-done.2 = f32[8,32,256]{2,1,0:T(8,128)S(1)} async-done(((f32[8,32,256]{2,1,0:T(8,128)}), f32[8,32,256]{2,1,0:T(8,128)S(1)}, u32[]{:S(2)}, u32[]{:S(2)}) %all-to-all-start.2) | async-done | bytes 262176 | tf_op jit(solution)/shard_map/all_to_all | solution.py:21
  84.6 1.6 copy.74
  86.1 2.4 copy.75
  88.5 6.7 %all-to-all-start.3 = ((f32[64,16,128]{2,1,0:T(8,128)}), f32[64,16,128]{2,1,0:T(8,128)}, u32[]{:S(2)}, u32[]{:S(2)}) async-start(f32[64,16,128]{2,1,0:T(8,128)} %copy.75), calls=%async_computation.3 | async-start | bytes 1048576 | tf_op jit(solution)/shard_map/all_to_all | solution.py:21
  95.3 17.5 %all-to-all-done.3 = f32[64,16,128]{2,1,0:T(8,128)} async-done(((f32[64,16,128]{2,1,0:T(8,128)}), f32[64,16,128]{2,1,0:T(8,128)}, u32[]{:S(2)}, u32[]{:S(2)}) %all-to-all-start.3) | async-done | bytes 524320 | tf_op jit(solution)/shard_map/all_to_all | solution.py:21
  112.8 1.1 reduce_sum.108
  114.0 25.6 %all_to_all.71 = f32[64,16,128]{2,1,0:T(8,128)} all-to-all(f32[64,16,128]{2,1,0:T(8,128)S(1)} %broadcast_in_dim.162), channel_id=1, replica_groups=mesh['grp'=8,'z'=8,'x'=4,'core'=2] {'grp','z'}, dimensions={0} | all-to-all | bytes 1048576 | tf_op jit(solution)/shard_map/all_to_all | solution.py:21
  139.5 1.1 reduce_sum.109
  141.6 1.1 copy.89
  145.1 13.3 %all_to_all.72 = f32[8,32,256]{2,1,0:T(8,128)} all-to-all(f32[8,32,256]{2,1,0:T(8,128)S(1)} %broadcast_in_dim.163), channel_id=1, replica_groups=mesh['grp'=8,'z'=8,'x'=4,'core'=2] {'x','core'}, dimensions={0} | all-to-all | bytes 524288 | tf_op jit(solution)/shard_map/all_to_all | solution.py:21
  158.4 1.0 reduce_sum.110
  159.7 13.9 %all_to_all.73 = f32[8,32,256]{2,1,0:T(8,128)} all-to-all(f32[8,32,256]{2,1,0:T(8,128)S(1)} %broadcast_in_dim.164), channel_id=1, replica_groups=mesh['grp'=8,'z'=8,'x'=4,'core'=2] {'grp'}, dimensions={0} | all-to-all | bytes 524288 | tf_op jit(solution)/shard_map/all_to_all | solution.py:21
  173.6 1.6 reduce_sum.111
  176.0 1.6 slice_subtract_fusion
  177.6 1.0 sub.49
  178.8 12.2 %all_to_all.74 = f32[8,32,256]{2,1,0:T(8,128)} all-to-all(f32[8,32,256]{2,1,0:T(8,128)S(1)} %broadcast_in_dim.165), channel_id=1, replica_groups=mesh['grp'=8,'z'=8,'x'=4,'core'=2] {'x','core'}, dimensions={0} | all-to-all | bytes 524288 | tf_op jit(solution)/shard_map/all_to_all | solution.py:21
  191.0 1.0 reduce_sum.113
  192.3 13.4 %all_to_all.75 = f32[8,32,256]{2,1,0:T(8,128)} all-to-all(f32[8,32,256]{2,1,0:T(8,128)S(1)} %broadcast_in_dim.166), channel_id=1, replica_groups=mesh['grp'=8,'z'=8,'x'=4,'core'=2] {'grp'}, dimensions={0} | all-to-all | bytes 524288 | tf_op jit(solution)/shard_map/all_to_all | solution.py:21
  206.8 12.0 %all_to_all.76 = f32[8,32,256]{2,1,0:T(8,128)} all-to-all(f32[8,32,256]{2,1,0:T(8,128)S(1)} %broadcast_in_dim.167), channel_id=1, replica_groups=mesh['grp'=8,'z'=8,'x'=4,'core'=2] {'x','core'}, dimensions={0} | all-to-all | bytes 524288 | tf_op jit(solution)/shard_map/all_to_all | solution.py:21
  220.2 13.4 %all_to_all.77 = f32[8,32,256]{2,1,0:T(8,128)} all-to-all(f32[8,32,256]{2,1,0:T(8,128)S(1)} %broadcast_in_dim.168), channel_id=1, replica_groups=mesh['grp'=8,'z'=8,'x'=4,'core'=2] {'grp'}, dimensions={0} | all-to-all | bytes 524288 | tf_op jit(solution)/shard_map/all_to_all | solution.py:21
  234.6 14.9 %all_to_all.78 = f32[8,32,512]{2,1,0:T(8,128)} all-to-all(f32[8,32,512]{2,1,0:T(8,128)S(1)} %broadcast_in_dim.169), channel_id=1, replica_groups=mesh['grp'=8,'z'=8,'x'=4,'core'=2] {'x','core'}, dimensions={0} | all-to-all | bytes 1048576 | tf_op jit(solution)/shard_map/all_to_all | solution.py:21
  249.5 2.8 reshape.158
  252.3 4.1 %copy.77 = f32[32,2,8,8,32]{4,3,2,1,0:T(8,128)} copy(f32[32,2,8,8,32]{4,2,1,0,3:T(8,128)} %bitcast.110) | data formatting | bytes 1048576 | tf_op jit(solution)/shard_map/transpose | solution.py:112
  256.4 3.3 %reshape.159 = f32[32,4096]{1,0:T(8,128)} reshape(f32[32,2,8,8,32]{4,3,2,1,0:T(8,128)} %copy.77) | data formatting | bytes 1048576 | tf_op jit(solution)/shard_map/reshape | solution.py:112
  259.8 1.4 fusion.8
  262.0 5.9 %all-to-all-start.12 = ((f32[64,8,128]{2,1,0:T(8,128)}), f32[64,8,128]{2,1,0:T(8,128)}, u32[]{:S(2)}, u32[]{:S(2)}) async-start(f32[64,8,128]{2,1,0:T(8,128)} %broadcast_in_dim.171), calls=%async_computation.12 | async-start | bytes 524288 | tf_op jit(solution)/shard_map/all_to_all | solution.py:21
  269.3 11.7 %all-to-all-done.12 = f32[64,8,128]{2,1,0:T(8,128)} async-done(((f32[64,8,128]{2,1,0:T(8,128)}), f32[64,8,128]{2,1,0:T(8,128)}, u32[]{:S(2)}, u32[]{:S(2)}) %all-to-all-start.12) | async-done | bytes 262176 | tf_op jit(solution)/shard_map/all_to_all | solution.py:21
  281.0 2.4 reshape_reshape.4
  283.3 2.9 copy.79
  286.2 2.2 reshape.161
  288.4 2.0 fusion.4
  291.2 3.8 %all-to-all-start.13 = ((f32[8,32,256]{2,1,0:T(8,128)}), f32[8,32,256]{2,1,0:T(8,128)S(1)}, u32[]{:S(2)}, u32[]{:S(2)}) async-start(f32[8,32,256]{2,1,0:T(8,128)} %broadcast_in_dim.172), calls=%async_computation.13 | async-start | bytes 524288 | tf_op jit(solution)/shard_map/all_to_all | solution.py:21
  295.8 5.7 %all-to-all-done.13 = f32[8,32,256]{2,1,0:T(8,128)S(1)} async-done(((f32[8,32,256]{2,1,0:T(8,128)}), f32[8,32,256]{2,1,0:T(8,128)S(1)}, u32[]{:S(2)}, u32[]{:S(2)}) %all-to-all-start.13) | async-done | bytes 262176 | tf_op jit(solution)/shard_map/all_to_all | solution.py:21
  (101 shorter events, 18.9 us)
Async XLA Ops:
  7.2 76.2 %copy-start = (f32[32,4096]{1,0:T(8,128)S(1)}, f32[32,4096]{1,0:T(8,128)}, u32[]{:S(2)}) copy-start(f32[32,4096]{1,0:T(8,128)} %param.22) | copy-start | bytes 1572868
  7.2 11.3 %copy-start.3 = (f32[2,128,128]{2,1,0:T(8,128)S(1)}, f32[2,128,128]{2,1,0:T(8,128)}, u32[]{:S(2)}) copy-start(f32[2,128,128]{2,1,0:T(8,128)} %param.16) | copy-start | bytes 393220
  7.2 59.0 %all-gather.2.cloned.1.call-start = ((), (), s32[]{:S(2)}) async-start(), calls=%async_computation.14 | async-start | bytes 3244032 | tf_op jit(solution)/shard_map/all_gather | solution.py:71
  17.2 1.0 copy-start.9
  19.0 11.6 %copy-start.15 = (f32[32,32]{1,0:T(8,128)S(1)}, f32[32,32]{1,0:T(8,128)}, u32[]{:S(2)}) copy-start(f32[32,32]{1,0:T(8,128)} %param.20) | copy-start | bytes 12292
  20.5 16.7 %all-to-all-start = ((f32[8,32,256]{2,1,0:T(8,128)}), f32[8,32,256]{2,1,0:T(8,128)S(1)}, u32[]{:S(2)}, u32[]{:S(2)}) async-start(f32[8,32,256]{2,1,0:T(8,128)} %reshape.150), calls=%async_computation | async-start | bytes 524288 | tf_op jit(solution)/shard_map/all_to_all | solution.py:21
  70.3 13.1 %all-to-all-start.2 = ((f32[8,32,256]{2,1,0:T(8,128)}), f32[8,32,256]{2,1,0:T(8,128)S(1)}, u32[]{:S(2)}, u32[]{:S(2)}) async-start(f32[8,32,256]{2,1,0:T(8,128)} %reshape.153), calls=%async_computation.2 | async-start | bytes 524288 | tf_op jit(solution)/shard_map/all_to_all | solution.py:21
  83.4 2.7 copy-start.11
  84.5 10.7 %copy-start.14 = (f32[32,2,32]{2,1,0:T(2,128)S(1)}, f32[32,2,32]{2,1,0:T(2,128)}, u32[]{:S(2)}) copy-start(f32[32,2,32]{2,1,0:T(2,128)} %param.23) | copy-start | bytes 24580
  88.5 55.6 %copy-start.1 = (f32[11,256,256]{2,1,0:T(8,128)S(1)}, f32[11,256,256]{2,1,0:T(8,128)}, u32[]{:S(2)}) copy-start(f32[11,256,256]{2,1,0:T(8,128)} %all-gather.2.cloned.1.call-done) | copy-start | bytes 8650756
  88.5 24.3 %all-to-all-start.3 = ((f32[64,16,128]{2,1,0:T(8,128)}), f32[64,16,128]{2,1,0:T(8,128)}, u32[]{:S(2)}, u32[]{:S(2)}) async-start(f32[64,16,128]{2,1,0:T(8,128)} %copy.75), calls=%async_computation.3 | async-start | bytes 1048576 | tf_op jit(solution)/shard_map/all_to_all | solution.py:21
  142.7 0.7 copy-start.2
  159.4 14.2 %copy-start.7 = (f32[32,256]{1,0:T(8,128)}, f32[32,256]{1,0:T(8,128)S(1)}, u32[]{:S(2)}) copy-start(f32[32,256]{1,0:T(8,128)S(1)} %reduce_sum.110) | copy-start | bytes 98308
  177.6 42.3 %copy-start.8 = (f32[32,256]{1,0:T(8,128)S(1)}, f32[32,256]{1,0:T(8,128)}, u32[]{:S(2)}) copy-start(f32[32,256]{1,0:T(8,128)} %copy-done.7) | copy-start | bytes 98308
  252.3 7.4 %copy-start.12 = (f32[32,256]{1,0:T(8,128)S(1)}, f32[32,256]{1,0:T(8,128)}, u32[]{:S(2)}) copy-start(f32[32,256]{1,0:T(8,128)} %copy-done.11) | copy-start | bytes 98308
  262.0 19.0 %all-to-all-start.12 = ((f32[64,8,128]{2,1,0:T(8,128)}), f32[64,8,128]{2,1,0:T(8,128)}, u32[]{:S(2)}, u32[]{:S(2)}) async-start(f32[64,8,128]{2,1,0:T(8,128)} %broadcast_in_dim.171), calls=%async_computation.12 | async-start | bytes 524288 | tf_op jit(solution)/shard_map/all_to_all | solution.py:21
  290.4 12.4 %copy-start.4 = (f32[2,128,128]{2,1,0:T(8,128)S(1)}, f32[2,128,128]{2,1,0:T(8,128)}, u32[]{:S(2)}) copy-start(f32[2,128,128]{2,1,0:T(8,128)} %param.16) | copy-start | bytes 393220
  290.4 12.4 %copy-start.10 = (f32[32,128]{1,0:T(8,128)S(1)}, f32[32,128]{1,0:T(8,128)}, u32[]{:S(2)}) copy-start(f32[32,128]{1,0:T(8,128)} %copy-done.9) | copy-start | bytes 49156
  290.5 12.6 %copy-start.5 = (f32[2,128,128]{2,1,0:T(8,128)S(1)}, f32[2,128,128]{2,1,0:T(8,128)}, u32[]{:S(2)}) copy-start(f32[2,128,128]{2,1,0:T(8,128)} %param.14) | copy-start | bytes 393220
  291.2 12.2 %copy-start.13 = (f32[2,128,128]{2,1,0:T(8,128)S(1)}, f32[2,128,128]{2,1,0:T(8,128)}, u32[]{:S(2)}) copy-start(f32[2,128,128]{2,1,0:T(8,128)} %param.15) | copy-start | bytes 393220
  291.2 10.2 %all-to-all-start.13 = ((f32[8,32,256]{2,1,0:T(8,128)}), f32[8,32,256]{2,1,0:T(8,128)S(1)}, u32[]{:S(2)}, u32[]{:S(2)}) async-start(f32[8,32,256]{2,1,0:T(8,128)} %broadcast_in_dim.172), calls=%async_computation.13 | async-start | bytes 524288 | tf_op jit(solution)/shard_map/all_to_all | solution.py:21
  302.8 1.6 copy-start.6
Sparse Core Ops, SparseCore 0:
  10.1 56.0 all-gather.1

commit v3 on v1

--- a/solution.py
+++ b/solution.py
@@ -29,24 +29,22 @@
     return jnp.sum(spread(values, axes, count), 0)
 
 
-def scatter_sum(values, axes, count):
+def fold(values, folds):
     rows, width = values.shape
-    chunks = values.reshape(rows, count, width // count).transpose(1, 0, 2)
-    return jnp.sum(swap(chunks, axes), 0)
+    tall = rows // folds
+    return values.reshape(folds, tall, width).transpose(1, 0, 2).reshape(tall, folds * width)
 
 
-def gather_columns(values, axes, count):
-    rows, width = values.shape
-    return spread(values, axes, count).transpose(1, 0, 2).reshape(rows, count * width)
+def unfold(values, folds):
+    tall, width = values.shape
+    thin = width // folds
+    return values.reshape(tall, folds, thin).transpose(1, 0, 2).reshape(folds * tall, thin)
 
 
 def make_body(sizes):
     n_grp, n_z = sizes["grp"], sizes["z"]
     n_near = sizes["x"] * sizes["core"]
     n_dev = n_z * n_near
-
-    def reduce_dev(values):
-        return reduce_over(reduce_over(values, NEAR, n_near), "z", n_z)
 
     def body(
         leaf_right,
@@ -67,8 +65,23 @@
         width = leaf_inverse.shape[1]
         front_order = front_inverse.shape[1]
         n_front = front_order // width
-        share = root_right.shape[2]
+        share = front_inverse.shape[0]
+        part = root_inverse.shape[2]
+        few = rows // n_near
         live = live_blocks[0]
+        my_dev = lax.axis_index(DEV)
+
+        chain = jnp.concatenate([root_inverse, root_couple], 0)
+        chain = spread(chain, NEAR, n_near).transpose(1, 0, 2, 3).reshape(3, n_near * share, part)
+
+        def dev_sum(natural):
+            chunks = natural.reshape(4, rows // 4, n_dev, share).transpose(2, 1, 0, 3)
+            return unfold(jnp.sum(swap(chunks.reshape(n_dev, rows // 4, 4 * share), DEV), 0), 4)
+
+        def dev_columns(values):
+            chunks = spread(fold(values, 4), DEV, n_dev).reshape(n_dev, rows // 4, 4, share)
+            return chunks.transpose(2, 1, 0, 3).reshape(rows, n_dev * share)
+
         has_parent = parents[0] < live
         right0, right1 = leaf_right[:, :width], leaf_right[:, width:]
         solved0 = jnp.where(live > 0, mm(right0, leaf_inverse[0]), 0.0)
@@ -79,33 +92,37 @@
         placed = jnp.where(slots == front_rows[0], given0[:, None, :], 0.0) + jnp.where(
             slots == front_rows[1], given1[:, None, :], 0.0
         )
-        update = scatter_sum(placed.reshape(rows, front_order), DEV, n_dev)
-        terms = mm(front_right - update, front_inverse)
-        y_front = scatter_sum(terms, DEV, n_dev)
+        placed, chain = lax.optimization_barrier((placed, chain))
+        w_low, w_high, link = chain[0], chain[1], chain[2]
+        start = front_right - dev_sum(placed.reshape(rows, front_order))
+        y_own = dev_sum(mm(start, front_inverse))
 
-        raised = mm(y_front, front_couple).reshape(rows, 2, n_dev, share)
-        raised = jnp.sum(swap(raised.transpose(2, 0, 1, 3).reshape(n_dev, rows, 2 * share), DEV), 0)
-        raised = reduce_over(raised, "grp", n_grp)
-        low = root_right[:, 0] - raised[:, :share]
-        high = root_right[:, 1] - raised[:, share:]
-        w_low, w_high, link = root_inverse[0], root_inverse[1], root_couple[0]
-        y_high = reduce_dev(mm(high, w_high))
+        spots = my_dev * share + jnp.arange(share, dtype=jnp.int32)
+        spots = jnp.concatenate([spots, front_order + spots])[:, None]
+        picks = spots == jnp.arange(2 * front_order, dtype=jnp.int32)[None, :]
+        picks = jnp.where(picks & (lax.axis_index("grp") == 0), 1.0, 0.0).astype(jnp.float32)
+        fed = jnp.concatenate([-y_own, root_right[:, 0], root_right[:, 1]], 1)
+        given = mm(fed, jnp.concatenate([front_couple, picks], 0))
+        chunks = given.reshape(n_near, few, 2, n_z, part).transpose(3, 0, 2, 1, 4)
+        given = jnp.sum(swap(chunks.reshape(n_dev, 2 * few, part), DEV), 0)
+        given = reduce_over(given, "grp", n_grp)
+
+        low, high = given[:few], given[few:]
+        y_high = reduce_over(mm(high, w_high), "z", n_z)
         low = low - reduce_over(mmt(y_high, link), "grp", n_grp)
-        y_low = reduce_dev(mm(low, w_low))
+        y_low = reduce_over(mm(low, w_low), "z", n_z)
         x_low = reduce_over(mmt(y_low, w_low), "grp", n_grp)
-        y_high = y_high - reduce_dev(mm(x_low, link))
+        y_high = y_high - reduce_over(mm(x_low, link), "z", n_z)
         x_high = reduce_over(mmt(y_high, w_high), "grp", n_grp)
 
-        both = jnp.concatenate([x_low, x_high], 1)
-        whole = spread(both, DEV, n_dev).reshape(n_dev, rows, 2, share)
-        whole = whole.transpose(1, 2, 0, 3).reshape(rows, 2 * n_dev * share)
-        rest = y_front - mmt(whole, front_couple)
-        rest = gather_columns(rest, DEV, n_dev)
-        front_solution = gather_columns(mmt(rest, front_inverse), DEV, n_dev)
+        whole = spread(jnp.concatenate([x_low, x_high], 0), DEV, n_dev)
+        whole = whole.reshape(n_z, n_near, 2, few, part).transpose(1, 3, 2, 0, 4)
+        whole = whole.reshape(rows, 2 * front_order)
+        rest = dev_columns(y_own - mmt(whole, front_couple))
+        front_solution = dev_columns(mmt(rest, front_inverse))
 
         def back(solved, block):
-            start = front_rows[block] * width
-            picked = lax.dynamic_slice(front_solution, (0, start), (rows, width))
+            picked = lax.dynamic_slice(front_solution, (0, front_rows[block] * width), (rows, width))
             return solved - mmt(picked, leaf_front[block])
 
         base0, base1 = back(solved0, 0), back(solved1, 1)
@@ -113,7 +130,9 @@
         carried = jnp.where(has_parent, mmt(leaf1, leaf_link[0]), 0.0)
         leaf0 = jnp.where(live > 0, mmt(base0 - carried, leaf_inverse[0]), 0.0)
         leaf_solution = jnp.concatenate([leaf0, leaf1], 1)
-        return leaf_solution, front_solution, jnp.stack([x_low, x_high], 1)
+        root = whole.reshape(rows, 2, front_order)
+        root = lax.dynamic_slice(root, (0, 0, my_dev * share), (rows, 2, share))
+        return leaf_solution, front_solution, root
 
     return body
 

time: 295 us -> 238 us (0.81)
  blocking collectives: 197 us -> 141 us
  waiting for transfers between devices: 29.7 us -> 45.1 us
  other arithmetic: 15.8 us -> 3.64 us
  starting transfers between devices: 16.8 us -> 28 us
  local copies, waits for them, and re-layouts: 21 us -> 10.5 us
  matrix products: 9.27 us -> 5.27 us
    all_to_all x13 -> x10, blocking collectives: 197 us -> 141 us  [swap(): return lax.all_to_all(chunks, axes, 0, 0, tiled=True)]
    all_to_all x3 -> x4, waiting for transfers between devices: 29.7 us -> 45.1 us  [swap(): return lax.all_to_all(chunks, axes, 0, 0, tiled=True)]
    all_to_all x10 -> x0, other arithmetic: 13.1 us -> none  [swap(): return lax.all_to_all(chunks, axes, 0, 0, tiled=True)]
    all_to_all x3 -> x4, starting transfers between devices: 16.8 us -> 28 us  [swap(): return lax.all_to_all(chunks, axes, 0, 0, tiled=True)]
    unnamed x43 -> x24, local copies, waits for them, and re-layouts: 9 us -> 0.88 us
    dot_general x10, matrix products: 6.94 us -> 2.58 us  [mm(): return jnp.dot(left, right, precision=EXACT)]
  transfers between devices with their start and end apart: 3 -> 4, of which waited for: 3 -> 4; matrix products, arithmetic and copies ran while one was open for 1% -> 2% of each run, Pallas kernels for 0% -> 0%
where the time goes in v3:
time: 238 us; the launch traced here: 237 us
  blocking collectives  141 us (59%)
  waiting for transfers between devices  45.1 us (19%)
  starting transfers between devices  28 us (12%)
  local copies, waits for them, and re-layouts  10.5 us (4%)
  matrix products  5.27 us (2%)
  other arithmetic  3.64 us (2%)
  between operations  3.18 us (1%)
    all_to_all x10, blocking collectives, swap(): return lax.all_to_all(chunks, axes, 0, 0, tiled=True)  141 us
    all_to_all x4, waiting for transfers between devices, swap(): return lax.all_to_all(chunks, axes, 0, 0, tiled=True)  45.1 us
    all_to_all x4, starting transfers between devices, swap(): return lax.all_to_all(chunks, axes, 0, 0, tiled=True)  28 us
  transfers between devices with their start and end apart: 4, of which 4 were waited for; matrix products, arithmetic and copies ran while one was open for 2% of the time, Pallas kernels for 0%

profile of v3, /device:TPU:1, one launch (start us, length us, event | category | flops | bytes accessed | tf_op | source)
XLA Modules:
  0.0 237.2 jit_solution(12905074473350076630)
XLA Ops:
  0.6 0.9 pad_maximum_fusion
  1.6 1.0 broadcast_in_dim.127
  2.6 10.4 %all-to-all-start = ((f32[8,3,32,256]{3,2,1,0:T(8,128)}), f32[8,3,32,256]{3,2,1,0:T(8,128)S(1)}, u32[]{:S(2)}, u32[]{:S(2)}) async-start(f32[8,3,32,256]{3,2,1,0:T(8,128)} %broadcast_in_dim.127), calls=%async_computation | async-start | bytes 1572864 | tf_op jit(solution)/shard_map/all_to_all | solution.py:21
  13.7 0.6 fusion.66
  14.8 1.3 iota_compare_fusion.1
  16.6 8.6 %all-to-all-done = f32[8,3,32,256]{3,2,1,0:T(8,128)S(1)} async-done(((f32[8,3,32,256]{3,2,1,0:T(8,128)}), f32[8,3,32,256]{3,2,1,0:T(8,128)S(1)}, u32[]{:S(2)}, u32[]{:S(2)}) %all-to-all-start) | async-done | bytes 786464 | tf_op jit(solution)/shard_map/all_to_all | solution.py:21
  25.2 0.3 reshape_reshape.6
  25.5 0.3 copy.85
  25.9 0.9 copy.86
  26.7 7.9 %all-to-all-start.1 = ((f32[64,8,128]{2,1,0:T(8,128)}), f32[64,8,128]{2,1,0:T(8,128)S(1)}, u32[]{:S(2)}, u32[]{:S(2)}) async-start(f32[64,8,128]{2,1,0:T(8,128)} %copy.86), calls=%async_computation.1 | async-start | bytes 524288 | tf_op jit(solution)/shard_map/all_to_all | solution.py:21
  34.8 13.0 %all-to-all-done.1 = f32[64,8,128]{2,1,0:T(8,128)S(1)} async-done(((f32[64,8,128]{2,1,0:T(8,128)}), f32[64,8,128]{2,1,0:T(8,128)S(1)}, u32[]{:S(2)}, u32[]{:S(2)}) %all-to-all-start.1) | async-done | bytes 262176 | tf_op jit(solution)/shard_map/all_to_all | solution.py:21
  47.9 0.4 fusion.55
  48.3 0.3 reshape.91
  48.6 0.3 copy.88
  48.9 0.9 copy.89
  49.8 4.9 %all-to-all-start.2 = ((f32[64,8,128]{2,1,0:T(8,128)}), f32[64,8,128]{2,1,0:T(8,128)S(1)}, u32[]{:S(2)}, u32[]{:S(2)}) async-start(f32[64,8,128]{2,1,0:T(8,128)} %copy.89), calls=%async_computation.2 | async-start | bytes 524288 | tf_op jit(solution)/shard_map/all_to_all | solution.py:21
  54.7 0.2 fusion.8
  55.0 12.8 %all-to-all-done.2 = f32[64,8,128]{2,1,0:T(8,128)S(1)} async-done(((f32[64,8,128]{2,1,0:T(8,128)}), f32[64,8,128]{2,1,0:T(8,128)S(1)}, u32[]{:S(2)}, u32[]{:S(2)}) %all-to-all-start.2) | async-done | bytes 262176 | tf_op jit(solution)/shard_map/all_to_all | solution.py:21
  68.0 0.9 fusion
  69.0 0.3 copy.93
  69.4 0.3 copy.94
  69.7 22.3 %all_to_all.70 = f32[64,8,256]{2,1,0:T(8,128)S(1)} all-to-all(f32[64,8,256]{2,1,0:T(8,128)S(1)} %copy.94), channel_id=1, replica_groups=mesh['grp'=8,'z'=8,'x'=4,'core'=2] {'z','x','core'}, dimensions={0} | all-to-all | bytes 1048576 | tf_op jit(solution)/shard_map/all_to_all | solution.py:21
  92.0 13.8 %all_to_all.71 = f32[8,8,256]{2,1,0:T(8,128)S(1)} all-to-all(f32[8,8,256]{2,1,0:T(8,128)S(1)} %broadcast_in_dim.130), channel_id=1, replica_groups=mesh['grp'=8,'z'=8,'x'=4,'core'=2] {'grp'}, dimensions={0} | all-to-all | bytes 131072 | tf_op jit(solution)/shard_map/all_to_all | solution.py:21
  106.1 10.2 %all_to_all.72 = f32[8,4,256]{2,1,0:T(4,128)S(1)} all-to-all(f32[8,4,256]{2,1,0:T(4,128)S(1)} %broadcast_in_dim.131), channel_id=1, replica_groups=mesh['grp'=8,'z'=8,'x'=4,'core'=2] {'z'}, dimensions={0} | all-to-all | bytes 65536 | tf_op jit(solution)/shard_map/all_to_all | solution.py:21
  116.4 0.3 fusion.16
  116.7 9.2 %all_to_all.73 = f32[8,4,256]{2,1,0:T(4,128)S(1)} all-to-all(f32[8,4,256]{2,1,0:T(4,128)S(1)} %broadcast_in_dim.132), channel_id=1, replica_groups=mesh['grp'=8,'z'=8,'x'=4,'core'=2] {'grp'}, dimensions={0} | all-to-all | bytes 65536 | tf_op jit(solution)/shard_map/all_to_all | solution.py:21
  126.2 9.2 %all_to_all.74 = f32[8,4,256]{2,1,0:T(4,128)S(1)} all-to-all(f32[8,4,256]{2,1,0:T(4,128)S(1)} %broadcast_in_dim.133), channel_id=1, replica_groups=mesh['grp'=8,'z'=8,'x'=4,'core'=2] {'z'}, dimensions={0} | all-to-all | bytes 65536 | tf_op jit(solution)/shard_map/all_to_all | solution.py:21
  135.5 0.3 fusion.10
  135.8 9.2 %all_to_all.75 = f32[8,4,256]{2,1,0:T(4,128)S(1)} all-to-all(f32[8,4,256]{2,1,0:T(4,128)S(1)} %broadcast_in_dim.134), channel_id=1, replica_groups=mesh['grp'=8,'z'=8,'x'=4,'core'=2] {'grp'}, dimensions={0} | all-to-all | bytes 65536 | tf_op jit(solution)/shard_map/all_to_all | solution.py:21
  145.3 9.2 %all_to_all.76 = f32[8,4,256]{2,1,0:T(4,128)S(1)} all-to-all(f32[8,4,256]{2,1,0:T(4,128)S(1)} %broadcast_in_dim.135), channel_id=1, replica_groups=mesh['grp'=8,'z'=8,'x'=4,'core'=2] {'z'}, dimensions={0} | all-to-all | bytes 65536 | tf_op jit(solution)/shard_map/all_to_all | solution.py:21
  154.6 0.3 fusion.18
  154.9 9.2 %all_to_all.77 = f32[8,4,256]{2,1,0:T(4,128)S(1)} all-to-all(f32[8,4,256]{2,1,0:T(4,128)S(1)} %broadcast_in_dim.136), channel_id=1, replica_groups=mesh['grp'=8,'z'=8,'x'=4,'core'=2] {'grp'}, dimensions={0} | all-to-all | bytes 65536 | tf_op jit(solution)/shard_map/all_to_all | solution.py:21
  164.2 30.4 %all_to_all.78 = f32[64,8,256]{2,1,0:T(8,128)S(1)} all-to-all(f32[64,8,256]{2,1,0:T(8,128)S(1)} %broadcast_in_dim.137), channel_id=1, replica_groups=mesh['grp'=8,'z'=8,'x'=4,'core'=2] {'z','x','core'}, dimensions={0} | all-to-all | bytes 1048576 | tf_op jit(solution)/shard_map/all_to_all | solution.py:21
  195.0 0.6 fusion.5
  195.7 18.6 %all_to_all.79 = f32[64,8,128]{2,1,0:T(8,128)S(1)} all-to-all(f32[64,8,128]{2,1,0:T(8,128)S(1)} %broadcast_in_dim.139), channel_id=1, replica_groups=mesh['grp'=8,'z'=8,'x'=4,'core'=2] {'z','x','core'}, dimensions={0} | all-to-all | bytes 524288 | tf_op jit(solution)/shard_map/all_to_all | solution.py:21
  214.5 0.4 copy.105
  214.9 0.5 dot_general.76
  215.4 0.3 convolution_bitcast_fusion
  215.8 0.7 broadcast_in_dim.141
  216.5 4.8 %all-to-all-start.13 = ((f32[64,8,128]{2,1,0:T(8,128)}), f32[64,8,128]{2,1,0:T(8,128)S(1)}, u32[]{:S(2)}, u32[]{:S(2)}) async-start(f32[64,8,128]{2,1,0:T(8,128)} %broadcast_in_dim.141), calls=%async_computation.13 | async-start | bytes 524288 | tf_op jit(solution)/shard_map/all_to_all | solution.py:21
  223.0 0.6 copy.110
  223.6 10.8 %all-to-all-done.13 = f32[64,8,128]{2,1,0:T(8,128)S(1)} async-done(((f32[64,8,128]{2,1,0:T(8,128)}), f32[64,8,128]{2,1,0:T(8,128)S(1)}, u32[]{:S(2)}, u32[]{:S(2)}) %all-to-all-start.13) | async-done | bytes 262176 | tf_op jit(solution)/shard_map/all_to_all | solution.py:21
  234.6 0.4 copy.108
  235.0 0.5 reshape.102
  235.7 0.2 convolution_select_fusion.2
  235.9 0.2 convolution_subtract_fusion.1
  236.1 0.2 fusion.4
  236.6 0.6 pad_maximum_fusion.1
  (73 shorter events, 4.5 us)
Async XLA Ops:
  0.6 47.3 %copy-start = (f32[32,2048]{1,0:T(8,128)S(1)}, f32[32,2048]{1,0:T(8,128)}, u32[]{:S(2)}) copy-start(f32[32,2048]{1,0:T(8,128)} %param.21) | copy-start | bytes 786436
  1.6 12.1 %copy-start.10 = (s32[2]{0:T(128)S(1)}, s32[2]{0:T(128)}, u32[]{:S(2)}) copy-start(s32[2]{0:T(128)} %param.17) | copy-start | bytes 28
  1.6 12.1 %copy-start.9 = (s32[2]{0:T(128)S(1)}, s32[2]{0:T(128)}, u32[]{:S(2)}) copy-start(s32[2]{0:T(128)} %param.18) | copy-start | bytes 28
  1.6 12.7 %copy-start.3 = (f32[2,128,128]{2,1,0:T(8,128)S(1)}, f32[2,128,128]{2,1,0:T(8,128)}, u32[]{:S(2)}) copy-start(f32[2,128,128]{2,1,0:T(8,128)} %param.14) | copy-start | bytes 393220
  1.6 12.7 %copy-start.6 = (f32[32,256]{1,0:T(8,128)S(1)}, f32[32,256]{1,0:T(8,128)}, u32[]{:S(2)}) copy-start(f32[32,256]{1,0:T(8,128)} %param.13) | copy-start | bytes 98308
  2.6 11.9 %copy-start.2 = (f32[2,128,128]{2,1,0:T(8,128)S(1)}, f32[2,128,128]{2,1,0:T(8,128)}, u32[]{:S(2)}) copy-start(f32[2,128,128]{2,1,0:T(8,128)} %param.16) | copy-start | bytes 393220
  2.6 12.1 %copy-start.5 = (f32[2,128,128]{2,1,0:T(8,128)S(1)}, f32[2,128,128]{2,1,0:T(8,128)}, u32[]{:S(2)}) copy-start(f32[2,128,128]{2,1,0:T(8,128)} %param.15) | copy-start | bytes 393220
  2.6 22.6 %all-to-all-start = ((f32[8,3,32,256]{3,2,1,0:T(8,128)}), f32[8,3,32,256]{3,2,1,0:T(8,128)S(1)}, u32[]{:S(2)}, u32[]{:S(2)}) async-start(f32[8,3,32,256]{3,2,1,0:T(8,128)} %broadcast_in_dim.127), calls=%async_computation | async-start | bytes 1572864 | tf_op jit(solution)/shard_map/all_to_all | solution.py:21
  25.8 22.1 %copy-start.8 = (f32[32,32]{1,0:T(8,128)S(1)}, f32[32,32]{1,0:T(8,128)}, u32[]{:S(2)}) copy-start(f32[32,32]{1,0:T(8,128)} %param.20) | copy-start | bytes 12292
  26.7 21.0 %all-to-all-start.1 = ((f32[64,8,128]{2,1,0:T(8,128)}), f32[64,8,128]{2,1,0:T(8,128)S(1)}, u32[]{:S(2)}, u32[]{:S(2)}) async-start(f32[64,8,128]{2,1,0:T(8,128)} %copy.86), calls=%async_computation.1 | async-start | bytes 524288 | tf_op jit(solution)/shard_map/all_to_all | solution.py:21
  48.9 6.1 %copy-start.7 = (f32[32,2,32]{2,1,0:T(2,128)S(1)}, f32[32,2,32]{2,1,0:T(2,128)}, u32[]{:S(2)}) copy-start(f32[32,2,32]{2,1,0:T(2,128)} %param.23) | copy-start | bytes 24580
  49.8 18.2 %copy-start.1 = (f32[32,4096]{1,0:T(8,128)S(1)}, f32[32,4096]{1,0:T(8,128)}, u32[]{:S(2)}) copy-start(f32[32,4096]{1,0:T(8,128)} %param.22) | copy-start | bytes 1572868
  49.8 18.0 %all-to-all-start.2 = ((f32[64,8,128]{2,1,0:T(8,128)}), f32[64,8,128]{2,1,0:T(8,128)S(1)}, u32[]{:S(2)}, u32[]{:S(2)}) async-start(f32[64,8,128]{2,1,0:T(8,128)} %copy.89), calls=%async_computation.2 | async-start | bytes 524288 | tf_op jit(solution)/shard_map/all_to_all | solution.py:21
  216.5 17.9 %all-to-all-start.13 = ((f32[64,8,128]{2,1,0:T(8,128)}), f32[64,8,128]{2,1,0:T(8,128)S(1)}, u32[]{:S(2)}, u32[]{:S(2)}) async-start(f32[64,8,128]{2,1,0:T(8,128)} %broadcast_in_dim.141), calls=%async_computation.13 | async-start | bytes 524288 | tf_op jit(solution)/shard_map/all_to_all | solution.py:21
  235.5 1.8 copy-start.4

commit v4 on v3

--- a/solution.py
+++ b/solution.py
@@ -5,8 +5,8 @@
 from jax.sharding import PartitionSpec as P
 
 EXACT = lax.Precision.HIGHEST
-NEAR = ("x", "core")
 DEV = ("z", "x", "core")
+LINE = ("z", "core")
 
 
 def mm(left, right):
@@ -43,8 +43,8 @@
 
 def make_body(sizes):
     n_grp, n_z = sizes["grp"], sizes["z"]
-    n_near = sizes["x"] * sizes["core"]
-    n_dev = n_z * n_near
+    n_x, n_core = sizes["x"], sizes["core"]
+    n_dev = n_z * n_x * n_core
 
     def body(
         leaf_right,
@@ -67,12 +67,13 @@
         n_front = front_order // width
         share = front_inverse.shape[0]
         part = root_inverse.shape[2]
-        few = rows // n_near
         live = live_blocks[0]
-        my_dev = lax.axis_index(DEV)
 
-        chain = jnp.concatenate([root_inverse, root_couple], 0)
-        chain = spread(chain, NEAR, n_near).transpose(1, 0, 2, 3).reshape(3, n_near * share, part)
+        with jax.named_scope("gather_x"):
+            chain = jnp.concatenate([root_inverse, root_couple], 0)
+            chain = spread(chain, "x", n_x).transpose(1, 0, 2, 3).reshape(3, n_x * share, part)
+        couple = front_couple.reshape(share, 2, n_z, n_x, n_core, share)
+        couple = couple.transpose(0, 1, 2, 4, 3, 5).reshape(share, 2 * front_order)
 
         def dev_sum(natural):
             chunks = natural.reshape(4, rows // 4, n_dev, share).transpose(2, 1, 0, 3)
@@ -93,32 +94,53 @@
             slots == front_rows[1], given1[:, None, :], 0.0
         )
         placed, chain = lax.optimization_barrier((placed, chain))
-        w_low, w_high, link = chain[0], chain[1], chain[2]
-        start = front_right - dev_sum(placed.reshape(rows, front_order))
-        y_own = dev_sum(mm(start, front_inverse))
+        with jax.named_scope("gather_grp"):
+            chain = lax.all_gather(chain, "grp", axis=0, tiled=False)
+        with jax.named_scope("sum_u"):
+            update = dev_sum(placed.reshape(rows, front_order))
+        with jax.named_scope("sum_y"):
+            y_own = dev_sum(mm(front_right - update, front_inverse))
 
-        spots = my_dev * share + jnp.arange(share, dtype=jnp.int32)
+        place = (lax.axis_index("z") * n_core + lax.axis_index("core")) * n_x + lax.axis_index("x")
+        spots = place * share + jnp.arange(share, dtype=jnp.int32)
         spots = jnp.concatenate([spots, front_order + spots])[:, None]
         picks = spots == jnp.arange(2 * front_order, dtype=jnp.int32)[None, :]
         picks = jnp.where(picks & (lax.axis_index("grp") == 0), 1.0, 0.0).astype(jnp.float32)
         fed = jnp.concatenate([-y_own, root_right[:, 0], root_right[:, 1]], 1)
-        given = mm(fed, jnp.concatenate([front_couple, picks], 0))
-        chunks = given.reshape(n_near, few, 2, n_z, part).transpose(3, 0, 2, 1, 4)
-        given = jnp.sum(swap(chunks.reshape(n_dev, 2 * few, part), DEV), 0)
-        given = reduce_over(given, "grp", n_grp)
+        given = mm(fed, jnp.concatenate([couple, picks], 0))
+        chunks = given.reshape(n_x, n_grp, 2, n_z, n_core, n_x * share).transpose(3, 0, 4, 1, 2, 5)
+        with jax.named_scope("sum_v"):
+            given = jnp.sum(swap(chunks.reshape(n_dev, n_grp, 2 * n_x * share), DEV), 0)
+        given, chain = lax.optimization_barrier((given, chain))
+        with jax.named_scope("sum_g"):
+            given = reduce_over(given, "grp", n_grp)
+        mine = jnp.arange(n_grp, dtype=jnp.int32)[:, None] == lax.axis_index("grp")
+        given = jnp.sum(jnp.where(mine, given, 0.0), 0, keepdims=True)
 
-        low, high = given[:few], given[few:]
-        y_high = reduce_over(mm(high, w_high), "z", n_z)
-        low = low - reduce_over(mmt(y_high, link), "grp", n_grp)
-        y_low = reduce_over(mm(low, w_low), "z", n_z)
-        x_low = reduce_over(mmt(y_low, w_low), "grp", n_grp)
-        y_high = y_high - reduce_over(mm(x_low, link), "z", n_z)
-        x_high = reduce_over(mmt(y_high, w_high), "grp", n_grp)
+        w_low, w_high, link = chain[:, 0], chain[:, 1], chain[:, 2]
 
-        whole = spread(jnp.concatenate([x_low, x_high], 0), DEV, n_dev)
-        whole = whole.reshape(n_z, n_near, 2, few, part).transpose(1, 3, 2, 0, 4)
+        def across(values, matrix):
+            wide = jnp.einsum("rk,gkc->rgc", values, matrix, precision=EXACT)
+            return reduce_over(wide.reshape(n_grp, part), LINE, n_z * n_core)
+
+        def along(values, matrix):
+            return jnp.einsum("gc,gkc->k", values, matrix, precision=EXACT)[None, :]
+
+        low, high = given[:, : n_x * share], given[:, n_x * share :]
+        y_high = across(high, w_high)
+        low = low - along(y_high, link)
+        x_low = along(across(low, w_low), w_low)
+        x_high = along(y_high - across(x_low, link), w_high)
+
+        with jax.named_scope("root_g"):
+            both = jnp.concatenate([x_low, x_high], 1)
+            whole = spread(both, "grp", n_grp).reshape(n_grp, 2 * n_x * share)
+        with jax.named_scope("root_d"):
+            whole = spread(whole, DEV, n_dev)
+        whole = whole.reshape(n_z, n_x, n_core, n_grp, 2, n_x * share).transpose(1, 3, 4, 0, 2, 5)
         whole = whole.reshape(rows, 2 * front_order)
-        rest = dev_columns(y_own - mmt(whole, front_couple))
+        rest = y_own - mmt(whole, couple)
+        rest = dev_columns(rest)
         front_solution = dev_columns(mmt(rest, front_inverse))
 
         def back(solved, block):
@@ -131,7 +153,7 @@
         leaf0 = jnp.where(live > 0, mmt(base0 - carried, leaf_inverse[0]), 0.0)
         leaf_solution = jnp.concatenate([leaf0, leaf1], 1)
         root = whole.reshape(rows, 2, front_order)
-        root = lax.dynamic_slice(root, (0, 0, my_dev * share), (rows, 2, share))
+        root = lax.dynamic_slice(root, (0, 0, place * share), (rows, 2, share))
         return leaf_solution, front_solution, root
 
     return body

time: 238 us -> 247 us (1.038)
  blocking collectives: 141 us -> 112 us
  between operations: 3.18 us -> 17.2 us
  matrix products: 5.27 us -> 18.3 us
  waiting for transfers between devices: 45.1 us -> 34.6 us
  local copies, waits for them, and re-layouts: 10.5 us -> 19.9 us
  starting transfers between devices: 28 us -> 36.3 us
  other arithmetic: 3.64 us -> 7.87 us
    all_to_all x10 -> x7, blocking collectives: 141 us -> 112 us  [swap(): return lax.all_to_all(chunks, axes, 0, 0, tiled=True)]
    all_to_all x4 -> x5, waiting for transfers between devices: 45.1 us -> 34.6 us  [swap(): return lax.all_to_all(chunks, axes, 0, 0, tiled=True)]
    dot_general x0 -> x6, matrix products: none -> 8.97 us  [the longest x3 4.68 us: along(): return jnp.einsum('gc,gkc->k', values, matrix, precision=EXACT)[None, :]]
    all_to_all x4 -> x5, starting transfers between devices: 28 us -> 36.3 us  [swap(): return lax.all_to_all(chunks, axes, 0, 0, tiled=True)]
    reshape x2 -> x4, local copies, waits for them, and re-layouts: 0.62 us -> 7.67 us  [the longest x2 5.7 us: body(): couple = front_couple.reshape(share, 2, n_z, n_x, n_core, share)]
    dot_general x10 -> x7, matrix products: 2.58 us -> 7.5 us  [mm(): return jnp.dot(left, right, precision=EXACT)]
  transfers between devices with their start and end apart: 4 -> 6, of which waited for: 4 -> 4; matrix products, arithmetic and copies ran while one was open for 2% -> 10% of each run, Pallas kernels for 0% -> 0%
where the time goes in v4:
time: 247 us; the launch traced here: 246 us
  blocking collectives  112 us (45%)
  starting transfers between devices  36.3 us (15%)
  waiting for transfers between devices  34.6 us (14%)
  local copies, waits for them, and re-layouts  19.9 us (8%)
  matrix products  18.3 us (7%)
  between operations  17.2 us (7%)
  other arithmetic  7.87 us (3%)
    all_to_all x7, blocking collectives, swap(): return lax.all_to_all(chunks, axes, 0, 0, tiled=True)  112 us
    all_to_all x5, starting transfers between devices, swap(): return lax.all_to_all(chunks, axes, 0, 0, tiled=True)  36.3 us
    all_to_all x5, waiting for transfers between devices, swap(): return lax.all_to_all(chunks, axes, 0, 0, tiled=True)  34.6 us
    dot_general x7, matrix products, mm(): return jnp.dot(left, right, precision=EXACT)  7.5 us
    reshape x2, local copies, waits for them, and re-layouts, body(): couple = front_couple.reshape(share, 2, n_z, n_x, n_core, share)  5.7 us
  transfers between devices with their start and end apart: 6, of which 4 were waited for; matrix products, arithmetic and copies ran while one was open for 10% of the time, Pallas kernels for 0%

profile of v4, /device:TPU:1, one launch (start us, length us, event | category | flops | bytes accessed | tf_op | source)
XLA Modules:
  0.0 246.1 jit_solution(12490410275332328704)
XLA Ops:
  7.2 0.9 pad_maximum_fusion
  8.1 0.8 broadcast_in_dim.140
  8.9 4.8 %all-to-all-start = ((f32[4,3,32,256]{3,2,1,0:T(8,128)}), f32[4,3,32,256]{3,2,1,0:T(8,128)S(1)}, u32[]{:S(2)}, u32[]{:S(2)}) async-start(f32[4,3,32,256]{3,2,1,0:T(8,128)} %broadcast_in_dim.140), calls=%async_computation | async-start | bytes 786432 | tf_op jit(solution)/shard_map/gather_x/all_to_all | solution.py:21
  15.0 1.0 convolution_select_fusion.5
  16.0 1.0 fusion.36
  17.1 1.0 fusion.6
  18.1 1.0 convolution_select_fusion.3
  19.1 1.0 fusion.29
  20.1 1.4 fusion.68
  21.5 1.3 iota_compare_fusion.2
  22.9 0.8 copy.64
  24.3 0.9 copy.66
  25.2 14.8 %all-to-all-start.1 = ((f32[64,8,128]{2,1,0:T(8,128)}), f32[64,8,128]{2,1,0:T(8,128)S(1)}, u32[]{:S(2)}, u32[]{:S(2)}) async-start(f32[64,8,128]{2,1,0:T(8,128)} %copy.66), calls=%async_computation.1 | async-start | bytes 524288 | tf_op jit(solution)/shard_map/sum_u/all_to_all | solution.py:21
  40.1 13.0 %all-to-all-done.1 = f32[64,8,128]{2,1,0:T(8,128)S(1)} async-done(((f32[64,8,128]{2,1,0:T(8,128)}), f32[64,8,128]{2,1,0:T(8,128)S(1)}, u32[]{:S(2)}, u32[]{:S(2)}) %all-to-all-start.1) | async-done | bytes 262176 | tf_op jit(solution)/shard_map/sum_u/all_to_all | solution.py:21
  54.3 0.9 copy.69
  55.2 4.8 %all-to-all-start.2 = ((f32[64,8,128]{2,1,0:T(8,128)}), f32[64,8,128]{2,1,0:T(8,128)S(1)}, u32[]{:S(2)}, u32[]{:S(2)}) async-start(f32[64,8,128]{2,1,0:T(8,128)} %copy.69), calls=%async_computation.2 | async-start | bytes 524288 | tf_op jit(solution)/shard_map/sum_y/all_to_all | solution.py:21
  60.0 1.3 fusion.20
  61.2 3.1 %reshape.122 = f32[32,2,8,4,2,32]{5,4,3,2,1,0:T(2,128)} reshape(f32[32,4096]{1,0:T(8,128)S(1)} %copy-done.4) | data formatting | bytes 1048576 | tf_op jit(solution)/shard_map/reshape | solution.py:75
  64.3 2.6 %copy.111 = f32[32,2,8,4,2,32]{5,3,4,2,1,0:T(4,128)S(1)} copy(f32[32,2,8,4,2,32]{5,4,3,2,1,0:T(2,128)} %reshape.122) | data formatting | bytes 1048576 | tf_op jit(solution)/shard_map/reshape | solution.py:75
  66.9 1.9 reshape.123
  68.9 4.2 %all-to-all-done.2 = f32[64,8,128]{2,1,0:T(8,128)S(1)} async-done(((f32[64,8,128]{2,1,0:T(8,128)}), f32[64,8,128]{2,1,0:T(8,128)S(1)}, u32[]{:S(2)}, u32[]{:S(2)}) %all-to-all-start.2) | async-done | bytes 262176 | tf_op jit(solution)/shard_map/sum_y/all_to_all | solution.py:21
  73.2 2.1 fusion
  75.4 23.7 %all_to_all.60 = f32[64,8,256]{2,1,0:T(8,128)S(1)} all-to-all(f32[64,8,256]{2,1,0:T(8,128)S(1)} %bitcast.173), channel_id=1, replica_groups=mesh['grp'=8,'z'=8,'x'=4,'core'=2] {'z','x','core'}, dimensions={0} | all-to-all | bytes 1048576 | tf_op jit(solution)/shard_map/sum_v/all_to_all | solution.py:21
  99.2 0.6 broadcast_in_dim.144
  99.8 7.0 %all-to-all-start.4 = ((f32[8,8,256]{2,1,0:T(8,128)}), f32[8,8,256]{2,1,0:T(8,128)S(1)}, u32[]{:S(2)}, u32[]{:S(2)}) async-start(f32[8,8,256]{2,1,0:T(8,128)} %broadcast_in_dim.144), calls=%async_computation.4 | async-start | bytes 131072 | tf_op jit(solution)/shard_map/sum_g/all_to_all | solution.py:21
  106.8 7.2 %all-to-all-done.4 = f32[8,8,256]{2,1,0:T(8,128)S(1)} async-done(((f32[8,8,256]{2,1,0:T(8,128)}), f32[8,8,256]{2,1,0:T(8,128)S(1)}, u32[]{:S(2)}, u32[]{:S(2)}) %all-to-all-start.4) | async-done | bytes 65568 | tf_op jit(solution)/shard_map/sum_g/all_to_all | solution.py:21
  114.1 1.8 fusion.17
  116.0 14.7 %all_to_all.61 = f32[16,8,256]{2,1,0:T(8,128)S(1)} all-to-all(f32[16,8,256]{2,1,0:T(8,128)S(1)} %broadcast_in_dim.147), channel_id=1, replica_groups=mesh['grp'=8,'z'=8,'x'=4,'core'=2] {'z','core'}, dimensions={0} | all-to-all | bytes 262144 | tf_op jit(solution)/shard_map/all_to_all | solution.py:21
  130.6 0.6 reduce_sum.77
  131.2 2.2 fusion.8
  133.4 1.8 fusion.11
  135.3 11.6 %all_to_all.62 = f32[16,8,256]{2,1,0:T(8,128)S(1)} all-to-all(f32[16,8,256]{2,1,0:T(8,128)S(1)} %broadcast_in_dim.149), channel_id=1, replica_groups=mesh['grp'=8,'z'=8,'x'=4,'core'=2] {'z','core'}, dimensions={0} | all-to-all | bytes 262144 | tf_op jit(solution)/shard_map/all_to_all | solution.py:21
  146.8 0.6 reduce_sum.78
  147.4 1.6 fusion.9
  149.0 0.6 fusion.13
  149.7 11.6 %all_to_all.63 = f32[16,8,256]{2,1,0:T(8,128)S(1)} all-to-all(f32[16,8,256]{2,1,0:T(8,128)S(1)} %broadcast_in_dim.151), channel_id=1, replica_groups=mesh['grp'=8,'z'=8,'x'=4,'core'=2] {'z','core'}, dimensions={0} | all-to-all | bytes 262144 | tf_op jit(solution)/shard_map/all_to_all | solution.py:21
  161.2 0.6 reduce_sum.79
  161.9 0.7 subtract_bitcast_fusion
  162.6 0.9 convolution_bitcast_fusion.1
  163.5 0.7 pad_maximum_fusion.2
  164.2 8.9 %all_to_all.64 = f32[8,1,256]{2,1,0:T(1,128)S(1)} all-to-all(f32[8,1,256]{2,1,0:T(1,128)S(1)} %broadcast_in_dim.154), channel_id=1, replica_groups=mesh['grp'=8,'z'=8,'x'=4,'core'=2] {'grp'}, dimensions={0} | all-to-all | bytes 16384 | tf_op jit(solution)/shard_map/root_g/all_to_all | solution.py:21
  173.2 23.0 %all_to_all.65 = f32[64,8,256]{2,1,0:T(8,128)S(1)} all-to-all(f32[64,8,256]{2,1,0:T(8,128)S(1)} %broadcast_in_dim.156), channel_id=1, replica_groups=mesh['grp'=8,'z'=8,'x'=4,'core'=2] {'z','x','core'}, dimensions={0} | all-to-all | bytes 1048576 | tf_op jit(solution)/shard_map/root_d/all_to_all | solution.py:21
  197.6 18.6 %all_to_all.66 = f32[64,8,128]{2,1,0:T(8,128)S(1)} all-to-all(f32[64,8,128]{2,1,0:T(8,128)S(1)} %broadcast_in_dim.158), channel_id=1, replica_groups=mesh['grp'=8,'z'=8,'x'=4,'core'=2] {'z','x','core'}, dimensions={0} | all-to-all | bytes 524288 | tf_op jit(solution)/shard_map/all_to_all | solution.py:21
  217.7 0.7 broadcast_in_dim.160
  218.4 4.9 %all-to-all-start.11 = ((f32[64,8,128]{2,1,0:T(8,128)}), f32[64,8,128]{2,1,0:T(8,128)S(1)}, u32[]{:S(2)}, u32[]{:S(2)}) async-start(f32[64,8,128]{2,1,0:T(8,128)} %broadcast_in_dim.160), calls=%async_computation.11 | async-start | bytes 524288 | tf_op jit(solution)/shard_map/all_to_all | solution.py:21
  225.5 0.6 copy.83
  226.1 10.3 %all-to-all-done.11 = f32[64,8,128]{2,1,0:T(8,128)S(1)} async-done(((f32[64,8,128]{2,1,0:T(8,128)}), f32[64,8,128]{2,1,0:T(8,128)S(1)}, u32[]{:S(2)}, u32[]{:S(2)}) %all-to-all-start.11) | async-done | bytes 262176 | tf_op jit(solution)/shard_map/all_to_all | solution.py:21
  238.6 0.6 pad_maximum_fusion.1
  (89 shorter events, 8.3 us)
Async XLA Ops:
  7.2 46.1 %copy-start = (f32[32,2048]{1,0:T(8,128)S(1)}, f32[32,2048]{1,0:T(8,128)}, u32[]{:S(2)}) copy-start(f32[32,2048]{1,0:T(8,128)} %param.21) | copy-start | bytes 786436
  8.9 14.0 %all-to-all-start = ((f32[4,3,32,256]{3,2,1,0:T(8,128)}), f32[4,3,32,256]{3,2,1,0:T(8,128)S(1)}, u32[]{:S(2)}, u32[]{:S(2)}) async-start(f32[4,3,32,256]{3,2,1,0:T(8,128)} %broadcast_in_dim.140), calls=%async_computation | async-start | bytes 786432 | tf_op jit(solution)/shard_map/gather_x/all_to_all | solution.py:21
  13.7 85.4 %all-gather.3.cloned.1.call-start = ((), (), s32[]{:S(2)}) async-start(), calls=%async_computation.12 | async-start | bytes 3538944 | tf_op jit(solution)/shard_map/gather_grp/all_gather | solution.py:98
  17.0 36.2 %copy-start.14 = (f32[32,32]{1,0:T(8,128)S(1)}, f32[32,32]{1,0:T(8,128)}, u32[]{:S(2)}) copy-start(f32[32,32]{1,0:T(8,128)} %param.20) | copy-start | bytes 12292
  19.1 4.6 %copy-start.10 = (f32[32,128]{1,0:T(8,128)}, f32[32,128]{1,0:T(8,128)S(1)}, u32[]{:S(2)}) copy-start(f32[32,128]{1,0:T(8,128)S(1)} %convolution_select_fusion.3) | copy-start | bytes 49156
  25.2 27.9 %all-to-all-start.1 = ((f32[64,8,128]{2,1,0:T(8,128)}), f32[64,8,128]{2,1,0:T(8,128)S(1)}, u32[]{:S(2)}, u32[]{:S(2)}) async-start(f32[64,8,128]{2,1,0:T(8,128)} %copy.66), calls=%async_computation.1 | async-start | bytes 524288 | tf_op jit(solution)/shard_map/sum_u/all_to_all | solution.py:21
  40.0 21.2 %copy-start.4 = (f32[32,4096]{1,0:T(8,128)S(1)}, f32[32,4096]{1,0:T(8,128)}, u32[]{:S(2)}) copy-start(f32[32,4096]{1,0:T(8,128)} %param.22) | copy-start | bytes 1572868
  55.2 17.9 %all-to-all-start.2 = ((f32[64,8,128]{2,1,0:T(8,128)}), f32[64,8,128]{2,1,0:T(8,128)S(1)}, u32[]{:S(2)}, u32[]{:S(2)}) async-start(f32[64,8,128]{2,1,0:T(8,128)} %copy.69), calls=%async_computation.2 | async-start | bytes 524288 | tf_op jit(solution)/shard_map/sum_y/all_to_all | solution.py:21
  64.3 4.5 %copy-start.13 = (f32[32,2,32]{2,1,0:T(2,128)S(1)}, f32[32,2,32]{2,1,0:T(2,128)}, u32[]{:S(2)}) copy-start(f32[32,2,32]{2,1,0:T(2,128)} %param.23) | copy-start | bytes 24580
  68.8 30.3 %copy-start.2 = (f32[32,4096]{1,0:T(8,128)}, f32[32,4096]{1,0:T(8,128)S(1)}, u32[]{:S(2)}) copy-start(f32[32,4096]{1,0:T(8,128)S(1)} %reshape.123) | copy-start | bytes 1572868
  73.2 2.2 copy-start.8
  99.2 48.3 %copy-start.1 = (f32[24,128,256]{2,1,0:T(8,128)S(1)}, f32[24,128,256]{2,1,0:T(8,128)}, u32[]{:S(2)}) copy-start(f32[24,128,256]{2,1,0:T(8,128)} %all-gather.3.cloned.1.call-done) | copy-start | bytes 9437188
  99.8 14.2 %all-to-all-start.4 = ((f32[8,8,256]{2,1,0:T(8,128)}), f32[8,8,256]{2,1,0:T(8,128)S(1)}, u32[]{:S(2)}, u32[]{:S(2)}) async-start(f32[8,8,256]{2,1,0:T(8,128)} %broadcast_in_dim.144), calls=%async_computation.4 | async-start | bytes 131072 | tf_op jit(solution)/shard_map/sum_g/all_to_all | solution.py:21
  114.1 1.8 copy-start.16
  149.0 0.7 copy-start.15
  161.9 35.0 %copy-start.9 = (f32[8,4,32]{2,1,0:T(4,128)S(1)}, f32[8,4,32]{2,1,0:T(4,128)}, u32[]{:S(2)}) copy-start(f32[8,4,32]{2,1,0:T(4,128)} %copy-done.8) | copy-start | bytes 12292
  163.5 33.4 %copy-start.3 = (f32[32,4096]{1,0:T(8,128)S(1)}, f32[32,4096]{1,0:T(8,128)}, u32[]{:S(2)}) copy-start(f32[32,4096]{1,0:T(8,128)} %copy-done.2) | copy-start | bytes 1572868
  218.4 19.1 %copy-start.5 = (f32[2,128,128]{2,1,0:T(8,128)S(1)}, f32[2,128,128]{2,1,0:T(8,128)}, u32[]{:S(2)}) copy-start(f32[2,128,128]{2,1,0:T(8,128)} %param.16) | copy-start | bytes 393220
  218.4 19.1 %copy-start.11 = (f32[32,128]{1,0:T(8,128)S(1)}, f32[32,128]{1,0:T(8,128)}, u32[]{:S(2)}) copy-start(f32[32,128]{1,0:T(8,128)} %copy-done.10) | copy-start | bytes 49156
  218.4 18.0 %all-to-all-start.11 = ((f32[64,8,128]{2,1,0:T(8,128)}), f32[64,8,128]{2,1,0:T(8,128)S(1)}, u32[]{:S(2)}, u32[]{:S(2)}) async-start(f32[64,8,128]{2,1,0:T(8,128)} %broadcast_in_dim.160), calls=%async_computation.11 | async-start | bytes 524288 | tf_op jit(solution)/shard_map/all_to_all | solution.py:21
  223.3 14.4 %copy-start.6 = (f32[2,128,128]{2,1,0:T(8,128)S(1)}, f32[2,128,128]{2,1,0:T(8,128)}, u32[]{:S(2)}) copy-start(f32[2,128,128]{2,1,0:T(8,128)} %param.14) | copy-start | bytes 393220
  223.3 14.9 %copy-start.12 = (f32[2,128,128]{2,1,0:T(8,128)S(1)}, f32[2,128,128]{2,1,0:T(8,128)}, u32[]{:S(2)}) copy-start(f32[2,128,128]{2,1,0:T(8,128)} %param.15) | copy-start | bytes 393220
  237.5 1.8 copy-start.7
Sparse Core Ops, SparseCore 0:
  23.9 51.9 all-gather.2

commit v5 on v3

--- a/solution.py
+++ b/solution.py
@@ -5,7 +5,6 @@
 from jax.sharding import PartitionSpec as P
 
 EXACT = lax.Precision.HIGHEST
-NEAR = ("x", "core")
 DEV = ("z", "x", "core")
 
 
@@ -43,7 +42,8 @@
 
 def make_body(sizes):
     n_grp, n_z = sizes["grp"], sizes["z"]
-    n_near = sizes["x"] * sizes["core"]
+    n_x = sizes["x"]
+    n_near = n_x * sizes["core"]
     n_dev = n_z * n_near
 
     def body(
@@ -72,7 +72,7 @@
         my_dev = lax.axis_index(DEV)
 
         chain = jnp.concatenate([root_inverse, root_couple], 0)
-        chain = spread(chain, NEAR, n_near).transpose(1, 0, 2, 3).reshape(3, n_near * share, part)
+        chain = spread(chain, "x", n_x)
 
         def dev_sum(natural):
             chunks = natural.reshape(4, rows // 4, n_dev, share).transpose(2, 1, 0, 3)
@@ -92,6 +92,9 @@
         placed = jnp.where(slots == front_rows[0], given0[:, None, :], 0.0) + jnp.where(
             slots == front_rows[1], given1[:, None, :], 0.0
         )
+        placed, chain = lax.optimization_barrier((placed, chain))
+        chain = lax.all_gather(chain, "core", axis=0).transpose(2, 1, 0, 3, 4)
+        chain = chain.reshape(3, n_near * share, part)
         placed, chain = lax.optimization_barrier((placed, chain))
         w_low, w_high, link = chain[0], chain[1], chain[2]
         start = front_right - dev_sum(placed.reshape(rows, front_order))

time: 238 us -> 235 us (0.987)
  blocking collectives: 141 us -> 150 us
  waiting for transfers between devices: 45.1 us -> 39 us
  starting transfers between devices: 28 us -> 22.6 us
    all_gather x0 -> x1, blocking collectives: none -> 8.57 us  [body(): chain = lax.all_gather(chain, 'core', axis=0).transpose(2, 1, 0, 3, 4)]
    all_to_all x4, waiting for transfers between devices: 45.1 us -> 39 us  [swap(): return lax.all_to_all(chunks, axes, 0, 0, tiled=True)]
    all_to_all x4, starting transfers between devices: 28 us -> 22.6 us  [swap(): return lax.all_to_all(chunks, axes, 0, 0, tiled=True)]
where the time goes in v5:
time: 235 us; the launch traced here: 234 us
  blocking collectives  150 us (64%)
  waiting for transfers between devices  39 us (17%)
  starting transfers between devices  22.6 us (10%)
  local copies, waits for them, and re-layouts  10.4 us (4%)
  matrix products  5.27 us (2%)
  other arithmetic  3.74 us (2%)
  between operations  3.25 us (1%)
    all_to_all x10, blocking collectives, swap(): return lax.all_to_all(chunks, axes, 0, 0, tiled=True)  141 us
    all_to_all x4, waiting for transfers between devices, swap(): return lax.all_to_all(chunks, axes, 0, 0, tiled=True)  39 us
    all_to_all x4, starting transfers between devices, swap(): return lax.all_to_all(chunks, axes, 0, 0, tiled=True)  22.6 us
    all_gather x1, blocking collectives, body(): chain = lax.all_gather(chain, 'core', axis=0).transpose(2, 1, 0, 3, 4)  8.57 us
  transfers between devices with their start and end apart: 4, of which 4 were waited for; matrix products, arithmetic and copies ran while one was open for 2% of the time, Pallas kernels for 0%

profile of v5, /device:TPU:1, one launch (start us, length us, event | category | flops | bytes accessed | tf_op | source)
XLA Modules:
  0.0 234.3 jit_solution(54049640995547002)
XLA Ops:
  0.7 1.0 pad_maximum_fusion
  1.7 0.8 broadcast_in_dim.127
  2.4 4.8 %all-to-all-start = ((f32[4,3,32,256]{3,2,1,0:T(8,128)}), f32[4,3,32,256]{3,2,1,0:T(8,128)S(1)}, u32[]{:S(2)}, u32[]{:S(2)}) async-start(f32[4,3,32,256]{3,2,1,0:T(8,128)} %broadcast_in_dim.127), calls=%async_computation | async-start | bytes 786432 | tf_op jit(solution)/shard_map/all_to_all | solution.py:20
  8.0 0.7 fusion.66
  9.5 1.4 iota_compare_fusion.1
  11.0 2.5 %all-to-all-done = f32[4,3,32,256]{3,2,1,0:T(8,128)S(1)} async-done(((f32[4,3,32,256]{3,2,1,0:T(8,128)}), f32[4,3,32,256]{3,2,1,0:T(8,128)S(1)}, u32[]{:S(2)}, u32[]{:S(2)}) %all-to-all-start) | async-done | bytes 393248 | tf_op jit(solution)/shard_map/all_to_all | solution.py:20
  13.5 8.6 %all-gather = f32[8,3,32,256]{3,2,1,0:T(8,128)S(1)} all-gather(f32[4,3,32,256]{3,2,1,0:T(8,128)S(1)} %all-to-all-done), channel_id=2, replica_groups=mesh['grp'=8,'z'=8,'x'=4,'core'=2] {'core'}, dimensions={0}, use_global_device_ids=true | all-gather | bytes 1179648 | tf_op jit(solution)/shard_map/all_gather | solution.py:96
  22.1 0.3 reshape_reshape.6
  22.4 0.3 copy.86
  22.7 0.9 copy.87
  23.6 8.1 %all-to-all-start.1 = ((f32[64,8,128]{2,1,0:T(8,128)}), f32[64,8,128]{2,1,0:T(8,128)S(1)}, u32[]{:S(2)}, u32[]{:S(2)}) async-start(f32[64,8,128]{2,1,0:T(8,128)} %copy.87), calls=%async_computation.1 | async-start | bytes 524288 | tf_op jit(solution)/shard_map/all_to_all | solution.py:20
  31.8 13.0 %all-to-all-done.1 = f32[64,8,128]{2,1,0:T(8,128)S(1)} async-done(((f32[64,8,128]{2,1,0:T(8,128)}), f32[64,8,128]{2,1,0:T(8,128)S(1)}, u32[]{:S(2)}, u32[]{:S(2)}) %all-to-all-start.1) | async-done | bytes 262176 | tf_op jit(solution)/shard_map/all_to_all | solution.py:20
  44.9 0.4 fusion.55
  45.3 0.3 reshape.91
  45.6 0.3 copy.89
  46.0 0.9 copy.90
  46.9 4.9 %all-to-all-start.2 = ((f32[64,8,128]{2,1,0:T(8,128)}), f32[64,8,128]{2,1,0:T(8,128)S(1)}, u32[]{:S(2)}, u32[]{:S(2)}) async-start(f32[64,8,128]{2,1,0:T(8,128)} %copy.90), calls=%async_computation.2 | async-start | bytes 524288 | tf_op jit(solution)/shard_map/all_to_all | solution.py:20
  51.8 0.2 fusion.8
  52.1 12.8 %all-to-all-done.2 = f32[64,8,128]{2,1,0:T(8,128)S(1)} async-done(((f32[64,8,128]{2,1,0:T(8,128)}), f32[64,8,128]{2,1,0:T(8,128)S(1)}, u32[]{:S(2)}, u32[]{:S(2)}) %all-to-all-start.2) | async-done | bytes 262176 | tf_op jit(solution)/shard_map/all_to_all | solution.py:20
  65.0 0.9 fusion
  66.1 0.3 copy.94
  66.4 0.3 copy.95
  66.7 22.3 %all_to_all.70 = f32[64,8,256]{2,1,0:T(8,128)S(1)} all-to-all(f32[64,8,256]{2,1,0:T(8,128)S(1)} %copy.95), channel_id=1, replica_groups=mesh['grp'=8,'z'=8,'x'=4,'core'=2] {'z','x','core'}, dimensions={0} | all-to-all | bytes 1048576 | tf_op jit(solution)/shard_map/all_to_all | solution.py:20
  89.0 13.8 %all_to_all.71 = f32[8,8,256]{2,1,0:T(8,128)S(1)} all-to-all(f32[8,8,256]{2,1,0:T(8,128)S(1)} %broadcast_in_dim.130), channel_id=1, replica_groups=mesh['grp'=8,'z'=8,'x'=4,'core'=2] {'grp'}, dimensions={0} | all-to-all | bytes 131072 | tf_op jit(solution)/shard_map/all_to_all | solution.py:20
  103.1 10.2 %all_to_all.72 = f32[8,4,256]{2,1,0:T(4,128)S(1)} all-to-all(f32[8,4,256]{2,1,0:T(4,128)S(1)} %broadcast_in_dim.131), channel_id=1, replica_groups=mesh['grp'=8,'z'=8,'x'=4,'core'=2] {'z'}, dimensions={0} | all-to-all | bytes 65536 | tf_op jit(solution)/shard_map/all_to_all | solution.py:20
  113.4 0.3 fusion.16
  113.7 9.2 %all_to_all.73 = f32[8,4,256]{2,1,0:T(4,128)S(1)} all-to-all(f32[8,4,256]{2,1,0:T(4,128)S(1)} %broadcast_in_dim.132), channel_id=1, replica_groups=mesh['grp'=8,'z'=8,'x'=4,'core'=2] {'grp'}, dimensions={0} | all-to-all | bytes 65536 | tf_op jit(solution)/shard_map/all_to_all | solution.py:20
  123.2 9.2 %all_to_all.74 = f32[8,4,256]{2,1,0:T(4,128)S(1)} all-to-all(f32[8,4,256]{2,1,0:T(4,128)S(1)} %broadcast_in_dim.133), channel_id=1, replica_groups=mesh['grp'=8,'z'=8,'x'=4,'core'=2] {'z'}, dimensions={0} | all-to-all | bytes 65536 | tf_op jit(solution)/shard_map/all_to_all | solution.py:20
  132.5 0.3 fusion.10
  132.8 9.2 %all_to_all.75 = f32[8,4,256]{2,1,0:T(4,128)S(1)} all-to-all(f32[8,4,256]{2,1,0:T(4,128)S(1)} %broadcast_in_dim.134), channel_id=1, replica_groups=mesh['grp'=8,'z'=8,'x'=4,'core'=2] {'grp'}, dimensions={0} | all-to-all | bytes 65536 | tf_op jit(solution)/shard_map/all_to_all | solution.py:20
  142.3 9.2 %all_to_all.76 = f32[8,4,256]{2,1,0:T(4,128)S(1)} all-to-all(f32[8,4,256]{2,1,0:T(4,128)S(1)} %broadcast_in_dim.135), channel_id=1, replica_groups=mesh['grp'=8,'z'=8,'x'=4,'core'=2] {'z'}, dimensions={0} | all-to-all | bytes 65536 | tf_op jit(solution)/shard_map/all_to_all | solution.py:20
  151.6 0.3 fusion.18
  151.9 9.2 %all_to_all.77 = f32[8,4,256]{2,1,0:T(4,128)S(1)} all-to-all(f32[8,4,256]{2,1,0:T(4,128)S(1)} %broadcast_in_dim.136), channel_id=1, replica_groups=mesh['grp'=8,'z'=8,'x'=4,'core'=2] {'grp'}, dimensions={0} | all-to-all | bytes 65536 | tf_op jit(solution)/shard_map/all_to_all | solution.py:20
  161.2 30.4 %all_to_all.78 = f32[64,8,256]{2,1,0:T(8,128)S(1)} all-to-all(f32[64,8,256]{2,1,0:T(8,128)S(1)} %broadcast_in_dim.137), channel_id=1, replica_groups=mesh['grp'=8,'z'=8,'x'=4,'core'=2] {'z','x','core'}, dimensions={0} | all-to-all | bytes 1048576 | tf_op jit(solution)/shard_map/all_to_all | solution.py:20
  192.1 0.5 fusion.5
  192.8 18.6 %all_to_all.79 = f32[64,8,128]{2,1,0:T(8,128)S(1)} all-to-all(f32[64,8,128]{2,1,0:T(8,128)S(1)} %broadcast_in_dim.139), channel_id=1, replica_groups=mesh['grp'=8,'z'=8,'x'=4,'core'=2] {'z','x','core'}, dimensions={0} | all-to-all | bytes 524288 | tf_op jit(solution)/shard_map/all_to_all | solution.py:20
  211.5 0.4 copy.106
  211.9 0.5 dot_general.76
  212.4 0.3 convolution_bitcast_fusion
  212.8 0.7 broadcast_in_dim.141
  213.6 4.8 %all-to-all-start.13 = ((f32[64,8,128]{2,1,0:T(8,128)}), f32[64,8,128]{2,1,0:T(8,128)S(1)}, u32[]{:S(2)}, u32[]{:S(2)}) async-start(f32[64,8,128]{2,1,0:T(8,128)} %broadcast_in_dim.141), calls=%async_computation.13 | async-start | bytes 524288 | tf_op jit(solution)/shard_map/all_to_all | solution.py:20
  220.0 0.6 copy.111
  220.7 10.7 %all-to-all-done.13 = f32[64,8,128]{2,1,0:T(8,128)S(1)} async-done(((f32[64,8,128]{2,1,0:T(8,128)}), f32[64,8,128]{2,1,0:T(8,128)S(1)}, u32[]{:S(2)}, u32[]{:S(2)}) %all-to-all-start.13) | async-done | bytes 262176 | tf_op jit(solution)/shard_map/all_to_all | solution.py:20
  231.6 0.4 copy.109
  232.0 0.5 reshape.102
  232.9 0.2 convolution_subtract_fusion.1
  233.2 0.2 fusion.4
  233.6 0.6 pad_maximum_fusion.1
  (74 shorter events, 4.7 us)
Async XLA Ops:
  0.6 44.3 %copy-start = (f32[32,2048]{1,0:T(8,128)S(1)}, f32[32,2048]{1,0:T(8,128)}, u32[]{:S(2)}) copy-start(f32[32,2048]{1,0:T(8,128)} %param.21) | copy-start | bytes 786436
  0.6 7.3 %copy-start.10 = (s32[2]{0:T(128)S(1)}, s32[2]{0:T(128)}, u32[]{:S(2)}) copy-start(s32[2]{0:T(128)} %param.17) | copy-start | bytes 28
  0.7 7.3 %copy-start.9 = (s32[2]{0:T(128)S(1)}, s32[2]{0:T(128)}, u32[]{:S(2)}) copy-start(s32[2]{0:T(128)} %param.18) | copy-start | bytes 28
  0.7 8.0 %copy-start.3 = (f32[2,128,128]{2,1,0:T(8,128)S(1)}, f32[2,128,128]{2,1,0:T(8,128)}, u32[]{:S(2)}) copy-start(f32[2,128,128]{2,1,0:T(8,128)} %param.14) | copy-start | bytes 393220
  0.7 8.0 %copy-start.6 = (f32[32,256]{1,0:T(8,128)S(1)}, f32[32,256]{1,0:T(8,128)}, u32[]{:S(2)}) copy-start(f32[32,256]{1,0:T(8,128)} %param.13) | copy-start | bytes 98308
  0.7 8.1 %copy-start.2 = (f32[2,128,128]{2,1,0:T(8,128)S(1)}, f32[2,128,128]{2,1,0:T(8,128)}, u32[]{:S(2)}) copy-start(f32[2,128,128]{2,1,0:T(8,128)} %param.16) | copy-start | bytes 393220
  0.7 8.3 %copy-start.5 = (f32[2,128,128]{2,1,0:T(8,128)S(1)}, f32[2,128,128]{2,1,0:T(8,128)}, u32[]{:S(2)}) copy-start(f32[2,128,128]{2,1,0:T(8,128)} %param.15) | copy-start | bytes 393220
  2.4 11.1 %all-to-all-start = ((f32[4,3,32,256]{3,2,1,0:T(8,128)}), f32[4,3,32,256]{3,2,1,0:T(8,128)S(1)}, u32[]{:S(2)}, u32[]{:S(2)}) async-start(f32[4,3,32,256]{3,2,1,0:T(8,128)} %broadcast_in_dim.127), calls=%async_computation | async-start | bytes 786432 | tf_op jit(solution)/shard_map/all_to_all | solution.py:20
  22.7 22.2 %copy-start.8 = (f32[32,32]{1,0:T(8,128)S(1)}, f32[32,32]{1,0:T(8,128)}, u32[]{:S(2)}) copy-start(f32[32,32]{1,0:T(8,128)} %param.20) | copy-start | bytes 12292
  23.6 21.1 %all-to-all-start.1 = ((f32[64,8,128]{2,1,0:T(8,128)}), f32[64,8,128]{2,1,0:T(8,128)S(1)}, u32[]{:S(2)}, u32[]{:S(2)}) async-start(f32[64,8,128]{2,1,0:T(8,128)} %copy.87), calls=%async_computation.1 | async-start | bytes 524288 | tf_op jit(solution)/shard_map/all_to_all | solution.py:20
  46.0 6.1 %copy-start.7 = (f32[32,2,32]{2,1,0:T(2,128)S(1)}, f32[32,2,32]{2,1,0:T(2,128)}, u32[]{:S(2)}) copy-start(f32[32,2,32]{2,1,0:T(2,128)} %param.23) | copy-start | bytes 24580
  46.9 18.2 %copy-start.1 = (f32[32,4096]{1,0:T(8,128)S(1)}, f32[32,4096]{1,0:T(8,128)}, u32[]{:S(2)}) copy-start(f32[32,4096]{1,0:T(8,128)} %param.22) | copy-start | bytes 1572868
  46.9 18.0 %all-to-all-start.2 = ((f32[64,8,128]{2,1,0:T(8,128)}), f32[64,8,128]{2,1,0:T(8,128)S(1)}, u32[]{:S(2)}, u32[]{:S(2)}) async-start(f32[64,8,128]{2,1,0:T(8,128)} %copy.90), calls=%async_computation.2 | async-start | bytes 524288 | tf_op jit(solution)/shard_map/all_to_all | solution.py:20
  213.6 17.9 %all-to-all-start.13 = ((f32[64,8,128]{2,1,0:T(8,128)}), f32[64,8,128]{2,1,0:T(8,128)S(1)}, u32[]{:S(2)}, u32[]{:S(2)}) async-start(f32[64,8,128]{2,1,0:T(8,128)} %broadcast_in_dim.141), calls=%async_computation.13 | async-start | bytes 524288 | tf_op jit(solution)/shard_map/all_to_all | solution.py:20
  232.5 1.8 copy-start.4

commit v6 on v3

v6 whole, which is shorter than its diff:
```python
import jax
import jax.numpy as jnp
from jax import lax
from jax.sharding import Mesh
from jax.sharding import PartitionSpec as P


EXACT = lax.Precision.HIGHEST
DEV = ("z", "x", "core")
LINE = ("z", "core")


def mm(left, right):
    return jnp.dot(left, right, precision=EXACT)


def mmt(left, right):
    return jnp.einsum("rn,mn->rm", left, right, precision=EXACT)


def swap(chunks, axes):
    return lax.all_to_all(chunks, axes, 0, 0, tiled=True)


def spread(values, axes, count):
    return swap(jnp.broadcast_to(values[None], (count,) + values.shape), axes)


def reduce_over(values, axes, count):
    return jnp.sum(spread(values, axes, count), 0)


def make_body(sizes):
    n_grp, n_z = sizes["grp"], sizes["z"]
    n_x, n_core = sizes["x"], sizes["core"]
    n_line = n_z * n_core
    n_dev = n_line * n_x

    def body(
        leaf_right,
        leaf_inverse,
        leaf_link,
        leaf_front,
        parents,
        front_rows,
        live_blocks,
        front_right,
        front_inverse,
        front_couple,
        root_right,
        root_inverse,
        root_couple,
    ):
        rows = leaf_right.shape[0]
        width = leaf_inverse.shape[1]
        front_order = front_inverse.shape[1]
        n_front = front_order // width
        share = front_inverse.shape[0]
        part = root_inverse.shape[2]
        some, few = rows // n_x, rows // (n_x * n_core)
        live = live_blocks[0]
        my_z, my_x, my_core = (lax.axis_index(name) for name in DEV)

        def from_right(values, step):
            pairs = [((i + step) % n_x, i) for i in range(n_x)]
            return lax.ppermute(values, "x", pairs)

        def turn(values, steps):
            return lax.dynamic_slice_in_dim(
                jnp.concatenate([values, values], 1), steps * share, n_x * share, 1
            )

        small = (root_inverse, root_couple, root_right, front_right)
        bundle = jnp.concatenate([item.reshape(-1, part) for item in small], 0)
        tall = bundle.shape[0]
        bundle = jnp.pad(bundle, ((0, -tall % 8), (0, 0)))
        bundle = spread(bundle, "x", n_x)

        has_parent = parents[0] < live
        right0, right1 = leaf_right[:, :width], leaf_right[:, width:]
        solved0 = jnp.where(live > 0, mm(right0, leaf_inverse[0]), 0.0)
        lifted = jnp.where(has_parent, mm(solved0, leaf_link[0]), 0.0)
        solved1 = jnp.where(live > 1, mm(right1 - lifted, leaf_inverse[1]), 0.0)
        given0, given1 = mm(solved0, leaf_front[0]), mm(solved1, leaf_front[1])
        slots = jnp.arange(n_front, dtype=jnp.int32)[None, :, None]
        placed = jnp.where(slots == front_rows[0], given0[:, None, :], 0.0) + jnp.where(
            slots == front_rows[1], given1[:, None, :], 0.0
        )
        placed, bundle = lax.optimization_barrier((placed, bundle))
        bundle = lax.all_gather(bundle, "core", axis=0)
        placed, bundle = lax.optimization_barrier((placed, bundle))
        chain = bundle[:, :, : 3 * share].reshape(n_core, n_x, 3, share, part)
        chain = chain.transpose(2, 1, 0, 3, 4).reshape(3, n_x * n_core * share, part)
        w_low, w_high, link = chain[0], chain[1], chain[2]
        n_root = root_right.size // part
        sides = bundle[:, :, 3 * share : 3 * share + n_root]
        sides = lax.dynamic_index_in_dim(sides, my_x * n_core + my_core, 2, False)
        sides = sides.reshape(n_core, n_x, few, 2, share).transpose(3, 2, 1, 0, 4)
        sides = sides.reshape(2 * few, part)
        fronts = bundle[:, :, 3 * share + n_root : tall]
        fronts = lax.dynamic_index_in_dim(fronts, my_core, 0, False)
        fronts = lax.dynamic_index_in_dim(fronts, my_x, 1, False)
        fronts = fronts.reshape(n_x, some, share).transpose(1, 0, 2).reshape(some, n_x * share)

        inverses, couples = [front_inverse], [front_couple]
        for step in (1, 3, 2):
            inverses.append(from_right(front_inverse, step))
        for step in (1, 3, 2):
            couples.append(from_right(front_couple, step))
        order = (0, 1, 3, 2)
        inverses = [inverses[order.index(step)] for step in range(n_x)]
        couples = [couples[order.index(step)] for step in range(n_x)]

        def across(values, pieces):
            values = turn(values, my_x)
            return sum(
                mm(values[:, step * share : (step + 1) * share], piece)
                for step, piece in enumerate(pieces)
            )

        def along(values, pieces):
            found = jnp.concatenate([mmt(values, piece) for piece in pieces], 1)
            return turn(found, (n_x - my_x) % n_x)

        chunks = placed.reshape(n_x, some, n_z, n_x, n_core, share).transpose(2, 0, 4, 1, 3, 5)
        update = jnp.sum(swap(chunks.reshape(n_dev, some, n_x * share), DEV), 0)
        terms = across(fronts - update, inverses)
        chunks = terms.reshape(some, n_z, n_x, n_core, share).transpose(1, 3, 0, 2, 4)
        y_front = jnp.sum(swap(chunks.reshape(n_line, some, n_x * share), LINE), 0)
        raised = across(y_front, couples).reshape(n_core, few, 2, n_z, part)
        chunks = raised.transpose(3, 0, 2, 1, 4).reshape(n_line, 2 * few, part)
        raised = jnp.sum(swap(chunks, LINE), 0)
        given = sides - reduce_over(raised, "grp", n_grp)

        low, high = given[:few], given[few:]
        y_high = reduce_over(mm(high, w_high), "z", n_z)
        low = low - reduce_over(mmt(y_high, link), "grp", n_grp)
        y_low = reduce_over(mm(low, w_low), "z", n_z)
        x_low = reduce_over(mmt(y_low, w_low), "grp", n_grp)
        y_high = y_high - reduce_over(mm(x_low, link), "z", n_z)
        x_high = reduce_over(mmt(y_high, w_high), "grp", n_grp)

        whole = spread(jnp.concatenate([x_low, x_high], 0), LINE, n_line)
        whole = whole.reshape(n_z, n_core, 2, few, part).transpose(1, 3, 2, 0, 4)
        whole = whole.reshape(some, 2 * front_order)
        rest = spread(y_front - along(whole, couples), LINE, n_line)
        rest = rest.reshape(n_z, n_core, some, n_x, share).transpose(2, 0, 3, 1, 4)
        found = along(rest.reshape(some, front_order), inverses)
        root = whole.reshape(some, 2, n_z * n_x * n_core, share).transpose(2, 0, 1, 3)
        root = jnp.pad(root.reshape(n_dev, some, 2 * share), ((0, 0), (0, 0), (0, 2 * share)))
        found = jnp.broadcast_to(found[None], (n_dev, some, n_x * share))
        mixed = swap(jnp.concatenate([found, root], 2), DEV)
        front_solution = mixed[:, :, : n_x * share].reshape(n_z, n_x, n_core, some, n_x, share)
        front_solution = front_solution.transpose(1, 3, 0, 4, 2, 5).reshape(rows, front_order)
        root = mixed[:, :, n_x * share : (n_x + 2) * share]
        root = root.reshape(n_z, n_x, n_core, some, 2 * share)
        root = lax.dynamic_index_in_dim(root, my_z, 0, False)
        root = lax.dynamic_index_in_dim(root, my_core, 1, False).reshape(rows, 2, share)

        def back(solved, block):
            picked = lax.dynamic_slice(front_solution, (0, front_rows[block] * width), (rows, width))
            return solved - mmt(picked, leaf_front[block])

        base0, base1 = back(solved0, 0), back(solved1, 1)
        leaf1 = jnp.where(live > 1, mmt(base1, leaf_inverse[1]), 0.0)
        carried = jnp.where(has_parent, mmt(leaf1, leaf_link[0]), 0.0)
        leaf0 = jnp.where(live > 0, mmt(base0 - carried, leaf_inverse[0]), 0.0)
        leaf_solution = jnp.concatenate([leaf0, leaf1], 1)
        return leaf_solution, front_solution, root

    return body


def solution(mesh):
    n_grp, n_dev = mesh.shape["grp"], mesh.shape["dev"]
    fine = Mesh(mesh.devices.reshape(n_grp, n_dev // 8, 4, 2), ("grp", "z", "x", "core"))
    every = ("grp",) + DEV
    in_specs = (
        P(None, every),
        P(every, None, None),
        P(every, None, None),
        P(every, None, None),
        P(every),
        P(every),
        P(every),
        P(None, every),
        P(every, None),
        P(every, None),
        P(None, None, DEV),
        P(None, DEV, "grp"),
        P(None, DEV, "grp"),
    )
    out_specs = (P(None, every), P(None, "grp"), P(None, None, DEV))
    inner = make_body(dict(fine.shape))

    return jax.shard_map(inner, mesh=fine, in_specs=in_specs, out_specs=out_specs, check_vma=False)
```

time: 238 us -> 259 us (1.088)
  blocking collectives: 141 us -> 45.7 us
  starting transfers between devices: 28 us -> 83 us
  waiting for transfers between devices: 45.1 us -> 87.7 us
  local copies, waits for them, and re-layouts: 10.5 us -> 22.7 us
  matrix products: 5.27 us -> 9.02 us
    all_to_all x10 -> x4, blocking collectives: 141 us -> 37 us  [swap(): return lax.all_to_all(chunks, axes, 0, 0, tiled=True)]
    all_to_all x4 -> x10, starting transfers between devices: 28 us -> 64.1 us  [swap(): return lax.all_to_all(chunks, axes, 0, 0, tiled=True)]
    ppermute x0 -> x6, waiting for transfers between devices: none -> 22.6 us  [from_right(): return lax.ppermute(values, 'x', pairs)]
    all_to_all x4 -> x10, waiting for transfers between devices: 45.1 us -> 65 us  [swap(): return lax.all_to_all(chunks, axes, 0, 0, tiled=True)]
    ppermute x0 -> x6, starting transfers between devices: none -> 18.9 us  [from_right(): return lax.ppermute(values, 'x', pairs)]
    all_gather x0 -> x1, blocking collectives: none -> 8.67 us  [body(): bundle = lax.all_gather(bundle, 'core', axis=0)]
    reshape x10 -> x20, local copies, waits for them, and re-layouts: 3.49 us -> 8.95 us  [the longest x2 1.66 us: body(): bundle = jnp.concatenate([item.reshape(-1, part) for item in small], 0)]
    unnamed x24 -> x53, local copies, waits for them, and re-layouts: 0.88 us -> 3.66 us
  transfers between devices with their start and end apart: 4 -> 16, of which waited for: 4 -> 12; matrix products, arithmetic and copies ran while one was open for 2% -> 3% of each run, Pallas kernels for 0% -> 0%
where the time goes in v6:
time: 259 us; the launch traced here: 257 us
  waiting for transfers between devices  87.7 us (34%)
  starting transfers between devices  83 us (32%)
  blocking collectives  45.7 us (18%)
  local copies, waits for them, and re-layouts  22.7 us (9%)
  matrix products  9.02 us (3%)
  other arithmetic  5.75 us (2%)
  between operations  3.44 us (1%)
    all_to_all x10, waiting for transfers between devices, swap(): return lax.all_to_all(chunks, axes, 0, 0, tiled=True)  65 us
    all_to_all x10, starting transfers between devices, swap(): return lax.all_to_all(chunks, axes, 0, 0, tiled=True)  64.1 us
    all_to_all x4, blocking collectives, swap(): return lax.all_to_all(chunks, axes, 0, 0, tiled=True)  37 us
    ppermute x6, waiting for transfers between devices, from_right(): return lax.ppermute(values, 'x', pairs)  22.6 us
    ppermute x6, starting transfers between devices, from_right(): return lax.ppermute(values, 'x', pairs)  18.9 us
    all_gather x1, blocking collectives, body(): bundle = lax.all_gather(bundle, 'core', axis=0)  8.67 us
  transfers between devices with their start and end apart: 16, of which 12 were waited for; matrix products, arithmetic and copies ran while one was open for 3% of the time, Pallas kernels for 0%

profile of v6, /device:TPU:1, one launch (start us, length us, event | category | flops | bytes accessed | tf_op | source)
XLA Modules:
  0.0 257.3 jit_solution(15064847820181330161)
XLA Ops:
  0.6 0.8 reshape.123
  1.4 0.9 reshape.122
  2.3 0.9 select_maximum_fusion.1
  3.2 0.8 broadcast_in_dim.115
  4.0 5.0 %all-to-all-start = ((f32[4,112,256]{2,1,0:T(8,128)}), f32[4,112,256]{2,1,0:T(8,128)S(1)}, u32[]{:S(2)}, u32[]{:S(2)}) async-start(f32[4,112,256]{2,1,0:T(8,128)} %broadcast_in_dim.115), calls=%async_computation | async-start | bytes 917504 | tf_op jit(solution)/shard_map/all_to_all | solution.py:22
  11.7 1.3 iota_compare_fusion.2
  13.1 2.4 all-to-all-done
  15.5 8.7 %all-gather = f32[8,112,256]{2,1,0:T(8,128)S(1)} all-gather(f32[4,112,256]{2,1,0:T(8,128)S(1)} %all-to-all-done), channel_id=2, replica_groups=mesh['grp'=8,'z'=8,'x'=4,'core'=2] {'core'}, dimensions={0}, use_global_device_ids=true | all-gather | bytes 1376256 | tf_op jit(solution)/shard_map/all_gather | solution.py:90
  24.2 0.8 reshape.126
  25.3 1.2 reshape.127
  26.5 8.5 %all-to-all-start.1 = ((f32[64,8,128]{2,1,0:T(8,128)}), f32[64,8,128]{2,1,0:T(8,128)S(1)}, u32[]{:S(2)}, u32[]{:S(2)}) async-start(f32[64,8,128]{2,1,0:T(8,128)} %reshape.127), calls=%async_computation.1 | async-start | bytes 524288 | tf_op jit(solution)/shard_map/all_to_all | solution.py:22
  35.1 3.3 %collective-permute-start.2 = (f32[32,2048]{1,0:T(8,128)S(1)}, f32[32,2048]{1,0:T(8,128)S(1)}, u32[]{:S(2)}, u32[]{:S(2)}) collective-permute-start(f32[32,2048]{1,0:T(8,128)S(1)} %copy-done.3), channel_id=1, source_target_pairs={{6,0},{0,2},{2,4},{4,6},{7,1},{1,3},{3,5},{5,7},{14,8},{8,10},{10,... | collective-permute-start | bytes 786440 | tf_op jit(solution)/shard_map/ppermute | solution.py:66
  38.3 3.2 %collective-permute-start = (f32[32,2048]{1,0:T(8,128)S(1)}, f32[32,2048]{1,0:T(8,128)S(1)}, u32[]{:S(2)}, u32[]{:S(2)}) collective-permute-start(f32[32,2048]{1,0:T(8,128)S(1)} %copy-done.3), channel_id=1, source_target_pairs={{2,0},{4,2},{6,4},{0,6},{3,1},{5,3},{7,5},{1,7},{10,8},{12,10},{14... | collective-permute-start | bytes 786440 | tf_op jit(solution)/shard_map/ppermute | solution.py:66
  41.6 3.6 %collective-permute-start.1 = (f32[32,2048]{1,0:T(8,128)S(1)}, f32[32,2048]{1,0:T(8,128)S(1)}, u32[]{:S(2)}, u32[]{:S(2)}) collective-permute-start(f32[32,2048]{1,0:T(8,128)S(1)} %copy-done.3), channel_id=1, source_target_pairs={{4,0},{6,2},{0,4},{2,6},{5,1},{7,3},{1,5},{3,7},{12,8},{14,10},{8,... | collective-permute-start | bytes 786440 | tf_op jit(solution)/shard_map/ppermute | solution.py:66
  45.1 2.2 collective-permute-start.5
  49.2 5.3 %collective-permute-done.1 = f32[32,2048]{1,0:T(8,128)S(1)} collective-permute-done((f32[32,2048]{1,0:T(8,128)S(1)}, f32[32,2048]{1,0:T(8,128)S(1)}, u32[]{:S(2)}, u32[]{:S(2)}) %collective-permute-start.1) | collective-permute-done | bytes 262176 | tf_op jit(solution)/shard_map/ppermute | solution.py:66
  55.2 0.8 reshape.129
  56.0 7.5 %all-to-all-start.2 = ((f32[16,8,128]{2,1,0:T(8,128)}), f32[16,8,128]{2,1,0:T(8,128)S(1)}, u32[]{:S(2)}, u32[]{:S(2)}) async-start(f32[16,8,128]{2,1,0:T(8,128)} %reshape.129), calls=%async_computation.2 | async-start | bytes 131072 | tf_op jit(solution)/shard_map/all_to_all | solution.py:22
  63.5 4.2 %collective-permute-start.3 = (f32[32,4096]{1,0:T(8,128)S(1)}, f32[32,4096]{1,0:T(8,128)S(1)}, u32[]{:S(2)}, u32[]{:S(2)}) collective-permute-start(f32[32,4096]{1,0:T(8,128)S(1)} %copy-done), channel_id=1, source_target_pairs={{2,0},{4,2},{6,4},{0,6},{3,1},{5,3},{7,5},{1,7},{10,8},{12,10},{14... | collective-permute-start | bytes 1572872 | tf_op jit(solution)/shard_map/ppermute | solution.py:66
  67.7 2.4 collective-permute-start.4
  70.2 1.1 all-to-all-done.2
  72.7 17.3 %collective-permute-done.3 = f32[32,4096]{1,0:T(8,128)S(1)} collective-permute-done((f32[32,4096]{1,0:T(8,128)S(1)}, f32[32,4096]{1,0:T(8,128)S(1)}, u32[]{:S(2)}, u32[]{:S(2)}) %collective-permute-start.3) | collective-permute-done | bytes 524320 | tf_op jit(solution)/shard_map/ppermute | solution.py:66
  91.3 0.7 reshape.133
  92.0 8.0 %all-to-all-start.3 = ((f32[16,8,256]{2,1,0:T(8,128)}), f32[16,8,256]{2,1,0:T(8,128)}, u32[]{:S(2)}, u32[]{:S(2)}) async-start(f32[16,8,256]{2,1,0:T(8,128)} %reshape.133), calls=%async_computation.3 | async-start | bytes 262144 | tf_op jit(solution)/shard_map/all_to_all | solution.py:22
  100.0 8.9 %all-to-all-done.3 = f32[16,8,256]{2,1,0:T(8,128)} async-done(((f32[16,8,256]{2,1,0:T(8,128)}), f32[16,8,256]{2,1,0:T(8,128)}, u32[]{:S(2)}, u32[]{:S(2)}) %all-to-all-start.3) | async-done | bytes 131104 | tf_op jit(solution)/shard_map/all_to_all | solution.py:22
  109.0 1.5 reduce_sum.92
  110.5 1.3 broadcast_in_dim.116
  111.8 6.8 %all-to-all-start.4 = ((f32[8,8,256]{2,1,0:T(8,128)}), f32[8,8,256]{2,1,0:T(8,128)}, u32[]{:S(2)}, u32[]{:S(2)}) async-start(f32[8,8,256]{2,1,0:T(8,128)} %broadcast_in_dim.116), calls=%async_computation.4 | async-start | bytes 131072 | tf_op jit(solution)/shard_map/all_to_all | solution.py:22
  118.6 0.9 fusion.50
  119.8 6.1 %all-to-all-done.4 = f32[8,8,256]{2,1,0:T(8,128)} async-done(((f32[8,8,256]{2,1,0:T(8,128)}), f32[8,8,256]{2,1,0:T(8,128)}, u32[]{:S(2)}, u32[]{:S(2)}) %all-to-all-start.4) | async-done | bytes 65568 | tf_op jit(solution)/shard_map/all_to_all | solution.py:22
  125.9 0.9 reduce_sum.93
  127.6 3.3 %all-to-all-start.5 = ((f32[8,4,256]{2,1,0:T(4,128)}), f32[8,4,256]{2,1,0:T(4,128)S(1)}, u32[]{:S(2)}, u32[]{:S(2)}) async-start(f32[8,4,256]{2,1,0:T(4,128)} %broadcast_in_dim.117), calls=%async_computation.5 | async-start | bytes 65536 | tf_op jit(solution)/shard_map/all_to_all | solution.py:22
  131.0 6.8 %all-to-all-done.5 = f32[8,4,256]{2,1,0:T(4,128)S(1)} async-done(((f32[8,4,256]{2,1,0:T(4,128)}), f32[8,4,256]{2,1,0:T(4,128)S(1)}, u32[]{:S(2)}, u32[]{:S(2)}) %all-to-all-start.5) | async-done | bytes 32800 | tf_op jit(solution)/shard_map/all_to_all | solution.py:22
  138.7 3.3 %all-to-all-start.6 = ((f32[8,4,256]{2,1,0:T(4,128)}), f32[8,4,256]{2,1,0:T(4,128)S(1)}, u32[]{:S(2)}, u32[]{:S(2)}) async-start(f32[8,4,256]{2,1,0:T(4,128)} %broadcast_in_dim.118), calls=%async_computation.6 | async-start | bytes 65536 | tf_op jit(solution)/shard_map/all_to_all | solution.py:22
  142.1 6.8 %all-to-all-done.6 = f32[8,4,256]{2,1,0:T(4,128)S(1)} async-done(((f32[8,4,256]{2,1,0:T(4,128)}), f32[8,4,256]{2,1,0:T(4,128)S(1)}, u32[]{:S(2)}, u32[]{:S(2)}) %all-to-all-start.6) | async-done | bytes 32800 | tf_op jit(solution)/shard_map/all_to_all | solution.py:22
  149.1 9.2 %all_to_all.70 = f32[8,4,256]{2,1,0:T(4,128)S(1)} all-to-all(f32[8,4,256]{2,1,0:T(4,128)S(1)} %broadcast_in_dim.119), channel_id=1, replica_groups=mesh['grp'=8,'z'=8,'x'=4,'core'=2] {'z'}, dimensions={0} | all-to-all | bytes 65536 | tf_op jit(solution)/shard_map/all_to_all | solution.py:22
  158.7 9.2 %all_to_all.71 = f32[8,4,256]{2,1,0:T(4,128)S(1)} all-to-all(f32[8,4,256]{2,1,0:T(4,128)S(1)} %broadcast_in_dim.120), channel_id=1, replica_groups=mesh['grp'=8,'z'=8,'x'=4,'core'=2] {'grp'}, dimensions={0} | all-to-all | bytes 65536 | tf_op jit(solution)/shard_map/all_to_all | solution.py:22
  168.2 9.2 %all_to_all.72 = f32[8,4,256]{2,1,0:T(4,128)S(1)} all-to-all(f32[8,4,256]{2,1,0:T(4,128)S(1)} %broadcast_in_dim.121), channel_id=1, replica_groups=mesh['grp'=8,'z'=8,'x'=4,'core'=2] {'z'}, dimensions={0} | all-to-all | bytes 65536 | tf_op jit(solution)/shard_map/all_to_all | solution.py:22
  177.8 9.2 %all_to_all.73 = f32[8,4,256]{2,1,0:T(4,128)S(1)} all-to-all(f32[8,4,256]{2,1,0:T(4,128)S(1)} %broadcast_in_dim.122), channel_id=1, replica_groups=mesh['grp'=8,'z'=8,'x'=4,'core'=2] {'grp'}, dimensions={0} | all-to-all | bytes 65536 | tf_op jit(solution)/shard_map/all_to_all | solution.py:22
  187.7 11.7 %all-to-all-start.11 = ((f32[16,8,256]{2,1,0:T(8,128)}), f32[16,8,256]{2,1,0:T(8,128)S(1)}, u32[]{:S(2)}, u32[]{:S(2)}) async-start(f32[16,8,256]{2,1,0:T(8,128)} %broadcast_in_dim.123), calls=%async_computation.11 | async-start | bytes 262144 | tf_op jit(solution)/shard_map/all_to_all | solution.py:22
  199.4 9.2 %all-to-all-done.11 = f32[16,8,256]{2,1,0:T(8,128)S(1)} async-done(((f32[16,8,256]{2,1,0:T(8,128)}), f32[16,8,256]{2,1,0:T(8,128)S(1)}, u32[]{:S(2)}, u32[]{:S(2)}) %all-to-all-start.11) | async-done | bytes 131104 | tf_op jit(solution)/shard_map/all_to_all | solution.py:22
  212.3 3.6 %all-to-all-start.12 = ((f32[16,8,128]{2,1,0:T(8,128)}), f32[16,8,128]{2,1,0:T(8,128)S(1)}, u32[]{:S(2)}, u32[]{:S(2)}) async-start(f32[16,8,128]{2,1,0:T(8,128)} %broadcast_in_dim.124), calls=%async_computation.12 | async-start | bytes 131072 | tf_op jit(solution)/shard_map/all_to_all | solution.py:22
  216.2 6.9 %all-to-all-done.12 = f32[16,8,128]{2,1,0:T(8,128)S(1)} async-done(((f32[16,8,128]{2,1,0:T(8,128)}), f32[16,8,128]{2,1,0:T(8,128)S(1)}, u32[]{:S(2)}, u32[]{:S(2)}) %all-to-all-start.12) | async-done | bytes 65568 | tf_op jit(solution)/shard_map/all_to_all | solution.py:22
  226.5 1.1 copy.82
  227.6 6.3 %all-to-all-start.13 = ((f32[64,8,256]{2,1,0:T(8,128)}), f32[64,8,256]{2,1,0:T(8,128)S(1)}, u32[]{:S(2)}, u32[]{:S(2)}) async-start(f32[64,8,256]{2,1,0:T(8,128)} %copy.82), calls=%async_computation.13 | async-start | bytes 1048576 | tf_op jit(solution)/shard_map/all_to_all | solution.py:22
  235.2 16.4 %all-to-all-done.13 = f32[64,8,256]{2,1,0:T(8,128)S(1)} async-done(((f32[64,8,256]{2,1,0:T(8,128)}), f32[64,8,256]{2,1,0:T(8,128)S(1)}, u32[]{:S(2)}, u32[]{:S(2)}) %all-to-all-start.13) | async-done | bytes 524320 | tf_op jit(solution)/shard_map/all_to_all | solution.py:22
  252.1 0.8 copy.83
  253.0 1.4 reshape.141
  (151 shorter events, 22.1 us)
Async XLA Ops:
  0.6 1.7 copy-start.22
  4.0 5.7 %copy-start.25 = (s32[2]{0:T(128)S(1)}, s32[2]{0:T(128)}, u32[]{:S(2)}) copy-start(s32[2]{0:T(128)} %param.17) | copy-start | bytes 28
  4.0 5.7 %copy-start.13 = (f32[2,128,128]{2,1,0:T(8,128)S(1)}, f32[2,128,128]{2,1,0:T(8,128)}, u32[]{:S(2)}) copy-start(f32[2,128,128]{2,1,0:T(8,128)} %param.14) | copy-start | bytes 393220
  4.0 5.7 %copy-start.23 = (f32[32,256]{1,0:T(8,128)S(1)}, f32[32,256]{1,0:T(8,128)}, u32[]{:S(2)}) copy-start(f32[32,256]{1,0:T(8,128)} %param.13) | copy-start | bytes 98308
  4.0 5.9 %copy-start.11 = (f32[2,128,128]{2,1,0:T(8,128)S(1)}, f32[2,128,128]{2,1,0:T(8,128)}, u32[]{:S(2)}) copy-start(f32[2,128,128]{2,1,0:T(8,128)} %param.16) | copy-start | bytes 393220
  4.0 11.6 %all-to-all-start = ((f32[4,112,256]{2,1,0:T(8,128)}), f32[4,112,256]{2,1,0:T(8,128)S(1)}, u32[]{:S(2)}, u32[]{:S(2)}) async-start(f32[4,112,256]{2,1,0:T(8,128)} %broadcast_in_dim.115), calls=%async_computation | async-start | bytes 917504 | tf_op jit(solution)/shard_map/all_to_all | solution.py:22
  8.9 1.1 copy-start.18
  10.4 0.6 copy-start.16
  10.4 0.7 copy-start.24
  25.3 9.7 %copy-start.3 = (f32[32,2048]{1,0:T(8,128)S(1)}, f32[32,2048]{1,0:T(8,128)}, u32[]{:S(2)}) copy-start(f32[32,2048]{1,0:T(8,128)} %param.21) | copy-start | bytes 786436
  26.5 18.6 %copy-start = (f32[32,4096]{1,0:T(8,128)S(1)}, f32[32,4096]{1,0:T(8,128)}, u32[]{:S(2)}) copy-start(f32[32,4096]{1,0:T(8,128)} %param.22) | copy-start | bytes 1572868
  26.5 21.6 %all-to-all-start.1 = ((f32[64,8,128]{2,1,0:T(8,128)}), f32[64,8,128]{2,1,0:T(8,128)S(1)}, u32[]{:S(2)}, u32[]{:S(2)}) async-start(f32[64,8,128]{2,1,0:T(8,128)} %reshape.127), calls=%async_computation.1 | async-start | bytes 524288 | tf_op jit(solution)/shard_map/all_to_all | solution.py:22
  35.1 13.5 %collective-permute-start.2 = (f32[32,2048]{1,0:T(8,128)S(1)}, f32[32,2048]{1,0:T(8,128)S(1)}, u32[]{:S(2)}, u32[]{:S(2)}) collective-permute-start(f32[32,2048]{1,0:T(8,128)S(1)} %copy-done.3), channel_id=1, source_target_pairs={{6,0},{0,2},{2,4},{4,6},{7,1},{1,3},{3,5},{5,7},{14,8},{8,10},{10,... | collective-permute-start | bytes 786440 | tf_op jit(solution)/shard_map/ppermute | solution.py:66
  38.3 10.5 %collective-permute-start = (f32[32,2048]{1,0:T(8,128)S(1)}, f32[32,2048]{1,0:T(8,128)S(1)}, u32[]{:S(2)}, u32[]{:S(2)}) collective-permute-start(f32[32,2048]{1,0:T(8,128)S(1)} %copy-done.3), channel_id=1, source_target_pairs={{2,0},{4,2},{6,4},{0,6},{3,1},{5,3},{7,5},{1,7},{10,8},{12,10},{14... | collective-permute-start | bytes 786440 | tf_op jit(solution)/shard_map/ppermute | solution.py:66
  41.6 13.0 %collective-permute-start.1 = (f32[32,2048]{1,0:T(8,128)S(1)}, f32[32,2048]{1,0:T(8,128)S(1)}, u32[]{:S(2)}, u32[]{:S(2)}) collective-permute-start(f32[32,2048]{1,0:T(8,128)S(1)} %copy-done.3), channel_id=1, source_target_pairs={{4,0},{6,2},{0,4},{2,6},{5,1},{7,3},{1,5},{3,7},{12,8},{14,10},{8,... | collective-permute-start | bytes 786440 | tf_op jit(solution)/shard_map/ppermute | solution.py:66
  45.1 27.1 %collective-permute-start.5 = (f32[32,4096]{1,0:T(8,128)S(1)}, f32[32,4096]{1,0:T(8,128)S(1)}, u32[]{:S(2)}, u32[]{:S(2)}) collective-permute-start(f32[32,4096]{1,0:T(8,128)S(1)} %copy-done), channel_id=1, source_target_pairs={{6,0},{0,2},{2,4},{4,6},{7,1},{1,3},{3,5},{5,7},{14,8},{8,10},{10,... | collective-permute-start | bytes 1572872 | tf_op jit(solution)/shard_map/ppermute | solution.py:66
  48.6 0.7 copy-start.5
  48.9 6.0 %copy-start.7 = (f32[32,2048]{1,0:T(8,128)}, f32[32,2048]{1,0:T(8,128)S(1)}, u32[]{:S(2)}) copy-start(f32[32,2048]{1,0:T(8,128)S(1)} %collective-permute-done) | copy-start | bytes 786436
  56.0 15.3 %all-to-all-start.2 = ((f32[16,8,128]{2,1,0:T(8,128)}), f32[16,8,128]{2,1,0:T(8,128)S(1)}, u32[]{:S(2)}, u32[]{:S(2)}) async-start(f32[16,8,128]{2,1,0:T(8,128)} %reshape.129), calls=%async_computation.2 | async-start | bytes 131072 | tf_op jit(solution)/shard_map/all_to_all | solution.py:22
  63.5 26.5 %collective-permute-start.3 = (f32[32,4096]{1,0:T(8,128)S(1)}, f32[32,4096]{1,0:T(8,128)S(1)}, u32[]{:S(2)}, u32[]{:S(2)}) collective-permute-start(f32[32,4096]{1,0:T(8,128)S(1)} %copy-done), channel_id=1, source_target_pairs={{2,0},{4,2},{6,4},{0,6},{3,1},{5,3},{7,5},{1,7},{10,8},{12,10},{14... | collective-permute-start | bytes 1572872 | tf_op jit(solution)/shard_map/ppermute | solution.py:66
  67.7 22.6 %collective-permute-start.4 = (f32[32,4096]{1,0:T(8,128)S(1)}, f32[32,4096]{1,0:T(8,128)S(1)}, u32[]{:S(2)}, u32[]{:S(2)}) collective-permute-start(f32[32,4096]{1,0:T(8,128)S(1)} %copy-done), channel_id=1, source_target_pairs={{4,0},{6,2},{0,4},{2,6},{5,1},{7,3},{1,5},{3,7},{12,8},{14,10},{8,... | collective-permute-start | bytes 1572872 | tf_op jit(solution)/shard_map/ppermute | solution.py:66
  71.3 0.6 copy-start.20
  90.4 0.8 copy-start.1
  92.0 17.0 %all-to-all-start.3 = ((f32[16,8,256]{2,1,0:T(8,128)}), f32[16,8,256]{2,1,0:T(8,128)}, u32[]{:S(2)}, u32[]{:S(2)}) async-start(f32[16,8,256]{2,1,0:T(8,128)} %reshape.133), calls=%async_computation.3 | async-start | bytes 262144 | tf_op jit(solution)/shard_map/all_to_all | solution.py:22
  111.8 14.1 %all-to-all-start.4 = ((f32[8,8,256]{2,1,0:T(8,128)}), f32[8,8,256]{2,1,0:T(8,128)}, u32[]{:S(2)}, u32[]{:S(2)}) async-start(f32[8,8,256]{2,1,0:T(8,128)} %broadcast_in_dim.116), calls=%async_computation.4 | async-start | bytes 131072 | tf_op jit(solution)/shard_map/all_to_all | solution.py:22
  119.7 11.3 %copy-start.10 = (f32[1,4,2,32,256]{4,3,0,1,2:T(8,128)S(1)}, f32[1,4,2,32,256]{4,3,0,1,2:T(8,128)}, u32[]{:S(2)}) copy-start(f32[1,4,2,32,256]{4,3,0,1,2:T(8,128)} %get-tuple-element.11) | copy-start | bytes 786436
  127.6 10.2 %all-to-all-start.5 = ((f32[8,4,256]{2,1,0:T(4,128)}), f32[8,4,256]{2,1,0:T(4,128)S(1)}, u32[]{:S(2)}, u32[]{:S(2)}) async-start(f32[8,4,256]{2,1,0:T(4,128)} %broadcast_in_dim.117), calls=%async_computation.5 | async-start | bytes 65536 | tf_op jit(solution)/shard_map/all_to_all | solution.py:22
  131.0 11.1 %copy-start.9 = (f32[1,4,2,32,256]{4,3,0,1,2:T(8,128)S(1)}, f32[1,4,2,32,256]{4,3,0,1,2:T(8,128)}, u32[]{:S(2)}) copy-start(f32[1,4,2,32,256]{4,3,0,1,2:T(8,128)} %get-tuple-element.12) | copy-start | bytes 786436
  138.7 10.1 %all-to-all-start.6 = ((f32[8,4,256]{2,1,0:T(4,128)}), f32[8,4,256]{2,1,0:T(4,128)S(1)}, u32[]{:S(2)}, u32[]{:S(2)}) async-start(f32[8,4,256]{2,1,0:T(4,128)} %broadcast_in_dim.118), calls=%async_computation.6 | async-start | bytes 65536 | tf_op jit(solution)/shard_map/all_to_all | solution.py:22
  187.7 20.8 %all-to-all-start.11 = ((f32[16,8,256]{2,1,0:T(8,128)}), f32[16,8,256]{2,1,0:T(8,128)S(1)}, u32[]{:S(2)}, u32[]{:S(2)}) async-start(f32[16,8,256]{2,1,0:T(8,128)} %broadcast_in_dim.123), calls=%async_computation.11 | async-start | bytes 262144 | tf_op jit(solution)/shard_map/all_to_all | solution.py:22
  208.8 1.0 copy-start.2
  210.9 0.7 copy-start.21
  212.3 10.8 %all-to-all-start.12 = ((f32[16,8,128]{2,1,0:T(8,128)}), f32[16,8,128]{2,1,0:T(8,128)S(1)}, u32[]{:S(2)}, u32[]{:S(2)}) async-start(f32[16,8,128]{2,1,0:T(8,128)} %broadcast_in_dim.124), calls=%async_computation.12 | async-start | bytes 131072 | tf_op jit(solution)/shard_map/all_to_all | solution.py:22
  223.5 1.0 copy-start.4
  223.5 1.2 copy-start.8
  224.7 1.0 copy-start.6
  227.6 24.0 %all-to-all-start.13 = ((f32[64,8,256]{2,1,0:T(8,128)}), f32[64,8,256]{2,1,0:T(8,128)S(1)}, u32[]{:S(2)}, u32[]{:S(2)}) async-start(f32[64,8,256]{2,1,0:T(8,128)} %copy.82), calls=%async_computation.13 | async-start | bytes 1048576 | tf_op jit(solution)/shard_map/all_to_all | solution.py:22
  252.9 1.4 copy-start.12
  252.9 1.4 copy-start.17
  252.9 1.6 copy-start.14
  254.3 1.6 copy-start.15
  254.6 0.9 copy-start.19

commit v7 on v5

--- a/solution.py
+++ b/solution.py
@@ -4,8 +4,10 @@
 from jax.sharding import Mesh
 from jax.sharding import PartitionSpec as P
 
+
 EXACT = lax.Precision.HIGHEST
 DEV = ("z", "x", "core")
+LINE = ("z", "core")
 
 
 def mm(left, right):
@@ -28,12 +30,6 @@
     return jnp.sum(spread(values, axes, count), 0)
 
 
-def fold(values, folds):
-    rows, width = values.shape
-    tall = rows // folds
-    return values.reshape(folds, tall, width).transpose(1, 0, 2).reshape(tall, folds * width)
-
-
 def unfold(values, folds):
     tall, width = values.shape
     thin = width // folds
@@ -42,8 +38,8 @@
 
 def make_body(sizes):
     n_grp, n_z = sizes["grp"], sizes["z"]
-    n_x = sizes["x"]
-    n_near = n_x * sizes["core"]
+    n_x, n_core = sizes["x"], sizes["core"]
+    n_near, n_line = n_x * n_core, n_z * n_core
     n_dev = n_z * n_near
 
     def body(
@@ -70,6 +66,23 @@
         few = rows // n_near
         live = live_blocks[0]
         my_dev = lax.axis_index(DEV)
+        my_z, my_x, my_core = (lax.axis_index(name) for name in DEV)
+        some = rows // n_x
+
+        def from_right(values, step):
+            pairs = [((i + step) % n_x, i) for i in range(n_x)]
+            return lax.ppermute(values, "x", pairs)
+
+        def turn(values, axis, steps):
+            size = values.shape[axis]
+            doubled = jnp.concatenate([values, values], axis)
+            return lax.dynamic_slice_in_dim(doubled, steps * (size // n_x), size, axis)
+
+        inverses = [front_inverse] + [from_right(front_inverse, i) for i in range(1, n_x)]
+        couples = [front_couple] + [from_right(front_couple, i) for i in range(1, n_x)]
+
+        def along(values, pieces):
+            return jnp.concatenate([mmt(values, piece) for piece in pieces], 1)
 
         chain = jnp.concatenate([root_inverse, root_couple], 0)
         chain = spread(chain, "x", n_x)
@@ -77,10 +90,6 @@
         def dev_sum(natural):
             chunks = natural.reshape(4, rows // 4, n_dev, share).transpose(2, 1, 0, 3)
             return unfold(jnp.sum(swap(chunks.reshape(n_dev, rows // 4, 4 * share), DEV), 0), 4)
-
-        def dev_columns(values):
-            chunks = spread(fold(values, 4), DEV, n_dev).reshape(n_dev, rows // 4, 4, share)
-            return chunks.transpose(2, 1, 0, 3).reshape(rows, n_dev * share)
 
         has_parent = parents[0] < live
         right0, right1 = leaf_right[:, :width], leaf_right[:, width:]
@@ -99,6 +108,12 @@
         w_low, w_high, link = chain[0], chain[1], chain[2]
         start = front_right - dev_sum(placed.reshape(rows, front_order))
         y_own = dev_sum(mm(start, front_inverse))
+        y_some = []
+        for step in range(n_x):
+            spot = (my_x + n_x - step) % n_x * some
+            piece = lax.dynamic_slice_in_dim(y_own, spot, some, 0)
+            y_some.append(from_right(piece, step) if step else piece)
+        y_some = jnp.concatenate(y_some, 1)
 
         spots = my_dev * share + jnp.arange(share, dtype=jnp.int32)
         spots = jnp.concatenate([spots, front_order + spots])[:, None]
@@ -118,11 +133,26 @@
         y_high = y_high - reduce_over(mm(x_low, link), "z", n_z)
         x_high = reduce_over(mmt(y_high, w_high), "grp", n_grp)
 
-        whole = spread(jnp.concatenate([x_low, x_high], 0), DEV, n_dev)
-        whole = whole.reshape(n_z, n_near, 2, few, part).transpose(1, 3, 2, 0, 4)
-        whole = whole.reshape(rows, 2 * front_order)
-        rest = dev_columns(y_own - mmt(whole, front_couple))
-        front_solution = dev_columns(mmt(rest, front_inverse))
+        whole = spread(jnp.concatenate([x_low, x_high], 0), LINE, n_line)
+        whole = whole.reshape(n_z, n_core, 2, few, part).transpose(1, 3, 2, 0, 4)
+        whole = whole.reshape(some, 2 * front_order)
+        rest = turn(y_some - along(whole, couples), 1, (n_x - my_x) % n_x)
+        rest = spread(rest, LINE, n_line)
+        rest = rest.reshape(n_z, n_core, some, n_x, share).transpose(2, 0, 3, 1, 4)
+        found = along(rest.reshape(some, front_order), inverses)
+        found = turn(found, 1, (n_x - my_x) % n_x)
+        found = spread(found, DEV, n_dev).reshape(n_z, n_x, n_core, some, n_x, share)
+        front_solution = found.transpose(1, 3, 0, 4, 2, 5).reshape(rows, front_order)
+        root = []
+        for step in range(n_x):
+            spot = my_z * part + (my_x + n_x - step) % n_x * (n_core * share) + my_core * share
+            pieces = [
+                lax.dynamic_slice_in_dim(whole, spot + level * front_order, share, 1)
+                for level in range(2)
+            ]
+            piece = jnp.concatenate(pieces, 1)
+            root.append(from_right(piece, step) if step else piece)
+        root = turn(jnp.concatenate(root, 0), 0, (n_x - my_x) % n_x).reshape(rows, 2, share)
 
         def back(solved, block):
             picked = lax.dynamic_slice(front_solution, (0, front_rows[block] * width), (rows, width))
@@ -133,8 +163,6 @@
         carried = jnp.where(has_parent, mmt(leaf1, leaf_link[0]), 0.0)
         leaf0 = jnp.where(live > 0, mmt(base0 - carried, leaf_inverse[0]), 0.0)
         leaf_solution = jnp.concatenate([leaf0, leaf1], 1)
-        root = whole.reshape(rows, 2, front_order)
-        root = lax.dynamic_slice(root, (0, 0, my_dev * share), (rows, 2, share))
         return leaf_solution, front_solution, root
 
     return body
@@ -160,5 +188,6 @@
         P(None, DEV, "grp"),
     )
     out_specs = (P(None, every), P(None, "grp"), P(None, None, DEV))
-    body = make_body(dict(fine.shape))
-    return jax.shard_map(body, mesh=fine, in_specs=in_specs, out_specs=out_specs, check_vma=False)
+    inner = make_body(dict(fine.shape))
+
+    return jax.shard_map(inner, mesh=fine, in_specs=in_specs, out_specs=out_specs, check_vma=False)

time: 235 us -> 270 us (1.15)
  starting transfers between devices: 22.6 us -> 82.5 us
  blocking collectives: 150 us -> 101 us
  waiting for transfers between devices: 39 us -> 56.7 us
  matrix products: 5.27 us -> 8.62 us
    all_to_all x10 -> x8, blocking collectives: 141 us -> 92.6 us  [swap(): return lax.all_to_all(chunks, axes, 0, 0, tiled=True)]
    ppermute x0 -> x12, starting transfers between devices: none -> 33.6 us  [from_right(): return lax.ppermute(values, 'x', pairs)]
    all_to_all x4 -> x6, starting transfers between devices: 22.6 us -> 48.9 us  [swap(): return lax.all_to_all(chunks, axes, 0, 0, tiled=True)]
    ppermute x0 -> x12, waiting for transfers between devices: none -> 14.5 us  [from_right(): return lax.ppermute(values, 'x', pairs)]
    dot_general x10 -> x16, matrix products: 2.68 us -> 6.03 us  [mmt(): return jnp.einsum('rn,mn->rm', left, right, precision=EXACT)]
    all_to_all x4 -> x6, waiting for transfers between devices: 39 us -> 42.2 us  [swap(): return lax.all_to_all(chunks, axes, 0, 0, tiled=True)]
  transfers between devices with their start and end apart: 4 -> 18, of which waited for: 4 -> 8; matrix products, arithmetic and copies ran while one was open for 2% -> 4% of each run, Pallas kernels for 0% -> 0%
where the time goes in v7:
time: 270 us; the launch traced here: 269 us
  blocking collectives  101 us (37%)
  starting transfers between devices  82.5 us (31%)
  waiting for transfers between devices  56.7 us (21%)
  local copies, waits for them, and re-layouts  12.4 us (5%)
  matrix products  8.62 us (3%)
  other arithmetic  4.12 us (2%)
  between operations  3.36 us (1%)
    all_to_all x8, blocking collectives, swap(): return lax.all_to_all(chunks, axes, 0, 0, tiled=True)  92.6 us
    all_to_all x6, starting transfers between devices, swap(): return lax.all_to_all(chunks, axes, 0, 0, tiled=True)  48.9 us
    all_to_all x6, waiting for transfers between devices, swap(): return lax.all_to_all(chunks, axes, 0, 0, tiled=True)  42.2 us
    ppermute x12, starting transfers between devices, from_right(): return lax.ppermute(values, 'x', pairs)  33.6 us
    ppermute x12, waiting for transfers between devices, from_right(): return lax.ppermute(values, 'x', pairs)  14.5 us
    all_gather x1, blocking collectives, body(): chain = lax.all_gather(chain, 'core', axis=0).transpose(2, 1, 0, 3, 4)  8.57 us
    dot_general x16, matrix products, mmt(): return jnp.einsum('rn,mn->rm', left, right, precision=EXACT)  6.03 us
  transfers between devices with their start and end apart: 18, of which 8 were waited for; matrix products, arithmetic and copies ran while one was open for 4% of the time, Pallas kernels for 0%

profile of v7, /device:TPU:1, one launch (start us, length us, event | category | flops | bytes accessed | tf_op | source)
XLA Modules:
  0.0 268.8 jit_solution(8926666443462977101)
XLA Ops:
  0.7 0.9 pad_maximum_fusion
  1.6 0.8 broadcast_in_dim.125
  2.4 4.8 %all-to-all-start = ((f32[4,3,32,256]{3,2,1,0:T(8,128)}), f32[4,3,32,256]{3,2,1,0:T(8,128)S(1)}, u32[]{:S(2)}, u32[]{:S(2)}) async-start(f32[4,3,32,256]{3,2,1,0:T(8,128)} %broadcast_in_dim.125), calls=%async_computation | async-start | bytes 786432 | tf_op jit(solution)/shard_map/all_to_all | solution.py:22
  9.4 1.2 iota_compare_fusion.1
  10.8 2.7 %all-to-all-done = f32[4,3,32,256]{3,2,1,0:T(8,128)S(1)} async-done(((f32[4,3,32,256]{3,2,1,0:T(8,128)}), f32[4,3,32,256]{3,2,1,0:T(8,128)S(1)}, u32[]{:S(2)}, u32[]{:S(2)}) %all-to-all-start) | async-done | bytes 393248 | tf_op jit(solution)/shard_map/all_to_all | solution.py:22
  13.5 8.6 %all-gather = f32[8,3,32,256]{3,2,1,0:T(8,128)S(1)} all-gather(f32[4,3,32,256]{3,2,1,0:T(8,128)S(1)} %all-to-all-done), channel_id=2, replica_groups=mesh['grp'=8,'z'=8,'x'=4,'core'=2] {'core'}, dimensions={0}, use_global_device_ids=true | all-gather | bytes 1179648 | tf_op jit(solution)/shard_map/all_gather | solution.py:105
  22.7 0.9 copy.65
  23.6 8.1 %all-to-all-start.1 = ((f32[64,8,128]{2,1,0:T(8,128)}), f32[64,8,128]{2,1,0:T(8,128)S(1)}, u32[]{:S(2)}, u32[]{:S(2)}) async-start(f32[64,8,128]{2,1,0:T(8,128)} %copy.65), calls=%async_computation.1 | async-start | bytes 524288 | tf_op jit(solution)/shard_map/all_to_all | solution.py:22
  31.8 13.0 %all-to-all-done.1 = f32[64,8,128]{2,1,0:T(8,128)S(1)} async-done(((f32[64,8,128]{2,1,0:T(8,128)}), f32[64,8,128]{2,1,0:T(8,128)S(1)}, u32[]{:S(2)}, u32[]{:S(2)}) %all-to-all-start.1) | async-done | bytes 262176 | tf_op jit(solution)/shard_map/all_to_all | solution.py:22
  45.9 0.9 copy.68
  46.8 4.9 %all-to-all-start.2 = ((f32[64,8,128]{2,1,0:T(8,128)}), f32[64,8,128]{2,1,0:T(8,128)S(1)}, u32[]{:S(2)}, u32[]{:S(2)}) async-start(f32[64,8,128]{2,1,0:T(8,128)} %copy.68), calls=%async_computation.2 | async-start | bytes 524288 | tf_op jit(solution)/shard_map/all_to_all | solution.py:22
  52.0 12.8 %all-to-all-done.2 = f32[64,8,128]{2,1,0:T(8,128)S(1)} async-done(((f32[64,8,128]{2,1,0:T(8,128)}), f32[64,8,128]{2,1,0:T(8,128)S(1)}, u32[]{:S(2)}, u32[]{:S(2)}) %all-to-all-start.2) | async-done | bytes 262176 | tf_op jit(solution)/shard_map/all_to_all | solution.py:22
  65.0 0.9 fusion
  66.7 22.3 %all_to_all.70 = f32[64,8,256]{2,1,0:T(8,128)S(1)} all-to-all(f32[64,8,256]{2,1,0:T(8,128)S(1)} %copy.73), channel_id=1, replica_groups=mesh['grp'=8,'z'=8,'x'=4,'core'=2] {'z','x','core'}, dimensions={0} | all-to-all | bytes 1048576 | tf_op jit(solution)/shard_map/all_to_all | solution.py:22
  89.0 13.8 %all_to_all.71 = f32[8,8,256]{2,1,0:T(8,128)S(1)} all-to-all(f32[8,8,256]{2,1,0:T(8,128)S(1)} %broadcast_in_dim.128), channel_id=1, replica_groups=mesh['grp'=8,'z'=8,'x'=4,'core'=2] {'grp'}, dimensions={0} | all-to-all | bytes 131072 | tf_op jit(solution)/shard_map/all_to_all | solution.py:22
  103.1 10.2 %all_to_all.72 = f32[8,4,256]{2,1,0:T(4,128)S(1)} all-to-all(f32[8,4,256]{2,1,0:T(4,128)S(1)} %broadcast_in_dim.129), channel_id=1, replica_groups=mesh['grp'=8,'z'=8,'x'=4,'core'=2] {'z'}, dimensions={0} | all-to-all | bytes 65536 | tf_op jit(solution)/shard_map/all_to_all | solution.py:22
  113.7 9.2 %all_to_all.73 = f32[8,4,256]{2,1,0:T(4,128)S(1)} all-to-all(f32[8,4,256]{2,1,0:T(4,128)S(1)} %broadcast_in_dim.130), channel_id=1, replica_groups=mesh['grp'=8,'z'=8,'x'=4,'core'=2] {'grp'}, dimensions={0} | all-to-all | bytes 65536 | tf_op jit(solution)/shard_map/all_to_all | solution.py:22
  123.2 9.2 %all_to_all.74 = f32[8,4,256]{2,1,0:T(4,128)S(1)} all-to-all(f32[8,4,256]{2,1,0:T(4,128)S(1)} %broadcast_in_dim.131), channel_id=1, replica_groups=mesh['grp'=8,'z'=8,'x'=4,'core'=2] {'z'}, dimensions={0} | all-to-all | bytes 65536 | tf_op jit(solution)/shard_map/all_to_all | solution.py:22
  132.8 9.2 %all_to_all.75 = f32[8,4,256]{2,1,0:T(4,128)S(1)} all-to-all(f32[8,4,256]{2,1,0:T(4,128)S(1)} %broadcast_in_dim.132), channel_id=1, replica_groups=mesh['grp'=8,'z'=8,'x'=4,'core'=2] {'grp'}, dimensions={0} | all-to-all | bytes 65536 | tf_op jit(solution)/shard_map/all_to_all | solution.py:22
  142.3 9.2 %all_to_all.76 = f32[8,4,256]{2,1,0:T(4,128)S(1)} all-to-all(f32[8,4,256]{2,1,0:T(4,128)S(1)} %broadcast_in_dim.133), channel_id=1, replica_groups=mesh['grp'=8,'z'=8,'x'=4,'core'=2] {'z'}, dimensions={0} | all-to-all | bytes 65536 | tf_op jit(solution)/shard_map/all_to_all | solution.py:22
  151.9 9.2 %all_to_all.77 = f32[8,4,256]{2,1,0:T(4,128)S(1)} all-to-all(f32[8,4,256]{2,1,0:T(4,128)S(1)} %broadcast_in_dim.134), channel_id=1, replica_groups=mesh['grp'=8,'z'=8,'x'=4,'core'=2] {'grp'}, dimensions={0} | all-to-all | bytes 65536 | tf_op jit(solution)/shard_map/all_to_all | solution.py:22
  161.2 0.7 broadcast_in_dim.135
  161.8 12.6 %all-to-all-start.11 = ((f32[16,8,256]{2,1,0:T(8,128)}), f32[16,8,256]{2,1,0:T(8,128)S(1)}, u32[]{:S(2)}, u32[]{:S(2)}) async-start(f32[16,8,256]{2,1,0:T(8,128)} %broadcast_in_dim.135), calls=%async_computation.11 | async-start | bytes 262144 | tf_op jit(solution)/shard_map/all_to_all | solution.py:22
  174.5 2.8 %collective-permute-start.3 = (f32[32,4096]{1,0:T(8,128)S(1)}, f32[32,4096]{1,0:T(8,128)S(1)}, u32[]{:S(2)}, u32[]{:S(2)}) collective-permute-start(f32[32,4096]{1,0:T(8,128)S(1)} %copy-done), channel_id=1, source_target_pairs={{2,0},{4,2},{6,4},{0,6},{3,1},{5,3},{7,5},{1,7},{10,8},{12,10},{14... | collective-permute-start | bytes 1572872 | tf_op jit(solution)/shard_map/ppermute | solution.py:74
  177.2 3.1 %collective-permute-start.4 = (f32[32,4096]{1,0:T(8,128)S(1)}, f32[32,4096]{1,0:T(8,128)S(1)}, u32[]{:S(2)}, u32[]{:S(2)}) collective-permute-start(f32[32,4096]{1,0:T(8,128)S(1)} %copy-done), channel_id=1, source_target_pairs={{4,0},{6,2},{0,4},{2,6},{5,1},{7,3},{1,5},{3,7},{12,8},{14,10},{8,... | collective-permute-start | bytes 1572872 | tf_op jit(solution)/shard_map/ppermute | solution.py:74
  180.4 1.9 collective-permute-start.5
  182.3 4.6 %collective-permute-start.6 = (f32[32,2048]{1,0:T(8,128)S(1)}, f32[32,2048]{1,0:T(8,128)}, u32[]{:S(2)}, u32[]{:S(2)}) collective-permute-start(f32[32,2048]{1,0:T(8,128)S(1)} %copy-done.1), channel_id=1, source_target_pairs={{2,0},{4,2},{6,4},{0,6},{3,1},{5,3},{7,5},{1,7},{10,8},{12,10},{14... | collective-permute-start | bytes 786440 | tf_op jit(solution)/shard_map/ppermute | solution.py:74
  186.9 2.5 collective-permute-start.7
  191.6 2.5 collective-permute-start
  194.7 3.9 %collective-permute-start.1 = (f32[8,32]{1,0:T(8,128)S(1)}, f32[8,32]{1,0:T(8,128)S(1)}, u32[]{:S(2)}, u32[]{:S(2)}) collective-permute-start(f32[8,32]{1,0:T(8,128)S(1)} %get-tuple-element.23), channel_id=1, source_target_pairs={{4,0},{6,2},{0,4},{2,6},{5,1},{7,3},{1,5},{3,7},{12,8},{14,10},{8,... | collective-permute-start | bytes 3080 | tf_op jit(solution)/shard_map/ppermute | solution.py:74
  199.1 7.5 %collective-permute-done.5 = f32[32,4096]{1,0:T(8,128)S(1)} collective-permute-done((f32[32,4096]{1,0:T(8,128)S(1)}, f32[32,4096]{1,0:T(8,128)S(1)}, u32[]{:S(2)}, u32[]{:S(2)}) %collective-permute-start.5) | collective-permute-done | bytes 524320 | tf_op jit(solution)/shard_map/ppermute | solution.py:74
  206.6 1.9 collective-permute-start.2
  209.1 2.8 %collective-permute-done = f32[8,32]{1,0:T(8,128)S(1)} collective-permute-done((f32[8,32]{1,0:T(8,128)S(1)}, f32[8,32]{1,0:T(8,128)S(1)}, u32[]{:S(2)}, u32[]{:S(2)}) %collective-permute-start) | collective-permute-done | bytes 1056 | tf_op jit(solution)/shard_map/ppermute | solution.py:74
  211.9 1.9 collective-permute-start.8
  213.8 3.0 %collective-permute-start.11 = (f32[8,64]{1,0:T(8,128)S(1)}, f32[8,64]{1,0:T(8,128)S(1)}, u32[]{:S(2)}, u32[]{:S(2)}) collective-permute-start(f32[8,64]{1,0:T(8,128)S(1)} %pad_maximum_fusion.5), channel_id=1, source_target_pairs={{6,0},{0,2},{2,4},{4,6},{7,1},{1,3},{3,5},{5,7},{14,8},{8,10},{10,... | collective-permute-start | bytes 6152 | tf_op jit(solution)/shard_map/ppermute | solution.py:74
  216.8 3.5 %collective-permute-start.9 = (f32[8,64]{1,0:T(8,128)S(1)}, f32[8,64]{1,0:T(8,128)S(1)}, u32[]{:S(2)}, u32[]{:S(2)}) collective-permute-start(f32[8,64]{1,0:T(8,128)S(1)} %pad_maximum_fusion.3), channel_id=1, source_target_pairs={{2,0},{4,2},{6,4},{0,6},{3,1},{5,3},{7,5},{1,7},{10,8},{12,10},{14... | collective-permute-start | bytes 6152 | tf_op jit(solution)/shard_map/ppermute | solution.py:74
  221.2 11.4 %all-to-all-start.12 = ((f32[16,8,128]{2,1,0:T(8,128)}), f32[16,8,128]{2,1,0:T(8,128)S(1)}, u32[]{:S(2)}, u32[]{:S(2)}) async-start(f32[16,8,128]{2,1,0:T(8,128)} %broadcast_in_dim.136), calls=%async_computation.12 | async-start | bytes 131072 | tf_op jit(solution)/shard_map/all_to_all | solution.py:22
  232.7 2.0 collective-permute-start.10
  234.7 4.1 %collective-permute-done.10 = f32[8,64]{1,0:T(8,128)S(1)} collective-permute-done((f32[8,64]{1,0:T(8,128)S(1)}, f32[8,64]{1,0:T(8,128)S(1)}, u32[]{:S(2)}, u32[]{:S(2)}) %collective-permute-start.10) | collective-permute-done | bytes 2080 | tf_op jit(solution)/shard_map/ppermute | solution.py:74
  238.8 1.5 all-to-all-done.12
  241.3 1.3 fusion.72
  243.4 0.7 broadcast_in_dim.137
  244.1 7.2 %all-to-all-start.13 = ((f32[64,8,128]{2,1,0:T(8,128)}), f32[64,8,128]{2,1,0:T(8,128)S(1)}, u32[]{:S(2)}, u32[]{:S(2)}) async-start(f32[64,8,128]{2,1,0:T(8,128)} %broadcast_in_dim.137), calls=%async_computation.13 | async-start | bytes 524288 | tf_op jit(solution)/shard_map/all_to_all | solution.py:22
  251.4 0.7 reshape.102
  252.1 12.3 %all-to-all-done.13 = f32[64,8,128]{2,1,0:T(8,128)S(1)} async-done(((f32[64,8,128]{2,1,0:T(8,128)}), f32[64,8,128]{2,1,0:T(8,128)S(1)}, u32[]{:S(2)}, u32[]{:S(2)}) %all-to-all-start.13) | async-done | bytes 262176 | tf_op jit(solution)/shard_map/all_to_all | solution.py:22
  264.8 0.8 copy.82
  265.6 1.4 reshape.101
  268.1 0.6 pad_maximum_fusion.1
  (120 shorter events, 13.4 us)
Async XLA Ops:
  0.6 7.3 %copy-start.11 = (s32[2]{0:T(128)S(1)}, s32[2]{0:T(128)}, u32[]{:S(2)}) copy-start(s32[2]{0:T(128)} %param.17) | copy-start | bytes 28
  0.6 7.3 %copy-start.7 = (f32[32,256]{1,0:T(8,128)S(1)}, f32[32,256]{1,0:T(8,128)}, u32[]{:S(2)}) copy-start(f32[32,256]{1,0:T(8,128)} %param.13) | copy-start | bytes 98308
  0.7 7.3 %copy-start.3 = (f32[2,128,128]{2,1,0:T(8,128)S(1)}, f32[2,128,128]{2,1,0:T(8,128)}, u32[]{:S(2)}) copy-start(f32[2,128,128]{2,1,0:T(8,128)} %param.14) | copy-start | bytes 393220
  0.7 7.5 %copy-start.2 = (f32[2,128,128]{2,1,0:T(8,128)S(1)}, f32[2,128,128]{2,1,0:T(8,128)}, u32[]{:S(2)}) copy-start(f32[2,128,128]{2,1,0:T(8,128)} %param.16) | copy-start | bytes 393220
  0.7 7.6 %copy-start.5 = (f32[2,128,128]{2,1,0:T(8,128)S(1)}, f32[2,128,128]{2,1,0:T(8,128)}, u32[]{:S(2)}) copy-start(f32[2,128,128]{2,1,0:T(8,128)} %param.15) | copy-start | bytes 393220
  0.7 8.2 %copy-start.10 = (s32[2]{0:T(128)S(1)}, s32[2]{0:T(128)}, u32[]{:S(2)}) copy-start(s32[2]{0:T(128)} %param.18) | copy-start | bytes 28
  2.4 11.1 %all-to-all-start = ((f32[4,3,32,256]{3,2,1,0:T(8,128)}), f32[4,3,32,256]{3,2,1,0:T(8,128)S(1)}, u32[]{:S(2)}, u32[]{:S(2)}) async-start(f32[4,3,32,256]{3,2,1,0:T(8,128)} %broadcast_in_dim.125), calls=%async_computation | async-start | bytes 786432 | tf_op jit(solution)/shard_map/all_to_all | solution.py:22
  22.7 22.2 %copy-start.1 = (f32[32,2048]{1,0:T(8,128)S(1)}, f32[32,2048]{1,0:T(8,128)}, u32[]{:S(2)}) copy-start(f32[32,2048]{1,0:T(8,128)} %param.21) | copy-start | bytes 786436
  22.7 22.2 %copy-start.9 = (f32[32,32]{1,0:T(8,128)S(1)}, f32[32,32]{1,0:T(8,128)}, u32[]{:S(2)}) copy-start(f32[32,32]{1,0:T(8,128)} %param.20) | copy-start | bytes 12292
  23.6 21.1 %all-to-all-start.1 = ((f32[64,8,128]{2,1,0:T(8,128)}), f32[64,8,128]{2,1,0:T(8,128)S(1)}, u32[]{:S(2)}, u32[]{:S(2)}) async-start(f32[64,8,128]{2,1,0:T(8,128)} %copy.65), calls=%async_computation.1 | async-start | bytes 524288 | tf_op jit(solution)/shard_map/all_to_all | solution.py:22
  45.9 6.1 %copy-start.8 = (f32[32,2,32]{2,1,0:T(2,128)S(1)}, f32[32,2,32]{2,1,0:T(2,128)}, u32[]{:S(2)}) copy-start(f32[32,2,32]{2,1,0:T(2,128)} %param.23) | copy-start | bytes 24580
  46.8 18.1 %copy-start = (f32[32,4096]{1,0:T(8,128)S(1)}, f32[32,4096]{1,0:T(8,128)}, u32[]{:S(2)}) copy-start(f32[32,4096]{1,0:T(8,128)} %param.22) | copy-start | bytes 1572868
  46.8 18.0 %all-to-all-start.2 = ((f32[64,8,128]{2,1,0:T(8,128)}), f32[64,8,128]{2,1,0:T(8,128)S(1)}, u32[]{:S(2)}, u32[]{:S(2)}) async-start(f32[64,8,128]{2,1,0:T(8,128)} %copy.68), calls=%async_computation.2 | async-start | bytes 524288 | tf_op jit(solution)/shard_map/all_to_all | solution.py:22
  161.8 28.9 %all-to-all-start.11 = ((f32[16,8,256]{2,1,0:T(8,128)}), f32[16,8,256]{2,1,0:T(8,128)S(1)}, u32[]{:S(2)}, u32[]{:S(2)}) async-start(f32[16,8,256]{2,1,0:T(8,128)} %broadcast_in_dim.135), calls=%async_computation.11 | async-start | bytes 262144 | tf_op jit(solution)/shard_map/all_to_all | solution.py:22
  174.5 17.1 %collective-permute-start.3 = (f32[32,4096]{1,0:T(8,128)S(1)}, f32[32,4096]{1,0:T(8,128)S(1)}, u32[]{:S(2)}, u32[]{:S(2)}) collective-permute-start(f32[32,4096]{1,0:T(8,128)S(1)} %copy-done), channel_id=1, source_target_pairs={{2,0},{4,2},{6,4},{0,6},{3,1},{5,3},{7,5},{1,7},{10,8},{12,10},{14... | collective-permute-start | bytes 1572872 | tf_op jit(solution)/shard_map/ppermute | solution.py:74
  177.2 17.4 %collective-permute-start.4 = (f32[32,4096]{1,0:T(8,128)S(1)}, f32[32,4096]{1,0:T(8,128)S(1)}, u32[]{:S(2)}, u32[]{:S(2)}) collective-permute-start(f32[32,4096]{1,0:T(8,128)S(1)} %copy-done), channel_id=1, source_target_pairs={{4,0},{6,2},{0,4},{2,6},{5,1},{7,3},{1,5},{3,7},{12,8},{14,10},{8,... | collective-permute-start | bytes 1572872 | tf_op jit(solution)/shard_map/ppermute | solution.py:74
  180.4 26.2 %collective-permute-start.5 = (f32[32,4096]{1,0:T(8,128)S(1)}, f32[32,4096]{1,0:T(8,128)S(1)}, u32[]{:S(2)}, u32[]{:S(2)}) collective-permute-start(f32[32,4096]{1,0:T(8,128)S(1)} %copy-done), channel_id=1, source_target_pairs={{6,0},{0,2},{2,4},{4,6},{7,1},{1,3},{3,5},{5,7},{14,8},{8,10},{10,... | collective-permute-start | bytes 1572872 | tf_op jit(solution)/shard_map/ppermute | solution.py:74
  182.3 59.0 %collective-permute-start.6 = (f32[32,2048]{1,0:T(8,128)S(1)}, f32[32,2048]{1,0:T(8,128)}, u32[]{:S(2)}, u32[]{:S(2)}) collective-permute-start(f32[32,2048]{1,0:T(8,128)S(1)} %copy-done.1), channel_id=1, source_target_pairs={{2,0},{4,2},{6,4},{0,6},{3,1},{5,3},{7,5},{1,7},{10,8},{12,10},{14... | collective-permute-start | bytes 786440 | tf_op jit(solution)/shard_map/ppermute | solution.py:74
  186.9 55.7 %collective-permute-start.7 = (f32[32,2048]{1,0:T(8,128)S(1)}, f32[32,2048]{1,0:T(8,128)S(1)}, u32[]{:S(2)}, u32[]{:S(2)}) collective-permute-start(f32[32,2048]{1,0:T(8,128)S(1)} %copy-done.1), channel_id=1, source_target_pairs={{4,0},{6,2},{0,4},{2,6},{5,1},{7,3},{1,5},{3,7},{12,8},{14,10},{8,... | collective-permute-start | bytes 786440 | tf_op jit(solution)/shard_map/ppermute | solution.py:74
  191.6 20.3 %collective-permute-start = (f32[8,32]{1,0:T(8,128)S(1)}, f32[8,32]{1,0:T(8,128)S(1)}, u32[]{:S(2)}, u32[]{:S(2)}) collective-permute-start(f32[8,32]{1,0:T(8,128)S(1)} %get-tuple-element.24), channel_id=1, source_target_pairs={{2,0},{4,2},{6,4},{0,6},{3,1},{5,3},{7,5},{1,7},{10,8},{12,10},{14... | collective-permute-start | bytes 3080 | tf_op jit(solution)/shard_map/ppermute | solution.py:74
  194.7 19.1 %collective-permute-start.1 = (f32[8,32]{1,0:T(8,128)S(1)}, f32[8,32]{1,0:T(8,128)S(1)}, u32[]{:S(2)}, u32[]{:S(2)}) collective-permute-start(f32[8,32]{1,0:T(8,128)S(1)} %get-tuple-element.23), channel_id=1, source_target_pairs={{4,0},{6,2},{0,4},{2,6},{5,1},{7,3},{1,5},{3,7},{12,8},{14,10},{8,... | collective-permute-start | bytes 3080 | tf_op jit(solution)/shard_map/ppermute | solution.py:74
  206.6 10.3 %collective-permute-start.2 = (f32[8,32]{1,0:T(8,128)S(1)}, f32[8,32]{1,0:T(8,128)S(1)}, u32[]{:S(2)}, u32[]{:S(2)}) collective-permute-start(f32[8,32]{1,0:T(8,128)S(1)} %get-tuple-element.22), channel_id=1, source_target_pairs={{6,0},{0,2},{2,4},{4,6},{7,1},{1,3},{3,5},{5,7},{14,8},{8,10},{10,... | collective-permute-start | bytes 3080 | tf_op jit(solution)/shard_map/ppermute | solution.py:74
  211.9 31.0 %collective-permute-start.8 = (f32[32,2048]{1,0:T(8,128)S(1)}, f32[32,2048]{1,0:T(8,128)S(1)}, u32[]{:S(2)}, u32[]{:S(2)}) collective-permute-start(f32[32,2048]{1,0:T(8,128)S(1)} %copy-done.1), channel_id=1, source_target_pairs={{6,0},{0,2},{2,4},{4,6},{7,1},{1,3},{3,5},{5,7},{14,8},{8,10},{10,... | collective-permute-start | bytes 786440 | tf_op jit(solution)/shard_map/ppermute | solution.py:74
  213.8 25.0 %collective-permute-start.11 = (f32[8,64]{1,0:T(8,128)S(1)}, f32[8,64]{1,0:T(8,128)S(1)}, u32[]{:S(2)}, u32[]{:S(2)}) collective-permute-start(f32[8,64]{1,0:T(8,128)S(1)} %pad_maximum_fusion.5), channel_id=1, source_target_pairs={{6,0},{0,2},{2,4},{4,6},{7,1},{1,3},{3,5},{5,7},{14,8},{8,10},{10,... | collective-permute-start | bytes 6152 | tf_op jit(solution)/shard_map/ppermute | solution.py:74
  216.8 15.8 %collective-permute-start.9 = (f32[8,64]{1,0:T(8,128)S(1)}, f32[8,64]{1,0:T(8,128)S(1)}, u32[]{:S(2)}, u32[]{:S(2)}) collective-permute-start(f32[8,64]{1,0:T(8,128)S(1)} %pad_maximum_fusion.3), channel_id=1, source_target_pairs={{2,0},{4,2},{6,4},{0,6},{3,1},{5,3},{7,5},{1,7},{10,8},{12,10},{14... | collective-permute-start | bytes 6152 | tf_op jit(solution)/shard_map/ppermute | solution.py:74
  221.2 19.1 %all-to-all-start.12 = ((f32[16,8,128]{2,1,0:T(8,128)}), f32[16,8,128]{2,1,0:T(8,128)S(1)}, u32[]{:S(2)}, u32[]{:S(2)}) async-start(f32[16,8,128]{2,1,0:T(8,128)} %broadcast_in_dim.136), calls=%async_computation.12 | async-start | bytes 131072 | tf_op jit(solution)/shard_map/all_to_all | solution.py:22
  232.7 6.1 %collective-permute-start.10 = (f32[8,64]{1,0:T(8,128)S(1)}, f32[8,64]{1,0:T(8,128)S(1)}, u32[]{:S(2)}, u32[]{:S(2)}) collective-permute-start(f32[8,64]{1,0:T(8,128)S(1)} %pad_maximum_fusion.4), channel_id=1, source_target_pairs={{4,0},{6,2},{0,4},{2,6},{5,1},{7,3},{1,5},{3,7},{12,8},{14,10},{8,... | collective-permute-start | bytes 6152 | tf_op jit(solution)/shard_map/ppermute | solution.py:74
  244.1 20.2 %all-to-all-start.13 = ((f32[64,8,128]{2,1,0:T(8,128)}), f32[64,8,128]{2,1,0:T(8,128)S(1)}, u32[]{:S(2)}, u32[]{:S(2)}) async-start(f32[64,8,128]{2,1,0:T(8,128)} %broadcast_in_dim.137), calls=%async_computation.13 | async-start | bytes 524288 | tf_op jit(solution)/shard_map/all_to_all | solution.py:22
  265.6 2.0 copy-start.6
  267.0 1.8 copy-start.4

commit v8 on v7

--- a/solution.py
+++ b/solution.py
@@ -78,14 +78,14 @@
             doubled = jnp.concatenate([values, values], axis)
             return lax.dynamic_slice_in_dim(doubled, steps * (size // n_x), size, axis)
 
-        inverses = [front_inverse] + [from_right(front_inverse, i) for i in range(1, n_x)]
-        couples = [front_couple] + [from_right(front_couple, i) for i in range(1, n_x)]
+        def from_all(values):
+            return [values] + [from_right(values, step) for step in range(1, n_x)]
 
-        def along(values, pieces):
-            return jnp.concatenate([mmt(values, piece) for piece in pieces], 1)
-
-        chain = jnp.concatenate([root_inverse, root_couple], 0)
-        chain = spread(chain, "x", n_x)
+        chain = from_all(jnp.concatenate([root_inverse, root_couple], 0))
+        chain = lax.all_gather(jnp.stack(chain, 0), "core", axis=0)
+        chain = chain.transpose(2, 1, 0, 3, 4).reshape(3, n_near * share, part)
+        w_low, w_high, link = chain[0], chain[1], chain[2]
+        inverses = from_all(front_inverse)
 
         def dev_sum(natural):
             chunks = natural.reshape(4, rows // 4, n_dev, share).transpose(2, 1, 0, 3)
@@ -101,19 +101,10 @@
         placed = jnp.where(slots == front_rows[0], given0[:, None, :], 0.0) + jnp.where(
             slots == front_rows[1], given1[:, None, :], 0.0
         )
-        placed, chain = lax.optimization_barrier((placed, chain))
-        chain = lax.all_gather(chain, "core", axis=0).transpose(2, 1, 0, 3, 4)
-        chain = chain.reshape(3, n_near * share, part)
-        placed, chain = lax.optimization_barrier((placed, chain))
-        w_low, w_high, link = chain[0], chain[1], chain[2]
         start = front_right - dev_sum(placed.reshape(rows, front_order))
         y_own = dev_sum(mm(start, front_inverse))
-        y_some = []
-        for step in range(n_x):
-            spot = (my_x + n_x - step) % n_x * some
-            piece = lax.dynamic_slice_in_dim(y_own, spot, some, 0)
-            y_some.append(from_right(piece, step) if step else piece)
-        y_some = jnp.concatenate(y_some, 1)
+        side = jnp.pad(y_own, ((0, 0), (0, width - share)))
+        couples = from_all(jnp.concatenate([front_couple, side], 1))
 
         spots = my_dev * share + jnp.arange(share, dtype=jnp.int32)
         spots = jnp.concatenate([spots, front_order + spots])[:, None]
@@ -125,22 +116,32 @@
         given = jnp.sum(swap(chunks.reshape(n_dev, 2 * few, part), DEV), 0)
         given = reduce_over(given, "grp", n_grp)
 
+        given = turn(given, 1, my_x)
         low, high = given[:few], given[few:]
         y_high = reduce_over(mm(high, w_high), "z", n_z)
         low = low - reduce_over(mmt(y_high, link), "grp", n_grp)
         y_low = reduce_over(mm(low, w_low), "z", n_z)
         x_low = reduce_over(mmt(y_low, w_low), "grp", n_grp)
+        joined = jnp.concatenate([piece[:, : 2 * front_order] for piece in couples], 0)
+        inverse = jnp.concatenate(inverses, 0)
+        y_some = [
+            lax.dynamic_slice_in_dim(piece[:, 2 * front_order :], my_x * some, some, 0)[:, :share]
+            for piece in couples
+        ]
+        y_some = jnp.concatenate(y_some, 1)
+        x_low, joined, inverse, y_some = lax.optimization_barrier((x_low, joined, inverse, y_some))
         y_high = y_high - reduce_over(mm(x_low, link), "z", n_z)
         x_high = reduce_over(mmt(y_high, w_high), "grp", n_grp)
 
-        whole = spread(jnp.concatenate([x_low, x_high], 0), LINE, n_line)
+        back_turn = (n_x - my_x) % n_x
+        both = turn(jnp.concatenate([x_low, x_high], 0), 1, back_turn)
+        whole = spread(both, LINE, n_line)
         whole = whole.reshape(n_z, n_core, 2, few, part).transpose(1, 3, 2, 0, 4)
         whole = whole.reshape(some, 2 * front_order)
-        rest = turn(y_some - along(whole, couples), 1, (n_x - my_x) % n_x)
+        rest = turn(y_some - mmt(whole, joined), 1, back_turn)
         rest = spread(rest, LINE, n_line)
         rest = rest.reshape(n_z, n_core, some, n_x, share).transpose(2, 0, 3, 1, 4)
-        found = along(rest.reshape(some, front_order), inverses)
-        found = turn(found, 1, (n_x - my_x) % n_x)
+        found = turn(mmt(rest.reshape(some, front_order), inverse), 1, back_turn)
         found = spread(found, DEV, n_dev).reshape(n_z, n_x, n_core, some, n_x, share)
         front_solution = found.transpose(1, 3, 0, 4, 2, 5).reshape(rows, front_order)
         root = []
@@ -152,7 +153,7 @@
             ]
             piece = jnp.concatenate(pieces, 1)
             root.append(from_right(piece, step) if step else piece)
-        root = turn(jnp.concatenate(root, 0), 0, (n_x - my_x) % n_x).reshape(rows, 2, share)
+        root = turn(jnp.concatenate(root, 0), 0, back_turn).reshape(rows, 2, share)
 
         def back(solved, block):
             picked = lax.dynamic_slice(front_solution, (0, front_rows[block] * width), (rows, width))

time: 270 us -> 280 us (1.037)
  blocking collectives: 101 us -> 11.9 us
  waiting for transfers between devices: 56.7 us -> 106 us
  starting transfers between devices: 82.5 us -> 112 us
  local copies, waits for them, and re-layouts: 12.4 us -> 23.4 us
  other arithmetic: 4.12 us -> 8.56 us
  matrix products: 8.62 us -> 12.2 us
    all_to_all x8 -> x1, blocking collectives: 92.6 us -> 9.25 us  [swap(): return lax.all_to_all(chunks, axes, 0, 0, tiled=True)]
    all_to_all x6 -> x12, waiting for transfers between devices: 42.2 us -> 85.4 us  [swap(): return lax.all_to_all(chunks, axes, 0, 0, tiled=True)]
    all_to_all x6 -> x12, starting transfers between devices: 48.9 us -> 70.6 us  [swap(): return lax.all_to_all(chunks, axes, 0, 0, tiled=True)]
    ppermute x12, starting transfers between devices: 33.6 us -> 41.7 us  [from_right(): return lax.ppermute(values, 'x', pairs)]
    all_gather x1, blocking collectives: 8.57 us -> 2.67 us  [body(): chain = lax.all_gather(jnp.stack(chain, 0), 'core', axis=0)]
    ppermute x12, waiting for transfers between devices: 14.5 us -> 20.2 us  [from_right(): return lax.ppermute(values, 'x', pairs)]
    dot_general x10, matrix products: 2.59 us -> 7.78 us  [mm(): return jnp.dot(left, right, precision=EXACT)]
    broadcast_in_dim x11 -> x10, local copies, waits for them, and re-layouts: 3.14 us -> 6.11 us  [spread(): return swap(jnp.broadcast_to(values[None], (count,) + values.shape), axes)]
  transfers between devices with their start and end apart: 18 -> 24, of which waited for: 8 -> 12; matrix products, arithmetic and copies ran while one was open for 4% -> 10% of each run, Pallas kernels for 0% -> 0%
where the time goes in v8:
time: 280 us; the launch traced here: 278 us
  starting transfers between devices  112 us (40%)
  waiting for transfers between devices  106 us (38%)
  local copies, waits for them, and re-layouts  23.4 us (8%)
  matrix products  12.2 us (4%)
  blocking collectives  11.9 us (4%)
  other arithmetic  8.56 us (3%)
  between operations  4.09 us (1%)
    all_to_all x12, waiting for transfers between devices, swap(): return lax.all_to_all(chunks, axes, 0, 0, tiled=True)  85.4 us
    all_to_all x12, starting transfers between devices, swap(): return lax.all_to_all(chunks, axes, 0, 0, tiled=True)  70.6 us
    ppermute x12, starting transfers between devices, from_right(): return lax.ppermute(values, 'x', pairs)  41.7 us
    ppermute x12, waiting for transfers between devices, from_right(): return lax.ppermute(values, 'x', pairs)  20.2 us
    all_to_all x1, blocking collectives, swap(): return lax.all_to_all(chunks, axes, 0, 0, tiled=True)  9.25 us
    dot_general x10, matrix products, mm(): return jnp.dot(left, right, precision=EXACT)  7.78 us
    broadcast_in_dim x10, local copies, waits for them, and re-layouts, spread(): return swap(jnp.broadcast_to(values[None], (count,) + values.shape), axes)  6.11 us
  transfers between devices with their start and end apart: 24, of which 12 were waited for; matrix products, arithmetic and copies ran while one was open for 10% of the time, Pallas kernels for 0%

profile of v8, /device:TPU:1, one launch (start us, length us, event | category | flops | bytes accessed | tf_op | source)
XLA Modules:
  0.0 278.1 jit_solution(2215467111872048072)
XLA Ops:
  2.3 5.2 %collective-permute-start = (f32[3,32,256]{2,1,0:T(8,128)S(1)}, f32[3,32,256]{2,1,0:T(8,128)}, u32[]{:S(2)}, u32[]{:S(2)}) collective-permute-start(f32[3,32,256]{2,1,0:T(8,128)S(1)} %constant_dynamic-update-slice_fusion), channel_id=1, source_target_pairs={{2,0},{4,2},{6,4},{0,6},{3,1},{5,3},{7,5},{1,7},{10,8},{12,10},{14... | collective-permute-start | bytes 294920 | tf_op jit(solution)/shard_map/ppermute | solution.py:74
  7.5 2.4 collective-permute-start.1
  9.9 2.5 collective-permute-start.2
  12.4 4.0 %collective-permute-start.6 = (f32[32,2048]{1,0:T(8,128)}, f32[32,2048]{1,0:T(8,128)S(1)}, u32[]{:S(2)}, u32[]{:S(2)}) collective-permute-start(f32[32,2048]{1,0:T(8,128)} %param.21), channel_id=1, source_target_pairs={{2,0},{4,2},{6,4},{0,6},{3,1},{5,3},{7,5},{1,7},{10,8},{12,10},{14... | collective-permute-start | bytes 786440 | tf_op jit(solution)/shard_map/ppermute | solution.py:74
  16.4 3.2 %collective-permute-start.7 = (f32[32,2048]{1,0:T(8,128)}, f32[32,2048]{1,0:T(8,128)}, u32[]{:S(2)}, u32[]{:S(2)}) collective-permute-start(f32[32,2048]{1,0:T(8,128)} %param.21), channel_id=1, source_target_pairs={{4,0},{6,2},{0,4},{2,6},{5,1},{7,3},{1,5},{3,7},{12,8},{14,10},{8,... | collective-permute-start | bytes 786440 | tf_op jit(solution)/shard_map/ppermute | solution.py:74
  20.9 1.0 convolution_select_fusion.5
  22.9 1.0 fusion.5
  23.9 1.0 convolution_select_fusion.3
  30.4 14.4 %all-to-all-start = ((f32[64,8,128]{2,1,0:T(8,128)}), f32[64,8,128]{2,1,0:T(8,128)S(1)}, u32[]{:S(2)}, u32[]{:S(2)}) async-start(f32[64,8,128]{2,1,0:T(8,128)} %copy.70), calls=%async_computation | async-start | bytes 524288 | tf_op jit(solution)/shard_map/all_to_all | solution.py:22
  45.2 12.7 %all-to-all-done = f32[64,8,128]{2,1,0:T(8,128)S(1)} async-done(((f32[64,8,128]{2,1,0:T(8,128)}), f32[64,8,128]{2,1,0:T(8,128)S(1)}, u32[]{:S(2)}, u32[]{:S(2)}) %all-to-all-start) | async-done | bytes 262176 | tf_op jit(solution)/shard_map/all_to_all | solution.py:22
  58.1 1.3 fusion.35
  60.9 4.8 %all-to-all-start.1 = ((f32[64,8,128]{2,1,0:T(8,128)}), f32[64,8,128]{2,1,0:T(8,128)S(1)}, u32[]{:S(2)}, u32[]{:S(2)}) async-start(f32[64,8,128]{2,1,0:T(8,128)} %copy.73), calls=%async_computation.1 | async-start | bytes 524288 | tf_op jit(solution)/shard_map/all_to_all | solution.py:22
  66.6 3.3 %collective-permute-start.8 = (f32[32,2048]{1,0:T(8,128)}, f32[32,2048]{1,0:T(8,128)}, u32[]{:S(2)}, u32[]{:S(2)}) collective-permute-start(f32[32,2048]{1,0:T(8,128)} %param.21), channel_id=1, source_target_pairs={{6,0},{0,2},{2,4},{4,6},{7,1},{1,3},{3,5},{5,7},{14,8},{8,10},{10,... | collective-permute-start | bytes 786440 | tf_op jit(solution)/shard_map/ppermute | solution.py:74
  69.9 1.0 pad_maximum_fusion.3
  70.9 2.7 all-gather
  73.6 5.2 %all-to-all-done.1 = f32[64,8,128]{2,1,0:T(8,128)S(1)} async-done(((f32[64,8,128]{2,1,0:T(8,128)}), f32[64,8,128]{2,1,0:T(8,128)S(1)}, u32[]{:S(2)}, u32[]{:S(2)}) %all-to-all-start.1) | async-done | bytes 262176 | tf_op jit(solution)/shard_map/all_to_all | solution.py:22
  80.4 1.1 copy.78
  81.4 4.8 %all-to-all-start.2 = ((f32[64,8,256]{2,1,0:T(8,128)}), f32[64,8,256]{2,1,0:T(8,128)S(1)}, u32[]{:S(2)}, u32[]{:S(2)}) async-start(f32[64,8,256]{2,1,0:T(8,128)} %copy.78), calls=%async_computation.2 | async-start | bytes 1048576 | tf_op jit(solution)/shard_map/all_to_all | solution.py:22
  86.3 3.3 %collective-permute-start.5 = (f32[32,4224]{1,0:T(8,128)S(1)}, f32[32,4224]{1,0:T(8,128)S(1)}, u32[]{:S(2)}, u32[]{:S(2)}) collective-permute-start(f32[32,4224]{1,0:T(8,128)S(1)} %pad_maximum_fusion.2), channel_id=1, source_target_pairs={{6,0},{0,2},{2,4},{4,6},{7,1},{1,3},{3,5},{5,7},{14,8},{8,10},{10,... | collective-permute-start | bytes 1622024 | tf_op jit(solution)/shard_map/ppermute | solution.py:74
  89.5 4.3 %collective-permute-start.4 = (f32[32,4224]{1,0:T(8,128)S(1)}, f32[32,4224]{1,0:T(8,128)S(1)}, u32[]{:S(2)}, u32[]{:S(2)}) collective-permute-start(f32[32,4224]{1,0:T(8,128)S(1)} %pad_maximum_fusion.2), channel_id=1, source_target_pairs={{4,0},{6,2},{0,4},{2,6},{5,1},{7,3},{1,5},{3,7},{12,8},{14,10},{8,... | collective-permute-start | bytes 1622024 | tf_op jit(solution)/shard_map/ppermute | solution.py:74
  93.9 3.1 %collective-permute-start.3 = (f32[32,4224]{1,0:T(8,128)S(1)}, f32[32,4224]{1,0:T(8,128)S(1)}, u32[]{:S(2)}, u32[]{:S(2)}) collective-permute-start(f32[32,4224]{1,0:T(8,128)S(1)} %pad_maximum_fusion.2), channel_id=1, source_target_pairs={{2,0},{4,2},{6,4},{0,6},{3,1},{5,3},{7,5},{1,7},{10,8},{12,10},{14... | collective-permute-start | bytes 1622024 | tf_op jit(solution)/shard_map/ppermute | solution.py:74
  97.2 2.3 pad_maximum_fusion.1
  100.0 20.2 %collective-permute-done.3 = f32[32,4224]{1,0:T(8,128)S(1)} collective-permute-done((f32[32,4224]{1,0:T(8,128)S(1)}, f32[32,4224]{1,0:T(8,128)S(1)}, u32[]{:S(2)}, u32[]{:S(2)}) %collective-permute-start.3) | collective-permute-done | bytes 540704 | tf_op jit(solution)/shard_map/ppermute | solution.py:74
  124.5 6.8 %all-to-all-start.3 = ((f32[8,8,256]{2,1,0:T(8,128)}), f32[8,8,256]{2,1,0:T(8,128)S(1)}, u32[]{:S(2)}, u32[]{:S(2)}) async-start(f32[8,8,256]{2,1,0:T(8,128)} %broadcast_in_dim.139), calls=%async_computation.3 | async-start | bytes 131072 | tf_op jit(solution)/shard_map/all_to_all | solution.py:22
  131.3 1.5 pad_maximum_fusion
  132.9 5.7 %all-to-all-done.3 = f32[8,8,256]{2,1,0:T(8,128)S(1)} async-done(((f32[8,8,256]{2,1,0:T(8,128)}), f32[8,8,256]{2,1,0:T(8,128)S(1)}, u32[]{:S(2)}, u32[]{:S(2)}) %all-to-all-start.3) | async-done | bytes 65568 | tf_op jit(solution)/shard_map/all_to_all | solution.py:22
  139.5 5.4 %all-to-all-start.4 = ((f32[8,4,256]{2,1,0:T(4,128)}), f32[8,4,256]{2,1,0:T(4,128)S(1)}, u32[]{:S(2)}, u32[]{:S(2)}) async-start(f32[8,4,256]{2,1,0:T(4,128)} %broadcast_in_dim.140), calls=%async_computation.4 | async-start | bytes 65536 | tf_op jit(solution)/shard_map/all_to_all | solution.py:22
  144.9 6.9 %all-to-all-done.4 = f32[8,4,256]{2,1,0:T(4,128)S(1)} async-done(((f32[8,4,256]{2,1,0:T(4,128)}), f32[8,4,256]{2,1,0:T(4,128)S(1)}, u32[]{:S(2)}, u32[]{:S(2)}) %all-to-all-start.4) | async-done | bytes 32800 | tf_op jit(solution)/shard_map/all_to_all | solution.py:22
  152.7 3.3 %all-to-all-start.5 = ((f32[8,4,256]{2,1,0:T(4,128)}), f32[8,4,256]{2,1,0:T(4,128)S(1)}, u32[]{:S(2)}, u32[]{:S(2)}) async-start(f32[8,4,256]{2,1,0:T(4,128)} %broadcast_in_dim.141), calls=%async_computation.5 | async-start | bytes 65536 | tf_op jit(solution)/shard_map/all_to_all | solution.py:22
  156.1 6.8 %all-to-all-done.5 = f32[8,4,256]{2,1,0:T(4,128)S(1)} async-done(((f32[8,4,256]{2,1,0:T(4,128)}), f32[8,4,256]{2,1,0:T(4,128)S(1)}, u32[]{:S(2)}, u32[]{:S(2)}) %all-to-all-start.5) | async-done | bytes 32800 | tf_op jit(solution)/shard_map/all_to_all | solution.py:22
  163.7 3.3 %all-to-all-start.6 = ((f32[8,4,256]{2,1,0:T(4,128)}), f32[8,4,256]{2,1,0:T(4,128)S(1)}, u32[]{:S(2)}, u32[]{:S(2)}) async-start(f32[8,4,256]{2,1,0:T(4,128)} %broadcast_in_dim.142), calls=%async_computation.6 | async-start | bytes 65536 | tf_op jit(solution)/shard_map/all_to_all | solution.py:22
  167.1 6.8 %all-to-all-done.6 = f32[8,4,256]{2,1,0:T(4,128)S(1)} async-done(((f32[8,4,256]{2,1,0:T(4,128)}), f32[8,4,256]{2,1,0:T(4,128)S(1)}, u32[]{:S(2)}, u32[]{:S(2)}) %all-to-all-start.6) | async-done | bytes 32800 | tf_op jit(solution)/shard_map/all_to_all | solution.py:22
  174.9 3.3 %all-to-all-start.7 = ((f32[8,4,256]{2,1,0:T(4,128)}), f32[8,4,256]{2,1,0:T(4,128)S(1)}, u32[]{:S(2)}, u32[]{:S(2)}) async-start(f32[8,4,256]{2,1,0:T(4,128)} %broadcast_in_dim.143), calls=%async_computation.7 | async-start | bytes 65536 | tf_op jit(solution)/shard_map/all_to_all | solution.py:22
  178.3 6.7 %all-to-all-done.7 = f32[8,4,256]{2,1,0:T(4,128)S(1)} async-done(((f32[8,4,256]{2,1,0:T(4,128)}), f32[8,4,256]{2,1,0:T(4,128)S(1)}, u32[]{:S(2)}, u32[]{:S(2)}) %all-to-all-start.7) | async-done | bytes 32800 | tf_op jit(solution)/shard_map/all_to_all | solution.py:22
  185.3 9.2 %all_to_all.65 = f32[8,4,256]{2,1,0:T(4,128)S(1)} all-to-all(f32[8,4,256]{2,1,0:T(4,128)S(1)} %broadcast_in_dim.144), channel_id=1, replica_groups=mesh['grp'=8,'z'=8,'x'=4,'core'=2] {'z'}, dimensions={0} | all-to-all | bytes 65536 | tf_op jit(solution)/shard_map/all_to_all | solution.py:22
  195.5 3.3 %all-to-all-start.9 = ((f32[8,4,256]{2,1,0:T(4,128)}), f32[8,4,256]{2,1,0:T(4,128)S(1)}, u32[]{:S(2)}, u32[]{:S(2)}) async-start(f32[8,4,256]{2,1,0:T(4,128)} %broadcast_in_dim.145), calls=%async_computation.9 | async-start | bytes 65536 | tf_op jit(solution)/shard_map/all_to_all | solution.py:22
  198.8 6.8 %all-to-all-done.9 = f32[8,4,256]{2,1,0:T(4,128)S(1)} async-done(((f32[8,4,256]{2,1,0:T(4,128)}), f32[8,4,256]{2,1,0:T(4,128)S(1)}, u32[]{:S(2)}, u32[]{:S(2)}) %all-to-all-start.9) | async-done | bytes 32800 | tf_op jit(solution)/shard_map/all_to_all | solution.py:22
  206.4 13.1 %all-to-all-start.10 = ((f32[16,8,256]{2,1,0:T(8,128)}), f32[16,8,256]{2,1,0:T(8,128)S(1)}, u32[]{:S(2)}, u32[]{:S(2)}) async-start(f32[16,8,256]{2,1,0:T(8,128)} %broadcast_in_dim.146), calls=%async_computation.10 | async-start | bytes 262144 | tf_op jit(solution)/shard_map/all_to_all | solution.py:22
  220.8 7.9 %all-to-all-done.10 = f32[16,8,256]{2,1,0:T(8,128)S(1)} async-done(((f32[16,8,256]{2,1,0:T(8,128)}), f32[16,8,256]{2,1,0:T(8,128)S(1)}, u32[]{:S(2)}, u32[]{:S(2)}) %all-to-all-start.10) | async-done | bytes 131104 | tf_op jit(solution)/shard_map/all_to_all | solution.py:22
  229.0 3.9 %collective-permute-start.11 = (f32[8,64]{1,0:T(8,128)S(1)}, f32[8,64]{1,0:T(8,128)S(1)}, u32[]{:S(2)}, u32[]{:S(2)}) collective-permute-start(f32[8,64]{1,0:T(8,128)S(1)} %pad_maximum_fusion.8), channel_id=1, source_target_pairs={{6,0},{0,2},{2,4},{4,6},{7,1},{1,3},{3,5},{5,7},{14,8},{8,10},{10,... | collective-permute-start | bytes 6152 | tf_op jit(solution)/shard_map/ppermute | solution.py:74
  233.0 3.6 %collective-permute-start.10 = (f32[8,64]{1,0:T(8,128)S(1)}, f32[8,64]{1,0:T(8,128)S(1)}, u32[]{:S(2)}, u32[]{:S(2)}) collective-permute-start(f32[8,64]{1,0:T(8,128)S(1)} %pad_maximum_fusion.7), channel_id=1, source_target_pairs={{4,0},{6,2},{0,4},{2,6},{5,1},{7,3},{1,5},{3,7},{12,8},{14,10},{8,... | collective-permute-start | bytes 6152 | tf_op jit(solution)/shard_map/ppermute | solution.py:74
  236.7 3.0 %collective-permute-start.9 = (f32[8,64]{1,0:T(8,128)S(1)}, f32[8,64]{1,0:T(8,128)S(1)}, u32[]{:S(2)}, u32[]{:S(2)}) collective-permute-start(f32[8,64]{1,0:T(8,128)S(1)} %pad_maximum_fusion.6), channel_id=1, source_target_pairs={{2,0},{4,2},{6,4},{0,6},{3,1},{5,3},{7,5},{1,7},{10,8},{12,10},{14... | collective-permute-start | bytes 6152 | tf_op jit(solution)/shard_map/ppermute | solution.py:74
  239.7 1.7 fusion.61
  242.2 3.8 %all-to-all-start.11 = ((f32[16,8,128]{2,1,0:T(8,128)}), f32[16,8,128]{2,1,0:T(8,128)S(1)}, u32[]{:S(2)}, u32[]{:S(2)}) async-start(f32[16,8,128]{2,1,0:T(8,128)} %broadcast_in_dim.147), calls=%async_computation.11 | async-start | bytes 131072 | tf_op jit(solution)/shard_map/all_to_all | solution.py:22
  246.1 7.7 %all-to-all-done.11 = f32[16,8,128]{2,1,0:T(8,128)S(1)} async-done(((f32[16,8,128]{2,1,0:T(8,128)}), f32[16,8,128]{2,1,0:T(8,128)S(1)}, u32[]{:S(2)}, u32[]{:S(2)}) %all-to-all-start.11) | async-done | bytes 65568 | tf_op jit(solution)/shard_map/all_to_all | solution.py:22
  256.3 4.2 %all-to-all-start.12 = ((f32[64,8,128]{2,1,0:T(8,128)}), f32[64,8,128]{2,1,0:T(8,128)S(1)}, u32[]{:S(2)}, u32[]{:S(2)}) async-start(f32[64,8,128]{2,1,0:T(8,128)} %broadcast_in_dim.148), calls=%async_computation.12 | async-start | bytes 524288 | tf_op jit(solution)/shard_map/all_to_all | solution.py:22
  261.3 12.4 %all-to-all-done.12 = f32[64,8,128]{2,1,0:T(8,128)S(1)} async-done(((f32[64,8,128]{2,1,0:T(8,128)}), f32[64,8,128]{2,1,0:T(8,128)S(1)}, u32[]{:S(2)}, u32[]{:S(2)}) %all-to-all-start.12) | async-done | bytes 262176 | tf_op jit(solution)/shard_map/all_to_all | solution.py:22
  274.9 1.4 reshape.107
  (154 shorter events, 30.8 us)
Async XLA Ops:
  0.6 25.9 %copy-start.14 = (s32[2]{0:T(128)S(1)}, s32[2]{0:T(128)}, u32[]{:S(2)}) copy-start(s32[2]{0:T(128)} %param.18) | copy-start | bytes 28
  2.3 64.3 %collective-permute-start = (f32[3,32,256]{2,1,0:T(8,128)S(1)}, f32[3,32,256]{2,1,0:T(8,128)}, u32[]{:S(2)}, u32[]{:S(2)}) collective-permute-start(f32[3,32,256]{2,1,0:T(8,128)S(1)} %constant_dynamic-update-slice_fusion), channel_id=1, source_target_pairs={{2,0},{4,2},{6,4},{0,6},{3,1},{5,3},{7,5},{1,7},{10,8},{12,10},{14... | collective-permute-start | bytes 294920 | tf_op jit(solution)/shard_map/ppermute | solution.py:74
  7.5 62.4 %collective-permute-start.1 = (f32[3,32,256]{2,1,0:T(8,128)S(1)}, f32[3,32,256]{2,1,0:T(8,128)}, u32[]{:S(2)}, u32[]{:S(2)}) collective-permute-start(f32[3,32,256]{2,1,0:T(8,128)S(1)} %constant_dynamic-update-slice_fusion), channel_id=1, source_target_pairs={{4,0},{6,2},{0,4},{2,6},{5,1},{7,3},{1,5},{3,7},{12,8},{14,10},{8,... | collective-permute-start | bytes 294920 | tf_op jit(solution)/shard_map/ppermute | solution.py:74
  9.9 60.0 %collective-permute-start.2 = (f32[3,32,256]{2,1,0:T(8,128)S(1)}, f32[3,32,256]{2,1,0:T(8,128)}, u32[]{:S(2)}, u32[]{:S(2)}) collective-permute-start(f32[3,32,256]{2,1,0:T(8,128)S(1)} %constant_dynamic-update-slice_fusion), channel_id=1, source_target_pairs={{6,0},{0,2},{2,4},{4,6},{7,1},{1,3},{3,5},{5,7},{14,8},{8,10},{10,... | collective-permute-start | bytes 294920 | tf_op jit(solution)/shard_map/ppermute | solution.py:74
  12.4 81.4 %collective-permute-start.6 = (f32[32,2048]{1,0:T(8,128)}, f32[32,2048]{1,0:T(8,128)S(1)}, u32[]{:S(2)}, u32[]{:S(2)}) collective-permute-start(f32[32,2048]{1,0:T(8,128)} %param.21), channel_id=1, source_target_pairs={{2,0},{4,2},{6,4},{0,6},{3,1},{5,3},{7,5},{1,7},{10,8},{12,10},{14... | collective-permute-start | bytes 786440 | tf_op jit(solution)/shard_map/ppermute | solution.py:74
  16.4 80.7 %collective-permute-start.7 = (f32[32,2048]{1,0:T(8,128)}, f32[32,2048]{1,0:T(8,128)}, u32[]{:S(2)}, u32[]{:S(2)}) collective-permute-start(f32[32,2048]{1,0:T(8,128)} %param.21), channel_id=1, source_target_pairs={{4,0},{6,2},{0,4},{2,6},{5,1},{7,3},{1,5},{3,7},{12,8},{14,10},{8,... | collective-permute-start | bytes 786440 | tf_op jit(solution)/shard_map/ppermute | solution.py:74
  24.9 4.3 %copy-start.9 = (f32[32,128]{1,0:T(8,128)}, f32[32,128]{1,0:T(8,128)S(1)}, u32[]{:S(2)}) copy-start(f32[32,128]{1,0:T(8,128)S(1)} %convolution_select_fusion.3) | copy-start | bytes 49156
  29.2 28.9 %copy-start.12 = (f32[32,32]{1,0:T(8,128)S(1)}, f32[32,32]{1,0:T(8,128)}, u32[]{:S(2)}) copy-start(f32[32,32]{1,0:T(8,128)} %param.20) | copy-start | bytes 12292
  30.4 27.5 %all-to-all-start = ((f32[64,8,128]{2,1,0:T(8,128)}), f32[64,8,128]{2,1,0:T(8,128)S(1)}, u32[]{:S(2)}, u32[]{:S(2)}) async-start(f32[64,8,128]{2,1,0:T(8,128)} %copy.70), calls=%async_computation | async-start | bytes 524288 | tf_op jit(solution)/shard_map/all_to_all | solution.py:22
  60.0 18.9 %copy-start = (f32[32,4096]{1,0:T(8,128)S(1)}, f32[32,4096]{1,0:T(8,128)}, u32[]{:S(2)}) copy-start(f32[32,4096]{1,0:T(8,128)} %param.22) | copy-start | bytes 1572868
  60.9 17.9 %all-to-all-start.1 = ((f32[64,8,128]{2,1,0:T(8,128)}), f32[64,8,128]{2,1,0:T(8,128)S(1)}, u32[]{:S(2)}, u32[]{:S(2)}) async-start(f32[64,8,128]{2,1,0:T(8,128)} %copy.73), calls=%async_computation.1 | async-start | bytes 524288 | tf_op jit(solution)/shard_map/all_to_all | solution.py:22
  66.6 30.6 %collective-permute-start.8 = (f32[32,2048]{1,0:T(8,128)}, f32[32,2048]{1,0:T(8,128)}, u32[]{:S(2)}, u32[]{:S(2)}) collective-permute-start(f32[32,2048]{1,0:T(8,128)} %param.21), channel_id=1, source_target_pairs={{6,0},{0,2},{2,4},{4,6},{7,1},{1,3},{3,5},{5,7},{14,8},{8,10},{10,... | collective-permute-start | bytes 786440 | tf_op jit(solution)/shard_map/ppermute | solution.py:74
  81.4 42.3 %all-to-all-start.2 = ((f32[64,8,256]{2,1,0:T(8,128)}), f32[64,8,256]{2,1,0:T(8,128)S(1)}, u32[]{:S(2)}, u32[]{:S(2)}) async-start(f32[64,8,256]{2,1,0:T(8,128)} %copy.78), calls=%async_computation.2 | async-start | bytes 1048576 | tf_op jit(solution)/shard_map/all_to_all | solution.py:22
  86.3 35.7 %collective-permute-start.5 = (f32[32,4224]{1,0:T(8,128)S(1)}, f32[32,4224]{1,0:T(8,128)S(1)}, u32[]{:S(2)}, u32[]{:S(2)}) collective-permute-start(f32[32,4224]{1,0:T(8,128)S(1)} %pad_maximum_fusion.2), channel_id=1, source_target_pairs={{6,0},{0,2},{2,4},{4,6},{7,1},{1,3},{3,5},{5,7},{14,8},{8,10},{10,... | collective-permute-start | bytes 1622024 | tf_op jit(solution)/shard_map/ppermute | solution.py:74
  89.5 31.6 %collective-permute-start.4 = (f32[32,4224]{1,0:T(8,128)S(1)}, f32[32,4224]{1,0:T(8,128)S(1)}, u32[]{:S(2)}, u32[]{:S(2)}) collective-permute-start(f32[32,4224]{1,0:T(8,128)S(1)} %pad_maximum_fusion.2), channel_id=1, source_target_pairs={{4,0},{6,2},{0,4},{2,6},{5,1},{7,3},{1,5},{3,7},{12,8},{14,10},{8,... | collective-permute-start | bytes 1622024 | tf_op jit(solution)/shard_map/ppermute | solution.py:74
  93.9 3.2 %copy-start.8 = (f32[32,2048]{1,0:T(8,128)}, f32[32,2048]{1,0:T(8,128)S(1)}, u32[]{:S(2)}) copy-start(f32[32,2048]{1,0:T(8,128)S(1)} %collective-permute-done.6) | copy-start | bytes 786436
  93.9 26.3 %collective-permute-start.3 = (f32[32,4224]{1,0:T(8,128)S(1)}, f32[32,4224]{1,0:T(8,128)S(1)}, u32[]{:S(2)}, u32[]{:S(2)}) collective-permute-start(f32[32,4224]{1,0:T(8,128)S(1)} %pad_maximum_fusion.2), channel_id=1, source_target_pairs={{2,0},{4,2},{6,4},{0,6},{3,1},{5,3},{7,5},{1,7},{10,8},{12,10},{14... | collective-permute-start | bytes 1622024 | tf_op jit(solution)/shard_map/ppermute | solution.py:74
  120.2 1.8 copy-start.4
  121.1 1.0 copy-start.3
  122.1 0.8 copy-start.2
  124.5 14.1 %all-to-all-start.3 = ((f32[8,8,256]{2,1,0:T(8,128)}), f32[8,8,256]{2,1,0:T(8,128)S(1)}, u32[]{:S(2)}, u32[]{:S(2)}) async-start(f32[8,8,256]{2,1,0:T(8,128)} %broadcast_in_dim.139), calls=%async_computation.3 | async-start | bytes 131072 | tf_op jit(solution)/shard_map/all_to_all | solution.py:22
  131.3 13.6 %slice-start = ((f32[32,4224]{1,0:T(8,128)}), f32[32,128]{1,0:T(8,128)S(1)}, s32[]{:S(2)}) async-start(f32[32,4224]{1,0:T(8,128)} %copy-done.2), calls=%async_computation.13 | async-start | bytes 32768 | tf_op jit(solution)/shard_map/slice | solution.py:128
  131.3 24.8 %slice-start.1 = ((f32[32,4224]{1,0:T(8,128)}), f32[32,128]{1,0:T(8,128)S(1)}, s32[]{:S(2)}) async-start(f32[32,4224]{1,0:T(8,128)} %copy-done.3), calls=%async_computation.14 | async-start | bytes 32768 | tf_op jit(solution)/shard_map/slice | solution.py:128
  131.3 35.8 %slice-start.2 = ((f32[32,4224]{1,0:T(8,128)}), f32[32,128]{1,0:T(8,128)S(1)}, s32[]{:S(2)}) async-start(f32[32,4224]{1,0:T(8,128)} %copy-done.4), calls=%async_computation.15 | async-start | bytes 32768 | tf_op jit(solution)/shard_map/slice | solution.py:128
  131.3 46.9 %copy-start.13 = (f32[8,128]{1,0:T(8,128)S(1)}, f32[8,128]{1,0:T(8,128)}, u32[]{:S(2)}) copy-start(f32[8,128]{1,0:T(8,128)} %constant_dynamic-slice_fusion.12) | copy-start | bytes 12292
  139.5 12.3 %all-to-all-start.4 = ((f32[8,4,256]{2,1,0:T(4,128)}), f32[8,4,256]{2,1,0:T(4,128)S(1)}, u32[]{:S(2)}, u32[]{:S(2)}) async-start(f32[8,4,256]{2,1,0:T(4,128)} %broadcast_in_dim.140), calls=%async_computation.4 | async-start | bytes 65536 | tf_op jit(solution)/shard_map/all_to_all | solution.py:22
  152.7 10.1 %all-to-all-start.5 = ((f32[8,4,256]{2,1,0:T(4,128)}), f32[8,4,256]{2,1,0:T(4,128)S(1)}, u32[]{:S(2)}, u32[]{:S(2)}) async-start(f32[8,4,256]{2,1,0:T(4,128)} %broadcast_in_dim.141), calls=%async_computation.5 | async-start | bytes 65536 | tf_op jit(solution)/shard_map/all_to_all | solution.py:22
  163.7 10.1 %all-to-all-start.6 = ((f32[8,4,256]{2,1,0:T(4,128)}), f32[8,4,256]{2,1,0:T(4,128)S(1)}, u32[]{:S(2)}, u32[]{:S(2)}) async-start(f32[8,4,256]{2,1,0:T(4,128)} %broadcast_in_dim.142), calls=%async_computation.6 | async-start | bytes 65536 | tf_op jit(solution)/shard_map/all_to_all | solution.py:22
  174.9 10.1 %all-to-all-start.7 = ((f32[8,4,256]{2,1,0:T(4,128)}), f32[8,4,256]{2,1,0:T(4,128)S(1)}, u32[]{:S(2)}, u32[]{:S(2)}) async-start(f32[8,4,256]{2,1,0:T(4,128)} %broadcast_in_dim.143), calls=%async_computation.7 | async-start | bytes 65536 | tf_op jit(solution)/shard_map/all_to_all | solution.py:22
  195.5 10.1 %all-to-all-start.9 = ((f32[8,4,256]{2,1,0:T(4,128)}), f32[8,4,256]{2,1,0:T(4,128)S(1)}, u32[]{:S(2)}, u32[]{:S(2)}) async-start(f32[8,4,256]{2,1,0:T(4,128)} %broadcast_in_dim.145), calls=%async_computation.9 | async-start | bytes 65536 | tf_op jit(solution)/shard_map/all_to_all | solution.py:22
  206.4 22.3 %all-to-all-start.10 = ((f32[16,8,256]{2,1,0:T(8,128)}), f32[16,8,256]{2,1,0:T(8,128)S(1)}, u32[]{:S(2)}, u32[]{:S(2)}) async-start(f32[16,8,256]{2,1,0:T(8,128)} %broadcast_in_dim.146), calls=%async_computation.10 | async-start | bytes 262144 | tf_op jit(solution)/shard_map/all_to_all | solution.py:22
  228.7 25.8 %copy-start.1 = (f32[128,2048]{1,0:T(8,128)S(1)}, f32[128,2048]{1,0:T(8,128)}, u32[]{:S(2)}) copy-start(f32[128,2048]{1,0:T(8,128)} %pad_maximum_fusion.1) | copy-start | bytes 3145732
  229.0 17.1 %collective-permute-start.11 = (f32[8,64]{1,0:T(8,128)S(1)}, f32[8,64]{1,0:T(8,128)S(1)}, u32[]{:S(2)}, u32[]{:S(2)}) collective-permute-start(f32[8,64]{1,0:T(8,128)S(1)} %pad_maximum_fusion.8), channel_id=1, source_target_pairs={{6,0},{0,2},{2,4},{4,6},{7,1},{1,3},{3,5},{5,7},{14,8},{8,10},{10,... | collective-permute-start | bytes 6152 | tf_op jit(solution)/shard_map/ppermute | solution.py:74
  233.0 13.0 %collective-permute-start.10 = (f32[8,64]{1,0:T(8,128)S(1)}, f32[8,64]{1,0:T(8,128)S(1)}, u32[]{:S(2)}, u32[]{:S(2)}) collective-permute-start(f32[8,64]{1,0:T(8,128)S(1)} %pad_maximum_fusion.7), channel_id=1, source_target_pairs={{4,0},{6,2},{0,4},{2,6},{5,1},{7,3},{1,5},{3,7},{12,8},{14,10},{8,... | collective-permute-start | bytes 6152 | tf_op jit(solution)/shard_map/ppermute | solution.py:74
  236.7 9.4 %collective-permute-start.9 = (f32[8,64]{1,0:T(8,128)S(1)}, f32[8,64]{1,0:T(8,128)S(1)}, u32[]{:S(2)}, u32[]{:S(2)}) collective-permute-start(f32[8,64]{1,0:T(8,128)S(1)} %pad_maximum_fusion.6), channel_id=1, source_target_pairs={{2,0},{4,2},{6,4},{0,6},{3,1},{5,3},{7,5},{1,7},{10,8},{12,10},{14... | collective-permute-start | bytes 6152 | tf_op jit(solution)/shard_map/ppermute | solution.py:74
  242.2 11.6 %all-to-all-start.11 = ((f32[16,8,128]{2,1,0:T(8,128)}), f32[16,8,128]{2,1,0:T(8,128)S(1)}, u32[]{:S(2)}, u32[]{:S(2)}) async-start(f32[16,8,128]{2,1,0:T(8,128)} %broadcast_in_dim.147), calls=%async_computation.11 | async-start | bytes 131072 | tf_op jit(solution)/shard_map/all_to_all | solution.py:22
  256.3 17.4 %all-to-all-start.12 = ((f32[64,8,128]{2,1,0:T(8,128)}), f32[64,8,128]{2,1,0:T(8,128)S(1)}, u32[]{:S(2)}, u32[]{:S(2)}) async-start(f32[64,8,128]{2,1,0:T(8,128)} %broadcast_in_dim.148), calls=%async_computation.12 | async-start | bytes 524288 | tf_op jit(solution)/shard_map/all_to_all | solution.py:22
  261.3 15.0 %copy-start.5 = (f32[2,128,128]{2,1,0:T(8,128)S(1)}, f32[2,128,128]{2,1,0:T(8,128)}, u32[]{:S(2)}) copy-start(f32[2,128,128]{2,1,0:T(8,128)} %param.16) | copy-start | bytes 393220
  261.3 15.2 %copy-start.10 = (f32[32,128]{1,0:T(8,128)S(1)}, f32[32,128]{1,0:T(8,128)}, u32[]{:S(2)}) copy-start(f32[32,128]{1,0:T(8,128)} %copy-done.9) | copy-start | bytes 49156
  274.1 2.7 copy-start.6
  274.1 2.9 %copy-start.11 = (f32[2,128,128]{2,1,0:T(8,128)S(1)}, f32[2,128,128]{2,1,0:T(8,128)}, u32[]{:S(2)}) copy-start(f32[2,128,128]{2,1,0:T(8,128)} %param.15) | copy-start | bytes 393220
  276.3 1.8 copy-start.7

commit v9 on v8

--- a/solution.py
+++ b/solution.py
@@ -73,18 +73,20 @@
             pairs = [((i + step) % n_x, i) for i in range(n_x)]
             return lax.ppermute(values, "x", pairs)
 
-        def turn(values, axis, steps):
-            size = values.shape[axis]
+        def turn(values, axis, start):
             doubled = jnp.concatenate([values, values], axis)
-            return lax.dynamic_slice_in_dim(doubled, steps * (size // n_x), size, axis)
+            return lax.dynamic_slice_in_dim(doubled, start, values.shape[axis], axis)
 
         def from_all(values):
             return [values] + [from_right(values, step) for step in range(1, n_x)]
 
         chain = from_all(jnp.concatenate([root_inverse, root_couple], 0))
         chain = lax.all_gather(jnp.stack(chain, 0), "core", axis=0)
-        chain = chain.transpose(2, 1, 0, 3, 4).reshape(3, n_near * share, part)
-        w_low, w_high, link = chain[0], chain[1], chain[2]
+        chain = [
+            chain[:, :, item].transpose(1, 0, 2, 3).reshape(n_near * share, part)
+            for item in range(3)
+        ]
+        w_low, w_high, link = lax.optimization_barrier(tuple(chain))
         inverses = from_all(front_inverse)
 
         def dev_sum(natural):
@@ -101,14 +103,25 @@
         placed = jnp.where(slots == front_rows[0], given0[:, None, :], 0.0) + jnp.where(
             slots == front_rows[1], given1[:, None, :], 0.0
         )
+        behind = (n_x - my_x) % n_x
+        spots = [my_x * (n_core * share), my_x * some]
+        spots += [behind * size for size in (n_core * share, share, some)]
+        for step in range(n_x):
+            spot = my_z * part + (my_x + n_x - step) % n_x * (n_core * share) + my_core * share
+            spots += [spot, spot + front_order]
+        spots += [front_rows[block] * width for block in range(2)]
+        spots = tuple(spot.astype(jnp.uint32) for spot in spots)
+        placed, spots = lax.optimization_barrier((placed, spots))
+        ahead_part, rows_x, back_part, back_share, back_rows = spots[:5]
+        root_spots, leaf_spots = spots[5:-2], spots[-2:]
         start = front_right - dev_sum(placed.reshape(rows, front_order))
         y_own = dev_sum(mm(start, front_inverse))
         side = jnp.pad(y_own, ((0, 0), (0, width - share)))
         couples = from_all(jnp.concatenate([front_couple, side], 1))
 
-        spots = my_dev * share + jnp.arange(share, dtype=jnp.int32)
-        spots = jnp.concatenate([spots, front_order + spots])[:, None]
-        picks = spots == jnp.arange(2 * front_order, dtype=jnp.int32)[None, :]
+        picks = my_dev * share + jnp.arange(share, dtype=jnp.int32)
+        picks = jnp.concatenate([picks, front_order + picks])[:, None]
+        picks = picks == jnp.arange(2 * front_order, dtype=jnp.int32)[None, :]
         picks = jnp.where(picks & (lax.axis_index("grp") == 0), 1.0, 0.0).astype(jnp.float32)
         fed = jnp.concatenate([-y_own, root_right[:, 0], root_right[:, 1]], 1)
         given = mm(fed, jnp.concatenate([front_couple, picks], 0))
@@ -116,7 +129,7 @@
         given = jnp.sum(swap(chunks.reshape(n_dev, 2 * few, part), DEV), 0)
         given = reduce_over(given, "grp", n_grp)
 
-        given = turn(given, 1, my_x)
+        given = turn(given, 1, ahead_part)
         low, high = given[:few], given[few:]
         y_high = reduce_over(mm(high, w_high), "z", n_z)
         low = low - reduce_over(mmt(y_high, link), "grp", n_grp)
@@ -125,7 +138,7 @@
         joined = jnp.concatenate([piece[:, : 2 * front_order] for piece in couples], 0)
         inverse = jnp.concatenate(inverses, 0)
         y_some = [
-            lax.dynamic_slice_in_dim(piece[:, 2 * front_order :], my_x * some, some, 0)[:, :share]
+            lax.dynamic_slice_in_dim(piece[:, 2 * front_order :], rows_x, some, 0)[:, :share]
             for piece in couples
         ]
         y_some = jnp.concatenate(y_some, 1)
@@ -133,30 +146,31 @@
         y_high = y_high - reduce_over(mm(x_low, link), "z", n_z)
         x_high = reduce_over(mmt(y_high, w_high), "grp", n_grp)
 
-        back_turn = (n_x - my_x) % n_x
-        both = turn(jnp.concatenate([x_low, x_high], 0), 1, back_turn)
+        both = turn(jnp.concatenate([x_low, x_high], 0), 1, back_part)
         whole = spread(both, LINE, n_line)
         whole = whole.reshape(n_z, n_core, 2, few, part).transpose(1, 3, 2, 0, 4)
         whole = whole.reshape(some, 2 * front_order)
-        rest = turn(y_some - mmt(whole, joined), 1, back_turn)
+        rest = turn(y_some - mmt(whole, joined), 1, back_share)
         rest = spread(rest, LINE, n_line)
         rest = rest.reshape(n_z, n_core, some, n_x, share).transpose(2, 0, 3, 1, 4)
-        found = turn(mmt(rest.reshape(some, front_order), inverse), 1, back_turn)
+        found = turn(mmt(rest.reshape(some, front_order), inverse), 1, back_share)
         found = spread(found, DEV, n_dev).reshape(n_z, n_x, n_core, some, n_x, share)
         front_solution = found.transpose(1, 3, 0, 4, 2, 5).reshape(rows, front_order)
-        root = []
-        for step in range(n_x):
-            spot = my_z * part + (my_x + n_x - step) % n_x * (n_core * share) + my_core * share
-            pieces = [
-                lax.dynamic_slice_in_dim(whole, spot + level * front_order, share, 1)
-                for level in range(2)
-            ]
-            piece = jnp.concatenate(pieces, 1)
-            root.append(from_right(piece, step) if step else piece)
-        root = turn(jnp.concatenate(root, 0), 0, back_turn).reshape(rows, 2, share)
+        root = [
+            jnp.concatenate(
+                [
+                    lax.dynamic_slice_in_dim(whole, spot, share, 1)
+                    for spot in root_spots[2 * step : 2 * step + 2]
+                ],
+                1,
+            )
+            for step in range(n_x)
+        ]
+        root = [root[0]] + [from_right(root[step], step) for step in range(1, n_x)]
+        root = turn(jnp.concatenate(root, 0), 0, back_rows).reshape(rows, 2, share)
 
         def back(solved, block):
-            picked = lax.dynamic_slice(front_solution, (0, front_rows[block] * width), (rows, width))
+            picked = lax.dynamic_slice_in_dim(front_solution, leaf_spots[block], width, 1)
             return solved - mmt(picked, leaf_front[block])
 
         base0, base1 = back(solved0, 0), back(solved1, 1)

time: 280 us -> 278 us (level)
  blocking collectives: 11.9 us -> 42.5 us
  starting transfers between devices: 112 us -> 95.9 us
  waiting for transfers between devices: 106 us -> 90.9 us
    all_to_all x1 -> x3, blocking collectives: 9.25 us -> 39.9 us  [swap(): return lax.all_to_all(chunks, axes, 0, 0, tiled=True)]
    all_to_all x12 -> x10, starting transfers between devices: 70.6 us -> 54.2 us  [swap(): return lax.all_to_all(chunks, axes, 0, 0, tiled=True)]
    all_to_all x12 -> x10, waiting for transfers between devices: 85.4 us -> 70.8 us  [swap(): return lax.all_to_all(chunks, axes, 0, 0, tiled=True)]
  transfers between devices with their start and end apart: 24 -> 22, of which waited for: 12 -> 10; matrix products, arithmetic and copies ran while one was open for 10% -> 10% of each run, Pallas kernels for 0% -> 0%
where the time goes in v9:
time: 278 us; the launch traced here: 276 us
  starting transfers between devices  95.9 us (34%)
  waiting for transfers between devices  90.9 us (33%)
  blocking collectives  42.5 us (15%)
  local copies, waits for them, and re-layouts  22.1 us (8%)
  matrix products  12.2 us (4%)
  other arithmetic  8.39 us (3%)
  between operations  4.07 us (1%)
    all_to_all x10, waiting for transfers between devices, swap(): return lax.all_to_all(chunks, axes, 0, 0, tiled=True)  70.8 us
    all_to_all x10, starting transfers between devices, swap(): return lax.all_to_all(chunks, axes, 0, 0, tiled=True)  54.2 us
    ppermute x12, starting transfers between devices, from_right(): return lax.ppermute(values, 'x', pairs)  41.8 us
    all_to_all x3, blocking collectives, swap(): return lax.all_to_all(chunks, axes, 0, 0, tiled=True)  39.9 us
    ppermute x12, waiting for transfers between devices, from_right(): return lax.ppermute(values, 'x', pairs)  20.2 us
    dot_general x10, matrix products, mm(): return jnp.dot(left, right, precision=EXACT)  7.78 us
  transfers between devices with their start and end apart: 22, of which 10 were waited for; matrix products, arithmetic and copies ran while one was open for 10% of the time, Pallas kernels for 0%

profile of v9, /device:TPU:1, one launch (start us, length us, event | category | flops | bytes accessed | tf_op | source)
XLA Modules:
  0.0 276.2 jit_solution(15118353101261554538)
XLA Ops:
  2.2 5.2 %collective-permute-start = (f32[3,32,256]{2,1,0:T(8,128)S(1)}, f32[3,32,256]{2,1,0:T(8,128)}, u32[]{:S(2)}, u32[]{:S(2)}) collective-permute-start(f32[3,32,256]{2,1,0:T(8,128)S(1)} %constant_dynamic-update-slice_fusion), channel_id=1, source_target_pairs={{2,0},{4,2},{6,4},{0,6},{3,1},{5,3},{7,5},{1,7},{10,8},{12,10},{14... | collective-permute-start | bytes 294920 | tf_op jit(solution)/shard_map/ppermute | solution.py:74
  7.4 2.4 collective-permute-start.1
  9.9 2.5 collective-permute-start.2
  12.4 4.0 %collective-permute-start.6 = (f32[32,2048]{1,0:T(8,128)}, f32[32,2048]{1,0:T(8,128)S(1)}, u32[]{:S(2)}, u32[]{:S(2)}) collective-permute-start(f32[32,2048]{1,0:T(8,128)} %param.21), channel_id=1, source_target_pairs={{2,0},{4,2},{6,4},{0,6},{3,1},{5,3},{7,5},{1,7},{10,8},{12,10},{14... | collective-permute-start | bytes 786440 | tf_op jit(solution)/shard_map/ppermute | solution.py:74
  16.4 3.2 %collective-permute-start.7 = (f32[32,2048]{1,0:T(8,128)}, f32[32,2048]{1,0:T(8,128)}, u32[]{:S(2)}, u32[]{:S(2)}) collective-permute-start(f32[32,2048]{1,0:T(8,128)} %param.21), channel_id=1, source_target_pairs={{4,0},{6,2},{0,4},{2,6},{5,1},{7,3},{1,5},{3,7},{12,8},{14,10},{8,... | collective-permute-start | bytes 786440 | tf_op jit(solution)/shard_map/ppermute | solution.py:74
  19.6 1.3 fusion.56
  20.9 1.3 iota_compare_fusion.1
  24.8 1.0 convolution_select_fusion.5
  26.9 1.0 fusion.5
  27.9 1.0 convolution_select_fusion.3
  31.5 14.4 %all-to-all-start = ((f32[64,8,128]{2,1,0:T(8,128)}), f32[64,8,128]{2,1,0:T(8,128)S(1)}, u32[]{:S(2)}, u32[]{:S(2)}) async-start(f32[64,8,128]{2,1,0:T(8,128)} %copy.70), calls=%async_computation | async-start | bytes 524288 | tf_op jit(solution)/shard_map/all_to_all | solution.py:22
  46.3 12.7 %all-to-all-done = f32[64,8,128]{2,1,0:T(8,128)S(1)} async-done(((f32[64,8,128]{2,1,0:T(8,128)}), f32[64,8,128]{2,1,0:T(8,128)S(1)}, u32[]{:S(2)}, u32[]{:S(2)}) %all-to-all-start) | async-done | bytes 262176 | tf_op jit(solution)/shard_map/all_to_all | solution.py:22
  59.2 1.3 fusion.35
  62.0 4.8 %all-to-all-start.1 = ((f32[64,8,128]{2,1,0:T(8,128)}), f32[64,8,128]{2,1,0:T(8,128)S(1)}, u32[]{:S(2)}, u32[]{:S(2)}) async-start(f32[64,8,128]{2,1,0:T(8,128)} %copy.73), calls=%async_computation.1 | async-start | bytes 524288 | tf_op jit(solution)/shard_map/all_to_all | solution.py:22
  67.7 3.3 %collective-permute-start.8 = (f32[32,2048]{1,0:T(8,128)}, f32[32,2048]{1,0:T(8,128)}, u32[]{:S(2)}, u32[]{:S(2)}) collective-permute-start(f32[32,2048]{1,0:T(8,128)} %param.21), channel_id=1, source_target_pairs={{6,0},{0,2},{2,4},{4,6},{7,1},{1,3},{3,5},{5,7},{14,8},{8,10},{10,... | collective-permute-start | bytes 786440 | tf_op jit(solution)/shard_map/ppermute | solution.py:74
  71.0 1.0 pad_maximum_fusion.3
  72.0 2.7 all-gather
  74.7 5.2 %all-to-all-done.1 = f32[64,8,128]{2,1,0:T(8,128)S(1)} async-done(((f32[64,8,128]{2,1,0:T(8,128)}), f32[64,8,128]{2,1,0:T(8,128)S(1)}, u32[]{:S(2)}, u32[]{:S(2)}) %all-to-all-start.1) | async-done | bytes 262176 | tf_op jit(solution)/shard_map/all_to_all | solution.py:22
  81.5 1.1 copy.78
  82.6 4.8 %all-to-all-start.2 = ((f32[64,8,256]{2,1,0:T(8,128)}), f32[64,8,256]{2,1,0:T(8,128)S(1)}, u32[]{:S(2)}, u32[]{:S(2)}) async-start(f32[64,8,256]{2,1,0:T(8,128)} %copy.78), calls=%async_computation.2 | async-start | bytes 1048576 | tf_op jit(solution)/shard_map/all_to_all | solution.py:22
  87.4 3.3 %collective-permute-start.5 = (f32[32,4224]{1,0:T(8,128)S(1)}, f32[32,4224]{1,0:T(8,128)S(1)}, u32[]{:S(2)}, u32[]{:S(2)}) collective-permute-start(f32[32,4224]{1,0:T(8,128)S(1)} %pad_maximum_fusion.2), channel_id=1, source_target_pairs={{6,0},{0,2},{2,4},{4,6},{7,1},{1,3},{3,5},{5,7},{14,8},{8,10},{10,... | collective-permute-start | bytes 1622024 | tf_op jit(solution)/shard_map/ppermute | solution.py:74
  90.6 4.3 %collective-permute-start.4 = (f32[32,4224]{1,0:T(8,128)S(1)}, f32[32,4224]{1,0:T(8,128)S(1)}, u32[]{:S(2)}, u32[]{:S(2)}) collective-permute-start(f32[32,4224]{1,0:T(8,128)S(1)} %pad_maximum_fusion.2), channel_id=1, source_target_pairs={{4,0},{6,2},{0,4},{2,6},{5,1},{7,3},{1,5},{3,7},{12,8},{14,10},{8,... | collective-permute-start | bytes 1622024 | tf_op jit(solution)/shard_map/ppermute | solution.py:74
  95.0 3.1 %collective-permute-start.3 = (f32[32,4224]{1,0:T(8,128)S(1)}, f32[32,4224]{1,0:T(8,128)S(1)}, u32[]{:S(2)}, u32[]{:S(2)}) collective-permute-start(f32[32,4224]{1,0:T(8,128)S(1)} %pad_maximum_fusion.2), channel_id=1, source_target_pairs={{2,0},{4,2},{6,4},{0,6},{3,1},{5,3},{7,5},{1,7},{10,8},{12,10},{14... | collective-permute-start | bytes 1622024 | tf_op jit(solution)/shard_map/ppermute | solution.py:74
  98.3 2.3 pad_maximum_fusion.1
  101.2 20.2 %collective-permute-done.3 = f32[32,4224]{1,0:T(8,128)S(1)} collective-permute-done((f32[32,4224]{1,0:T(8,128)S(1)}, f32[32,4224]{1,0:T(8,128)S(1)}, u32[]{:S(2)}, u32[]{:S(2)}) %collective-permute-start.3) | collective-permute-done | bytes 540704 | tf_op jit(solution)/shard_map/ppermute | solution.py:74
  125.6 6.8 %all-to-all-start.3 = ((f32[8,8,256]{2,1,0:T(8,128)}), f32[8,8,256]{2,1,0:T(8,128)S(1)}, u32[]{:S(2)}, u32[]{:S(2)}) async-start(f32[8,8,256]{2,1,0:T(8,128)} %broadcast_in_dim.121), calls=%async_computation.3 | async-start | bytes 131072 | tf_op jit(solution)/shard_map/all_to_all | solution.py:22
  132.4 1.5 pad_maximum_fusion
  134.0 5.7 %all-to-all-done.3 = f32[8,8,256]{2,1,0:T(8,128)S(1)} async-done(((f32[8,8,256]{2,1,0:T(8,128)}), f32[8,8,256]{2,1,0:T(8,128)S(1)}, u32[]{:S(2)}, u32[]{:S(2)}) %all-to-all-start.3) | async-done | bytes 65568 | tf_op jit(solution)/shard_map/all_to_all | solution.py:22
  140.6 5.4 %all-to-all-start.4 = ((f32[8,4,256]{2,1,0:T(4,128)}), f32[8,4,256]{2,1,0:T(4,128)S(1)}, u32[]{:S(2)}, u32[]{:S(2)}) async-start(f32[8,4,256]{2,1,0:T(4,128)} %broadcast_in_dim.122), calls=%async_computation.4 | async-start | bytes 65536 | tf_op jit(solution)/shard_map/all_to_all | solution.py:22
  146.0 6.9 %all-to-all-done.4 = f32[8,4,256]{2,1,0:T(4,128)S(1)} async-done(((f32[8,4,256]{2,1,0:T(4,128)}), f32[8,4,256]{2,1,0:T(4,128)S(1)}, u32[]{:S(2)}, u32[]{:S(2)}) %all-to-all-start.4) | async-done | bytes 32800 | tf_op jit(solution)/shard_map/all_to_all | solution.py:22
  153.8 3.3 %all-to-all-start.5 = ((f32[8,4,256]{2,1,0:T(4,128)}), f32[8,4,256]{2,1,0:T(4,128)S(1)}, u32[]{:S(2)}, u32[]{:S(2)}) async-start(f32[8,4,256]{2,1,0:T(4,128)} %broadcast_in_dim.123), calls=%async_computation.5 | async-start | bytes 65536 | tf_op jit(solution)/shard_map/all_to_all | solution.py:22
  157.2 6.8 %all-to-all-done.5 = f32[8,4,256]{2,1,0:T(4,128)S(1)} async-done(((f32[8,4,256]{2,1,0:T(4,128)}), f32[8,4,256]{2,1,0:T(4,128)S(1)}, u32[]{:S(2)}, u32[]{:S(2)}) %all-to-all-start.5) | async-done | bytes 32800 | tf_op jit(solution)/shard_map/all_to_all | solution.py:22
  164.9 3.3 %all-to-all-start.6 = ((f32[8,4,256]{2,1,0:T(4,128)}), f32[8,4,256]{2,1,0:T(4,128)S(1)}, u32[]{:S(2)}, u32[]{:S(2)}) async-start(f32[8,4,256]{2,1,0:T(4,128)} %broadcast_in_dim.124), calls=%async_computation.6 | async-start | bytes 65536 | tf_op jit(solution)/shard_map/all_to_all | solution.py:22
  168.2 6.8 %all-to-all-done.6 = f32[8,4,256]{2,1,0:T(4,128)S(1)} async-done(((f32[8,4,256]{2,1,0:T(4,128)}), f32[8,4,256]{2,1,0:T(4,128)S(1)}, u32[]{:S(2)}, u32[]{:S(2)}) %all-to-all-start.6) | async-done | bytes 32800 | tf_op jit(solution)/shard_map/all_to_all | solution.py:22
  176.0 3.3 %all-to-all-start.7 = ((f32[8,4,256]{2,1,0:T(4,128)}), f32[8,4,256]{2,1,0:T(4,128)S(1)}, u32[]{:S(2)}, u32[]{:S(2)}) async-start(f32[8,4,256]{2,1,0:T(4,128)} %broadcast_in_dim.125), calls=%async_computation.7 | async-start | bytes 65536 | tf_op jit(solution)/shard_map/all_to_all | solution.py:22
  179.4 6.7 %all-to-all-done.7 = f32[8,4,256]{2,1,0:T(4,128)S(1)} async-done(((f32[8,4,256]{2,1,0:T(4,128)}), f32[8,4,256]{2,1,0:T(4,128)S(1)}, u32[]{:S(2)}, u32[]{:S(2)}) %all-to-all-start.7) | async-done | bytes 32800 | tf_op jit(solution)/shard_map/all_to_all | solution.py:22
  186.4 9.2 %all_to_all.65 = f32[8,4,256]{2,1,0:T(4,128)S(1)} all-to-all(f32[8,4,256]{2,1,0:T(4,128)S(1)} %broadcast_in_dim.126), channel_id=1, replica_groups=mesh['grp'=8,'z'=8,'x'=4,'core'=2] {'z'}, dimensions={0} | all-to-all | bytes 65536 | tf_op jit(solution)/shard_map/all_to_all | solution.py:22
  196.0 9.2 %all_to_all.66 = f32[8,4,256]{2,1,0:T(4,128)S(1)} all-to-all(f32[8,4,256]{2,1,0:T(4,128)S(1)} %broadcast_in_dim.127), channel_id=1, replica_groups=mesh['grp'=8,'z'=8,'x'=4,'core'=2] {'grp'}, dimensions={0} | all-to-all | bytes 65536 | tf_op jit(solution)/shard_map/all_to_all | solution.py:22
  205.3 21.4 %all_to_all.67 = f32[16,8,256]{2,1,0:T(8,128)S(1)} all-to-all(f32[16,8,256]{2,1,0:T(8,128)S(1)} %broadcast_in_dim.128), channel_id=1, replica_groups=mesh['grp'=8,'z'=8,'x'=4,'core'=2] {'z','core'}, dimensions={0} | all-to-all | bytes 262144 | tf_op jit(solution)/shard_map/all_to_all | solution.py:22
  227.1 3.8 %collective-permute-start.11 = (f32[8,64]{1,0:T(8,128)S(1)}, f32[8,64]{1,0:T(8,128)S(1)}, u32[]{:S(2)}, u32[]{:S(2)}) collective-permute-start(f32[8,64]{1,0:T(8,128)S(1)} %pad_maximum_fusion.8), channel_id=1, source_target_pairs={{6,0},{0,2},{2,4},{4,6},{7,1},{1,3},{3,5},{5,7},{14,8},{8,10},{10,... | collective-permute-start | bytes 6152 | tf_op jit(solution)/shard_map/ppermute | solution.py:74
  230.9 3.6 %collective-permute-start.10 = (f32[8,64]{1,0:T(8,128)S(1)}, f32[8,64]{1,0:T(8,128)S(1)}, u32[]{:S(2)}, u32[]{:S(2)}) collective-permute-start(f32[8,64]{1,0:T(8,128)S(1)} %pad_maximum_fusion.7), channel_id=1, source_target_pairs={{4,0},{6,2},{0,4},{2,6},{5,1},{7,3},{1,5},{3,7},{12,8},{14,10},{8,... | collective-permute-start | bytes 6152 | tf_op jit(solution)/shard_map/ppermute | solution.py:74
  234.6 3.2 %collective-permute-start.9 = (f32[8,64]{1,0:T(8,128)S(1)}, f32[8,64]{1,0:T(8,128)S(1)}, u32[]{:S(2)}, u32[]{:S(2)}) collective-permute-start(f32[8,64]{1,0:T(8,128)S(1)} %pad_maximum_fusion.6), channel_id=1, source_target_pairs={{2,0},{4,2},{6,4},{0,6},{3,1},{5,3},{7,5},{1,7},{10,8},{12,10},{14... | collective-permute-start | bytes 6152 | tf_op jit(solution)/shard_map/ppermute | solution.py:74
  237.8 1.7 fusion.60
  240.3 3.8 %all-to-all-start.11 = ((f32[16,8,128]{2,1,0:T(8,128)}), f32[16,8,128]{2,1,0:T(8,128)S(1)}, u32[]{:S(2)}, u32[]{:S(2)}) async-start(f32[16,8,128]{2,1,0:T(8,128)} %broadcast_in_dim.129), calls=%async_computation.11 | async-start | bytes 131072 | tf_op jit(solution)/shard_map/all_to_all | solution.py:22
  244.2 7.7 %all-to-all-done.11 = f32[16,8,128]{2,1,0:T(8,128)S(1)} async-done(((f32[16,8,128]{2,1,0:T(8,128)}), f32[16,8,128]{2,1,0:T(8,128)S(1)}, u32[]{:S(2)}, u32[]{:S(2)}) %all-to-all-start.11) | async-done | bytes 65568 | tf_op jit(solution)/shard_map/all_to_all | solution.py:22
  254.3 4.2 %all-to-all-start.12 = ((f32[64,8,128]{2,1,0:T(8,128)}), f32[64,8,128]{2,1,0:T(8,128)S(1)}, u32[]{:S(2)}, u32[]{:S(2)}) async-start(f32[64,8,128]{2,1,0:T(8,128)} %broadcast_in_dim.130), calls=%async_computation.12 | async-start | bytes 524288 | tf_op jit(solution)/shard_map/all_to_all | solution.py:22
  259.4 12.3 %all-to-all-done.12 = f32[64,8,128]{2,1,0:T(8,128)S(1)} async-done(((f32[64,8,128]{2,1,0:T(8,128)}), f32[64,8,128]{2,1,0:T(8,128)S(1)}, u32[]{:S(2)}, u32[]{:S(2)}) %all-to-all-start.12) | async-done | bytes 262176 | tf_op jit(solution)/shard_map/all_to_all | solution.py:22
  273.0 1.4 reshape.108
  (142 shorter events, 26.8 us)
Async XLA Ops:
  2.2 65.5 %collective-permute-start = (f32[3,32,256]{2,1,0:T(8,128)S(1)}, f32[3,32,256]{2,1,0:T(8,128)}, u32[]{:S(2)}, u32[]{:S(2)}) collective-permute-start(f32[3,32,256]{2,1,0:T(8,128)S(1)} %constant_dynamic-update-slice_fusion), channel_id=1, source_target_pairs={{2,0},{4,2},{6,4},{0,6},{3,1},{5,3},{7,5},{1,7},{10,8},{12,10},{14... | collective-permute-start | bytes 294920 | tf_op jit(solution)/shard_map/ppermute | solution.py:74
  7.4 63.5 %collective-permute-start.1 = (f32[3,32,256]{2,1,0:T(8,128)S(1)}, f32[3,32,256]{2,1,0:T(8,128)}, u32[]{:S(2)}, u32[]{:S(2)}) collective-permute-start(f32[3,32,256]{2,1,0:T(8,128)S(1)} %constant_dynamic-update-slice_fusion), channel_id=1, source_target_pairs={{4,0},{6,2},{0,4},{2,6},{5,1},{7,3},{1,5},{3,7},{12,8},{14,10},{8,... | collective-permute-start | bytes 294920 | tf_op jit(solution)/shard_map/ppermute | solution.py:74
  9.9 61.1 %collective-permute-start.2 = (f32[3,32,256]{2,1,0:T(8,128)S(1)}, f32[3,32,256]{2,1,0:T(8,128)}, u32[]{:S(2)}, u32[]{:S(2)}) collective-permute-start(f32[3,32,256]{2,1,0:T(8,128)S(1)} %constant_dynamic-update-slice_fusion), channel_id=1, source_target_pairs={{6,0},{0,2},{2,4},{4,6},{7,1},{1,3},{3,5},{5,7},{14,8},{8,10},{10,... | collective-permute-start | bytes 294920 | tf_op jit(solution)/shard_map/ppermute | solution.py:74
  12.4 82.6 %collective-permute-start.6 = (f32[32,2048]{1,0:T(8,128)}, f32[32,2048]{1,0:T(8,128)S(1)}, u32[]{:S(2)}, u32[]{:S(2)}) collective-permute-start(f32[32,2048]{1,0:T(8,128)} %param.21), channel_id=1, source_target_pairs={{2,0},{4,2},{6,4},{0,6},{3,1},{5,3},{7,5},{1,7},{10,8},{12,10},{14... | collective-permute-start | bytes 786440 | tf_op jit(solution)/shard_map/ppermute | solution.py:74
  16.4 81.9 %collective-permute-start.7 = (f32[32,2048]{1,0:T(8,128)}, f32[32,2048]{1,0:T(8,128)}, u32[]{:S(2)}, u32[]{:S(2)}) collective-permute-start(f32[32,2048]{1,0:T(8,128)} %param.21), channel_id=1, source_target_pairs={{4,0},{6,2},{0,4},{2,6},{5,1},{7,3},{1,5},{3,7},{12,8},{14,10},{8,... | collective-permute-start | bytes 786440 | tf_op jit(solution)/shard_map/ppermute | solution.py:74
  28.9 2.6 copy-start.9
  30.3 28.9 %copy-start.12 = (f32[32,32]{1,0:T(8,128)S(1)}, f32[32,32]{1,0:T(8,128)}, u32[]{:S(2)}) copy-start(f32[32,32]{1,0:T(8,128)} %param.20) | copy-start | bytes 12292
  31.5 27.5 %all-to-all-start = ((f32[64,8,128]{2,1,0:T(8,128)}), f32[64,8,128]{2,1,0:T(8,128)S(1)}, u32[]{:S(2)}, u32[]{:S(2)}) async-start(f32[64,8,128]{2,1,0:T(8,128)} %copy.70), calls=%async_computation | async-start | bytes 524288 | tf_op jit(solution)/shard_map/all_to_all | solution.py:22
  61.1 18.9 %copy-start = (f32[32,4096]{1,0:T(8,128)S(1)}, f32[32,4096]{1,0:T(8,128)}, u32[]{:S(2)}) copy-start(f32[32,4096]{1,0:T(8,128)} %param.22) | copy-start | bytes 1572868
  62.0 17.9 %all-to-all-start.1 = ((f32[64,8,128]{2,1,0:T(8,128)}), f32[64,8,128]{2,1,0:T(8,128)S(1)}, u32[]{:S(2)}, u32[]{:S(2)}) async-start(f32[64,8,128]{2,1,0:T(8,128)} %copy.73), calls=%async_computation.1 | async-start | bytes 524288 | tf_op jit(solution)/shard_map/all_to_all | solution.py:22
  67.7 30.6 %collective-permute-start.8 = (f32[32,2048]{1,0:T(8,128)}, f32[32,2048]{1,0:T(8,128)}, u32[]{:S(2)}, u32[]{:S(2)}) collective-permute-start(f32[32,2048]{1,0:T(8,128)} %param.21), channel_id=1, source_target_pairs={{6,0},{0,2},{2,4},{4,6},{7,1},{1,3},{3,5},{5,7},{14,8},{8,10},{10,... | collective-permute-start | bytes 786440 | tf_op jit(solution)/shard_map/ppermute | solution.py:74
  82.6 42.3 %all-to-all-start.2 = ((f32[64,8,256]{2,1,0:T(8,128)}), f32[64,8,256]{2,1,0:T(8,128)S(1)}, u32[]{:S(2)}, u32[]{:S(2)}) async-start(f32[64,8,256]{2,1,0:T(8,128)} %copy.78), calls=%async_computation.2 | async-start | bytes 1048576 | tf_op jit(solution)/shard_map/all_to_all | solution.py:22
  87.4 35.7 %collective-permute-start.5 = (f32[32,4224]{1,0:T(8,128)S(1)}, f32[32,4224]{1,0:T(8,128)S(1)}, u32[]{:S(2)}, u32[]{:S(2)}) collective-permute-start(f32[32,4224]{1,0:T(8,128)S(1)} %pad_maximum_fusion.2), channel_id=1, source_target_pairs={{6,0},{0,2},{2,4},{4,6},{7,1},{1,3},{3,5},{5,7},{14,8},{8,10},{10,... | collective-permute-start | bytes 1622024 | tf_op jit(solution)/shard_map/ppermute | solution.py:74
  90.6 31.6 %collective-permute-start.4 = (f32[32,4224]{1,0:T(8,128)S(1)}, f32[32,4224]{1,0:T(8,128)S(1)}, u32[]{:S(2)}, u32[]{:S(2)}) collective-permute-start(f32[32,4224]{1,0:T(8,128)S(1)} %pad_maximum_fusion.2), channel_id=1, source_target_pairs={{4,0},{6,2},{0,4},{2,6},{5,1},{7,3},{1,5},{3,7},{12,8},{14,10},{8,... | collective-permute-start | bytes 1622024 | tf_op jit(solution)/shard_map/ppermute | solution.py:74
  95.0 3.2 %copy-start.8 = (f32[32,2048]{1,0:T(8,128)}, f32[32,2048]{1,0:T(8,128)S(1)}, u32[]{:S(2)}) copy-start(f32[32,2048]{1,0:T(8,128)S(1)} %collective-permute-done.6) | copy-start | bytes 786436
  95.0 26.3 %collective-permute-start.3 = (f32[32,4224]{1,0:T(8,128)S(1)}, f32[32,4224]{1,0:T(8,128)S(1)}, u32[]{:S(2)}, u32[]{:S(2)}) collective-permute-start(f32[32,4224]{1,0:T(8,128)S(1)} %pad_maximum_fusion.2), channel_id=1, source_target_pairs={{2,0},{4,2},{6,4},{0,6},{3,1},{5,3},{7,5},{1,7},{10,8},{12,10},{14... | collective-permute-start | bytes 1622024 | tf_op jit(solution)/shard_map/ppermute | solution.py:74
  121.3 1.8 copy-start.4
  122.2 1.0 copy-start.3
  123.2 0.8 copy-start.2
  125.6 14.0 %all-to-all-start.3 = ((f32[8,8,256]{2,1,0:T(8,128)}), f32[8,8,256]{2,1,0:T(8,128)S(1)}, u32[]{:S(2)}, u32[]{:S(2)}) async-start(f32[8,8,256]{2,1,0:T(8,128)} %broadcast_in_dim.121), calls=%async_computation.3 | async-start | bytes 131072 | tf_op jit(solution)/shard_map/all_to_all | solution.py:22
  132.4 13.6 %slice-start = ((f32[32,4224]{1,0:T(8,128)}), f32[32,128]{1,0:T(8,128)S(1)}, s32[]{:S(2)}) async-start(f32[32,4224]{1,0:T(8,128)} %copy-done.2), calls=%async_computation.13 | async-start | bytes 32768 | tf_op jit(solution)/shard_map/slice | solution.py:141
  132.4 24.8 %slice-start.1 = ((f32[32,4224]{1,0:T(8,128)}), f32[32,128]{1,0:T(8,128)S(1)}, s32[]{:S(2)}) async-start(f32[32,4224]{1,0:T(8,128)} %copy-done.3), calls=%async_computation.14 | async-start | bytes 32768 | tf_op jit(solution)/shard_map/slice | solution.py:141
  132.4 35.8 %slice-start.2 = ((f32[32,4224]{1,0:T(8,128)}), f32[32,128]{1,0:T(8,128)S(1)}, s32[]{:S(2)}) async-start(f32[32,4224]{1,0:T(8,128)} %copy-done.4), calls=%async_computation.15 | async-start | bytes 32768 | tf_op jit(solution)/shard_map/slice | solution.py:141
  132.4 46.9 %copy-start.13 = (f32[8,128]{1,0:T(8,128)S(1)}, f32[8,128]{1,0:T(8,128)}, u32[]{:S(2)}) copy-start(f32[8,128]{1,0:T(8,128)} %constant_dynamic-slice_fusion.12) | copy-start | bytes 12292
  140.6 12.3 %all-to-all-start.4 = ((f32[8,4,256]{2,1,0:T(4,128)}), f32[8,4,256]{2,1,0:T(4,128)S(1)}, u32[]{:S(2)}, u32[]{:S(2)}) async-start(f32[8,4,256]{2,1,0:T(4,128)} %broadcast_in_dim.122), calls=%async_computation.4 | async-start | bytes 65536 | tf_op jit(solution)/shard_map/all_to_all | solution.py:22
  153.8 10.1 %all-to-all-start.5 = ((f32[8,4,256]{2,1,0:T(4,128)}), f32[8,4,256]{2,1,0:T(4,128)S(1)}, u32[]{:S(2)}, u32[]{:S(2)}) async-start(f32[8,4,256]{2,1,0:T(4,128)} %broadcast_in_dim.123), calls=%async_computation.5 | async-start | bytes 65536 | tf_op jit(solution)/shard_map/all_to_all | solution.py:22
  164.9 10.1 %all-to-all-start.6 = ((f32[8,4,256]{2,1,0:T(4,128)}), f32[8,4,256]{2,1,0:T(4,128)S(1)}, u32[]{:S(2)}, u32[]{:S(2)}) async-start(f32[8,4,256]{2,1,0:T(4,128)} %broadcast_in_dim.124), calls=%async_computation.6 | async-start | bytes 65536 | tf_op jit(solution)/shard_map/all_to_all | solution.py:22
  176.0 10.1 %all-to-all-start.7 = ((f32[8,4,256]{2,1,0:T(4,128)}), f32[8,4,256]{2,1,0:T(4,128)S(1)}, u32[]{:S(2)}, u32[]{:S(2)}) async-start(f32[8,4,256]{2,1,0:T(4,128)} %broadcast_in_dim.125), calls=%async_computation.7 | async-start | bytes 65536 | tf_op jit(solution)/shard_map/all_to_all | solution.py:22
  226.8 25.8 %copy-start.1 = (f32[128,2048]{1,0:T(8,128)S(1)}, f32[128,2048]{1,0:T(8,128)}, u32[]{:S(2)}) copy-start(f32[128,2048]{1,0:T(8,128)} %pad_maximum_fusion.1) | copy-start | bytes 3145732
  227.1 17.1 %collective-permute-start.11 = (f32[8,64]{1,0:T(8,128)S(1)}, f32[8,64]{1,0:T(8,128)S(1)}, u32[]{:S(2)}, u32[]{:S(2)}) collective-permute-start(f32[8,64]{1,0:T(8,128)S(1)} %pad_maximum_fusion.8), channel_id=1, source_target_pairs={{6,0},{0,2},{2,4},{4,6},{7,1},{1,3},{3,5},{5,7},{14,8},{8,10},{10,... | collective-permute-start | bytes 6152 | tf_op jit(solution)/shard_map/ppermute | solution.py:74
  230.9 13.2 %collective-permute-start.10 = (f32[8,64]{1,0:T(8,128)S(1)}, f32[8,64]{1,0:T(8,128)S(1)}, u32[]{:S(2)}, u32[]{:S(2)}) collective-permute-start(f32[8,64]{1,0:T(8,128)S(1)} %pad_maximum_fusion.7), channel_id=1, source_target_pairs={{4,0},{6,2},{0,4},{2,6},{5,1},{7,3},{1,5},{3,7},{12,8},{14,10},{8,... | collective-permute-start | bytes 6152 | tf_op jit(solution)/shard_map/ppermute | solution.py:74
  234.6 9.5 %collective-permute-start.9 = (f32[8,64]{1,0:T(8,128)S(1)}, f32[8,64]{1,0:T(8,128)S(1)}, u32[]{:S(2)}, u32[]{:S(2)}) collective-permute-start(f32[8,64]{1,0:T(8,128)S(1)} %pad_maximum_fusion.6), channel_id=1, source_target_pairs={{2,0},{4,2},{6,4},{0,6},{3,1},{5,3},{7,5},{1,7},{10,8},{12,10},{14... | collective-permute-start | bytes 6152 | tf_op jit(solution)/shard_map/ppermute | solution.py:74
  240.3 11.6 %all-to-all-start.11 = ((f32[16,8,128]{2,1,0:T(8,128)}), f32[16,8,128]{2,1,0:T(8,128)S(1)}, u32[]{:S(2)}, u32[]{:S(2)}) async-start(f32[16,8,128]{2,1,0:T(8,128)} %broadcast_in_dim.129), calls=%async_computation.11 | async-start | bytes 131072 | tf_op jit(solution)/shard_map/all_to_all | solution.py:22
  254.3 17.4 %all-to-all-start.12 = ((f32[64,8,128]{2,1,0:T(8,128)}), f32[64,8,128]{2,1,0:T(8,128)S(1)}, u32[]{:S(2)}, u32[]{:S(2)}) async-start(f32[64,8,128]{2,1,0:T(8,128)} %broadcast_in_dim.130), calls=%async_computation.12 | async-start | bytes 524288 | tf_op jit(solution)/shard_map/all_to_all | solution.py:22
  259.4 15.0 %copy-start.5 = (f32[2,128,128]{2,1,0:T(8,128)S(1)}, f32[2,128,128]{2,1,0:T(8,128)}, u32[]{:S(2)}) copy-start(f32[2,128,128]{2,1,0:T(8,128)} %param.16) | copy-start | bytes 393220
  259.4 15.3 %copy-start.10 = (f32[32,128]{1,0:T(8,128)S(1)}, f32[32,128]{1,0:T(8,128)}, u32[]{:S(2)}) copy-start(f32[32,128]{1,0:T(8,128)} %copy-done.9) | copy-start | bytes 49156
  272.2 2.7 copy-start.6
  272.2 3.0 %copy-start.11 = (f32[2,128,128]{2,1,0:T(8,128)S(1)}, f32[2,128,128]{2,1,0:T(8,128)}, u32[]{:S(2)}) copy-start(f32[2,128,128]{2,1,0:T(8,128)} %param.15) | copy-start | bytes 393220
  274.4 1.9 copy-start.7

commit v10 on v9

--- a/solution.py
+++ b/solution.py
@@ -1,6 +1,8 @@
 import jax
 import jax.numpy as jnp
 from jax import lax
+from jax.experimental import pallas as pl
+from jax.experimental.pallas import tpu as pltpu
 from jax.sharding import Mesh
 from jax.sharding import PartitionSpec as P
 
@@ -34,6 +36,57 @@
     tall, width = values.shape
     thin = width // folds
     return values.reshape(tall, folds, thin).transpose(1, 0, 2).reshape(folds * tall, thin)
+
+
+def leaf_forward(parents, targets, live, right, inverse, link, front, solved, chunks):
+    rows, width = right.shape[0], inverse.shape[1]
+    folds = chunks.shape[2] // (width // 4)
+    tall = rows // folds
+    alive = jnp.full((rows, width), live[0], jnp.int32)
+    first = jnp.where(alive > 0, mm(right[:, :width], inverse[0]), 0.0)
+    lifted = jnp.where(alive > parents[0], mm(first, link[0]), 0.0)
+    second = jnp.where(alive > 1, mm(right[:, width:] - lifted, inverse[1]), 0.0)
+    solved[:, :width] = first
+    solved[:, width:] = second
+    chunks[...] = jnp.zeros(chunks.shape, jnp.float32)
+    lane = lax.broadcasted_iota(jnp.int32, (tall, width), 1)
+    for block, values in enumerate((first, second)):
+        given = mm(values, front[block])
+        for piece in range(4):
+            made = jnp.zeros((tall, width), jnp.float32)
+            for fold in range(folds):
+                move = (fold - piece) * (width // 4) % width
+                moved = given[fold * tall : (fold + 1) * tall]
+                moved = pltpu.roll(moved, move, 1) if move else moved
+                inside = (lane >= fold * (width // 4)) & (lane < (fold + 1) * (width // 4))
+                made = jnp.where(inside, moved, made)
+            spot = targets[block] * 4 + piece
+            chunks[spot] = chunks[spot] + made
+
+
+def whole_block(array, space=None):
+    zeros = (0,) * array.ndim
+    if space is not None:
+        return pl.BlockSpec(memory_space=space)
+    return pl.BlockSpec(array.shape, lambda i: zeros)
+
+
+def leaf_start(parents, targets, live, right, inverse, link, front, n_dev):
+    rows, span = right.shape
+    outs = (
+        jax.ShapeDtypeStruct((rows, span), jnp.float32),
+        jax.ShapeDtypeStruct((n_dev, rows // 4, 128), jnp.float32),
+    )
+    scalars, arrays = (parents, targets, live), (right, inverse, link, front)
+    specs = [whole_block(item, pltpu.SMEM) for item in scalars]
+    specs += [whole_block(item) for item in arrays]
+    return pl.pallas_call(
+        leaf_forward,
+        grid=(1,),
+        in_specs=specs,
+        out_specs=tuple(whole_block(item) for item in outs),
+        out_shape=outs,
+    )(*scalars, *arrays)
 
 
 def make_body(sizes):
@@ -60,7 +113,6 @@
         rows = leaf_right.shape[0]
         width = leaf_inverse.shape[1]
         front_order = front_inverse.shape[1]
-        n_front = front_order // width
         share = front_inverse.shape[0]
         part = root_inverse.shape[2]
         few = rows // n_near
@@ -94,15 +146,10 @@
             return unfold(jnp.sum(swap(chunks.reshape(n_dev, rows // 4, 4 * share), DEV), 0), 4)
 
         has_parent = parents[0] < live
-        right0, right1 = leaf_right[:, :width], leaf_right[:, width:]
-        solved0 = jnp.where(live > 0, mm(right0, leaf_inverse[0]), 0.0)
-        lifted = jnp.where(has_parent, mm(solved0, leaf_link[0]), 0.0)
-        solved1 = jnp.where(live > 1, mm(right1 - lifted, leaf_inverse[1]), 0.0)
-        given0, given1 = mm(solved0, leaf_front[0]), mm(solved1, leaf_front[1])
-        slots = jnp.arange(n_front, dtype=jnp.int32)[None, :, None]
-        placed = jnp.where(slots == front_rows[0], given0[:, None, :], 0.0) + jnp.where(
-            slots == front_rows[1], given1[:, None, :], 0.0
+        solved, placed = leaf_start(
+            parents, front_rows, live_blocks, leaf_right, leaf_inverse, leaf_link, leaf_front, n_dev
         )
+        solved0, solved1 = solved[:, :width], solved[:, width:]
         behind = (n_x - my_x) % n_x
         spots = [my_x * (n_core * share), my_x * some]
         spots += [behind * size for size in (n_core * share, share, some)]
@@ -111,10 +158,10 @@
             spots += [spot, spot + front_order]
         spots += [front_rows[block] * width for block in range(2)]
         spots = tuple(spot.astype(jnp.uint32) for spot in spots)
-        placed, spots = lax.optimization_barrier((placed, spots))
+        start = front_right - unfold(jnp.sum(swap(placed, DEV), 0), 4)
+        start, spots = lax.optimization_barrier((start, spots))
         ahead_part, rows_x, back_part, back_share, back_rows = spots[:5]
         root_spots, leaf_spots = spots[5:-2], spots[-2:]
-        start = front_right - dev_sum(placed.reshape(rows, front_order))
         y_own = dev_sum(mm(start, front_inverse))
         side = jnp.pad(y_own, ((0, 0), (0, width - share)))
         couples = from_all(jnp.concatenate([front_couple, side], 1))

time: 278 us -> 271 us (0.975)
  blocking collectives: 42.5 us -> 21.2 us
  starting transfers between devices: 95.9 us -> 109 us
  waiting for transfers between devices: 90.9 us -> 98.9 us
  matrix products: 12.2 us -> 7.24 us
    all_to_all x3 -> x2, blocking collectives: 39.9 us -> 18.5 us  [swap(): return lax.all_to_all(chunks, axes, 0, 0, tiled=True)]
    all_to_all x10 -> x11, starting transfers between devices: 54.2 us -> 67.3 us  [swap(): return lax.all_to_all(chunks, axes, 0, 0, tiled=True)]
    all_to_all x10 -> x11, waiting for transfers between devices: 70.8 us -> 78.1 us  [swap(): return lax.all_to_all(chunks, axes, 0, 0, tiled=True)]
    dot_general x10 -> x5, matrix products: 7.78 us -> 2.75 us  [mm(): return jnp.dot(left, right, precision=EXACT)]
  transfers between devices with their start and end apart: 22 -> 23, of which waited for: 10 -> 11; matrix products, arithmetic and copies ran while one was open for 10% -> 7% of each run, Pallas kernels for 0% -> 1%
where the time goes in v10:
time: 271 us; the launch traced here: 269 us
  starting transfers between devices  109 us (40%)
  waiting for transfers between devices  98.9 us (36%)
  blocking collectives  21.2 us (8%)
  local copies, waits for them, and re-layouts  19.8 us (7%)
  matrix products  7.24 us (3%)
  other arithmetic  6.97 us (3%)
  between operations  3.31 us (1%)
    all_to_all x11, waiting for transfers between devices, swap(): return lax.all_to_all(chunks, axes, 0, 0, tiled=True)  78.1 us
    all_to_all x11, starting transfers between devices, swap(): return lax.all_to_all(chunks, axes, 0, 0, tiled=True)  67.3 us
    ppermute x12, starting transfers between devices, from_right(): return lax.ppermute(values, 'x', pairs)  41.9 us
    ppermute x12, waiting for transfers between devices, from_right(): return lax.ppermute(values, 'x', pairs)  20.8 us
    all_to_all x2, blocking collectives, swap(): return lax.all_to_all(chunks, axes, 0, 0, tiled=True)  18.5 us
    broadcast_in_dim x10, local copies, waits for them, and re-layouts, spread(): return swap(jnp.broadcast_to(values[None], (count,) + values.shape), axes)  5.49 us
  transfers between devices with their start and end apart: 23, of which 11 were waited for; matrix products, arithmetic and copies ran while one was open for 7% of the time, Pallas kernels for 1%

profile of v10, /device:TPU:1, one launch (start us, length us, event | category | flops | bytes accessed | tf_op | source)
XLA Modules:
  0.0 269.2 jit_solution(6662355300262196155)
XLA Ops:
  2.3 5.2 %collective-permute-start = (f32[3,32,256]{2,1,0:T(8,128)S(1)}, f32[3,32,256]{2,1,0:T(8,128)}, u32[]{:S(2)}, u32[]{:S(2)}) collective-permute-start(f32[3,32,256]{2,1,0:T(8,128)S(1)} %constant_dynamic-update-slice_fusion), channel_id=1, source_target_pairs={{2,0},{4,2},{6,4},{0,6},{3,1},{5,3},{7,5},{1,7},{10,8},{12,10},{14... | collective-permute-start | bytes 294920 | tf_op jit(solution)/shard_map/ppermute | solution.py:126
  7.5 2.4 collective-permute-start.1
  9.9 2.5 collective-permute-start.2
  12.4 4.0 %collective-permute-start.6 = (f32[32,2048]{1,0:T(8,128)}, f32[32,2048]{1,0:T(8,128)S(1)}, u32[]{:S(2)}, u32[]{:S(2)}) collective-permute-start(f32[32,2048]{1,0:T(8,128)} %param.21), channel_id=1, source_target_pairs={{2,0},{4,2},{6,4},{0,6},{3,1},{5,3},{7,5},{1,7},{10,8},{12,10},{14... | collective-permute-start | bytes 786440 | tf_op jit(solution)/shard_map/ppermute | solution.py:126
  16.4 3.2 %collective-permute-start.7 = (f32[32,2048]{1,0:T(8,128)}, f32[32,2048]{1,0:T(8,128)}, u32[]{:S(2)}, u32[]{:S(2)}) collective-permute-start(f32[32,2048]{1,0:T(8,128)} %param.21), channel_id=1, source_target_pairs={{4,0},{6,2},{0,4},{2,6},{5,1},{7,3},{1,5},{3,7},{12,8},{14,10},{8,... | collective-permute-start | bytes 786440 | tf_op jit(solution)/shard_map/ppermute | solution.py:126
  20.2 2.6 shard_map.148
  22.8 14.4 %all-to-all-start = ((f32[64,8,128]{2,1,0:T(8,128)}), f32[64,8,128]{2,1,0:T(8,128)S(1)}, u32[]{:S(2)}, u32[]{:S(2)}) async-start(f32[64,8,128]{2,1,0:T(8,128)} %get-tuple-element.29), calls=%async_computation | async-start | bytes 524288 | tf_op jit(solution)/shard_map/all_to_all | solution.py:24
  37.3 1.3 fusion.40
  40.2 10.1 %all-to-all-done = f32[64,8,128]{2,1,0:T(8,128)S(1)} async-done(((f32[64,8,128]{2,1,0:T(8,128)}), f32[64,8,128]{2,1,0:T(8,128)S(1)}, u32[]{:S(2)}, u32[]{:S(2)}) %all-to-all-start) | async-done | bytes 262176 | tf_op jit(solution)/shard_map/all_to_all | solution.py:24
  50.5 1.3 fusion.41
  53.4 4.8 %all-to-all-start.1 = ((f32[64,8,128]{2,1,0:T(8,128)}), f32[64,8,128]{2,1,0:T(8,128)S(1)}, u32[]{:S(2)}, u32[]{:S(2)}) async-start(f32[64,8,128]{2,1,0:T(8,128)} %copy.65), calls=%async_computation.1 | async-start | bytes 524288 | tf_op jit(solution)/shard_map/all_to_all | solution.py:24
  58.2 3.3 %collective-permute-start.8 = (f32[32,2048]{1,0:T(8,128)}, f32[32,2048]{1,0:T(8,128)}, u32[]{:S(2)}, u32[]{:S(2)}) collective-permute-start(f32[32,2048]{1,0:T(8,128)} %param.21), channel_id=1, source_target_pairs={{6,0},{0,2},{2,4},{4,6},{7,1},{1,3},{3,5},{5,7},{14,8},{8,10},{10,... | collective-permute-start | bytes 786440 | tf_op jit(solution)/shard_map/ppermute | solution.py:126
  61.5 1.0 pad_maximum_fusion.3
  62.5 2.7 all-gather
  65.2 6.0 %all-to-all-done.1 = f32[64,8,128]{2,1,0:T(8,128)S(1)} async-done(((f32[64,8,128]{2,1,0:T(8,128)}), f32[64,8,128]{2,1,0:T(8,128)S(1)}, u32[]{:S(2)}, u32[]{:S(2)}) %all-to-all-start.1) | async-done | bytes 262176 | tf_op jit(solution)/shard_map/all_to_all | solution.py:24
  72.8 1.1 copy.70
  73.9 4.8 %all-to-all-start.2 = ((f32[64,8,256]{2,1,0:T(8,128)}), f32[64,8,256]{2,1,0:T(8,128)S(1)}, u32[]{:S(2)}, u32[]{:S(2)}) async-start(f32[64,8,256]{2,1,0:T(8,128)} %copy.70), calls=%async_computation.2 | async-start | bytes 1048576 | tf_op jit(solution)/shard_map/all_to_all | solution.py:24
  78.7 3.3 %collective-permute-start.5 = (f32[32,4224]{1,0:T(8,128)S(1)}, f32[32,4224]{1,0:T(8,128)S(1)}, u32[]{:S(2)}, u32[]{:S(2)}) collective-permute-start(f32[32,4224]{1,0:T(8,128)S(1)} %pad_maximum_fusion.2), channel_id=1, source_target_pairs={{6,0},{0,2},{2,4},{4,6},{7,1},{1,3},{3,5},{5,7},{14,8},{8,10},{10,... | collective-permute-start | bytes 1622024 | tf_op jit(solution)/shard_map/ppermute | solution.py:126
  82.0 4.3 %collective-permute-start.4 = (f32[32,4224]{1,0:T(8,128)S(1)}, f32[32,4224]{1,0:T(8,128)S(1)}, u32[]{:S(2)}, u32[]{:S(2)}) collective-permute-start(f32[32,4224]{1,0:T(8,128)S(1)} %pad_maximum_fusion.2), channel_id=1, source_target_pairs={{4,0},{6,2},{0,4},{2,6},{5,1},{7,3},{1,5},{3,7},{12,8},{14,10},{8,... | collective-permute-start | bytes 1622024 | tf_op jit(solution)/shard_map/ppermute | solution.py:126
  86.3 3.1 %collective-permute-start.3 = (f32[32,4224]{1,0:T(8,128)S(1)}, f32[32,4224]{1,0:T(8,128)S(1)}, u32[]{:S(2)}, u32[]{:S(2)}) collective-permute-start(f32[32,4224]{1,0:T(8,128)S(1)} %pad_maximum_fusion.2), channel_id=1, source_target_pairs={{2,0},{4,2},{6,4},{0,6},{3,1},{5,3},{7,5},{1,7},{10,8},{12,10},{14... | collective-permute-start | bytes 1622024 | tf_op jit(solution)/shard_map/ppermute | solution.py:126
  89.6 2.3 pad_maximum_fusion.1
  91.9 20.8 %collective-permute-done.3 = f32[32,4224]{1,0:T(8,128)S(1)} collective-permute-done((f32[32,4224]{1,0:T(8,128)S(1)}, f32[32,4224]{1,0:T(8,128)S(1)}, u32[]{:S(2)}, u32[]{:S(2)}) %collective-permute-start.3) | collective-permute-done | bytes 540704 | tf_op jit(solution)/shard_map/ppermute | solution.py:126
  112.7 0.9 slice.113
  116.9 6.8 %all-to-all-start.3 = ((f32[8,8,256]{2,1,0:T(8,128)}), f32[8,8,256]{2,1,0:T(8,128)S(1)}, u32[]{:S(2)}, u32[]{:S(2)}) async-start(f32[8,8,256]{2,1,0:T(8,128)} %broadcast_in_dim.35), calls=%async_computation.3 | async-start | bytes 131072 | tf_op jit(solution)/shard_map/all_to_all | solution.py:24
  123.8 1.5 pad_maximum_fusion
  125.3 5.7 %all-to-all-done.3 = f32[8,8,256]{2,1,0:T(8,128)S(1)} async-done(((f32[8,8,256]{2,1,0:T(8,128)}), f32[8,8,256]{2,1,0:T(8,128)S(1)}, u32[]{:S(2)}, u32[]{:S(2)}) %all-to-all-start.3) | async-done | bytes 65568 | tf_op jit(solution)/shard_map/all_to_all | solution.py:24
  131.9 5.4 %all-to-all-start.4 = ((f32[8,4,256]{2,1,0:T(4,128)}), f32[8,4,256]{2,1,0:T(4,128)S(1)}, u32[]{:S(2)}, u32[]{:S(2)}) async-start(f32[8,4,256]{2,1,0:T(4,128)} %broadcast_in_dim.36), calls=%async_computation.4 | async-start | bytes 65536 | tf_op jit(solution)/shard_map/all_to_all | solution.py:24
  137.3 6.9 %all-to-all-done.4 = f32[8,4,256]{2,1,0:T(4,128)S(1)} async-done(((f32[8,4,256]{2,1,0:T(4,128)}), f32[8,4,256]{2,1,0:T(4,128)S(1)}, u32[]{:S(2)}, u32[]{:S(2)}) %all-to-all-start.4) | async-done | bytes 32800 | tf_op jit(solution)/shard_map/all_to_all | solution.py:24
  145.2 3.3 %all-to-all-start.5 = ((f32[8,4,256]{2,1,0:T(4,128)}), f32[8,4,256]{2,1,0:T(4,128)S(1)}, u32[]{:S(2)}, u32[]{:S(2)}) async-start(f32[8,4,256]{2,1,0:T(4,128)} %broadcast_in_dim.37), calls=%async_computation.5 | async-start | bytes 65536 | tf_op jit(solution)/shard_map/all_to_all | solution.py:24
  148.5 6.8 %all-to-all-done.5 = f32[8,4,256]{2,1,0:T(4,128)S(1)} async-done(((f32[8,4,256]{2,1,0:T(4,128)}), f32[8,4,256]{2,1,0:T(4,128)S(1)}, u32[]{:S(2)}, u32[]{:S(2)}) %all-to-all-start.5) | async-done | bytes 32800 | tf_op jit(solution)/shard_map/all_to_all | solution.py:24
  156.2 3.3 %all-to-all-start.6 = ((f32[8,4,256]{2,1,0:T(4,128)}), f32[8,4,256]{2,1,0:T(4,128)S(1)}, u32[]{:S(2)}, u32[]{:S(2)}) async-start(f32[8,4,256]{2,1,0:T(4,128)} %broadcast_in_dim.38), calls=%async_computation.6 | async-start | bytes 65536 | tf_op jit(solution)/shard_map/all_to_all | solution.py:24
  159.6 6.8 %all-to-all-done.6 = f32[8,4,256]{2,1,0:T(4,128)S(1)} async-done(((f32[8,4,256]{2,1,0:T(4,128)}), f32[8,4,256]{2,1,0:T(4,128)S(1)}, u32[]{:S(2)}, u32[]{:S(2)}) %all-to-all-start.6) | async-done | bytes 32800 | tf_op jit(solution)/shard_map/all_to_all | solution.py:24
  167.3 3.3 %all-to-all-start.7 = ((f32[8,4,256]{2,1,0:T(4,128)}), f32[8,4,256]{2,1,0:T(4,128)S(1)}, u32[]{:S(2)}, u32[]{:S(2)}) async-start(f32[8,4,256]{2,1,0:T(4,128)} %broadcast_in_dim.39), calls=%async_computation.7 | async-start | bytes 65536 | tf_op jit(solution)/shard_map/all_to_all | solution.py:24
  170.7 6.7 %all-to-all-done.7 = f32[8,4,256]{2,1,0:T(4,128)S(1)} async-done(((f32[8,4,256]{2,1,0:T(4,128)}), f32[8,4,256]{2,1,0:T(4,128)S(1)}, u32[]{:S(2)}, u32[]{:S(2)}) %all-to-all-start.7) | async-done | bytes 32800 | tf_op jit(solution)/shard_map/all_to_all | solution.py:24
  177.7 9.2 %all_to_all.65 = f32[8,4,256]{2,1,0:T(4,128)S(1)} all-to-all(f32[8,4,256]{2,1,0:T(4,128)S(1)} %broadcast_in_dim.40), channel_id=1, replica_groups=mesh['grp'=8,'z'=8,'x'=4,'core'=2] {'z'}, dimensions={0} | all-to-all | bytes 65536 | tf_op jit(solution)/shard_map/all_to_all | solution.py:24
  187.3 9.2 %all_to_all.66 = f32[8,4,256]{2,1,0:T(4,128)S(1)} all-to-all(f32[8,4,256]{2,1,0:T(4,128)S(1)} %broadcast_in_dim.41), channel_id=1, replica_groups=mesh['grp'=8,'z'=8,'x'=4,'core'=2] {'grp'}, dimensions={0} | all-to-all | bytes 65536 | tf_op jit(solution)/shard_map/all_to_all | solution.py:24
  197.3 13.1 %all-to-all-start.10 = ((f32[16,8,256]{2,1,0:T(8,128)}), f32[16,8,256]{2,1,0:T(8,128)S(1)}, u32[]{:S(2)}, u32[]{:S(2)}) async-start(f32[16,8,256]{2,1,0:T(8,128)} %broadcast_in_dim.42), calls=%async_computation.10 | async-start | bytes 262144 | tf_op jit(solution)/shard_map/all_to_all | solution.py:24
  210.4 9.1 %all-to-all-done.10 = f32[16,8,256]{2,1,0:T(8,128)S(1)} async-done(((f32[16,8,256]{2,1,0:T(8,128)}), f32[16,8,256]{2,1,0:T(8,128)S(1)}, u32[]{:S(2)}, u32[]{:S(2)}) %all-to-all-start.10) | async-done | bytes 131104 | tf_op jit(solution)/shard_map/all_to_all | solution.py:24
  219.9 3.9 %collective-permute-start.11 = (f32[8,64]{1,0:T(8,128)S(1)}, f32[8,64]{1,0:T(8,128)S(1)}, u32[]{:S(2)}, u32[]{:S(2)}) collective-permute-start(f32[8,64]{1,0:T(8,128)S(1)} %pad_maximum_fusion.8), channel_id=1, source_target_pairs={{6,0},{0,2},{2,4},{4,6},{7,1},{1,3},{3,5},{5,7},{14,8},{8,10},{10,... | collective-permute-start | bytes 6152 | tf_op jit(solution)/shard_map/ppermute | solution.py:126
  223.9 3.6 %collective-permute-start.10 = (f32[8,64]{1,0:T(8,128)S(1)}, f32[8,64]{1,0:T(8,128)S(1)}, u32[]{:S(2)}, u32[]{:S(2)}) collective-permute-start(f32[8,64]{1,0:T(8,128)S(1)} %pad_maximum_fusion.7), channel_id=1, source_target_pairs={{4,0},{6,2},{0,4},{2,6},{5,1},{7,3},{1,5},{3,7},{12,8},{14,10},{8,... | collective-permute-start | bytes 6152 | tf_op jit(solution)/shard_map/ppermute | solution.py:126
  227.6 3.2 %collective-permute-start.9 = (f32[8,64]{1,0:T(8,128)S(1)}, f32[8,64]{1,0:T(8,128)S(1)}, u32[]{:S(2)}, u32[]{:S(2)}) collective-permute-start(f32[8,64]{1,0:T(8,128)S(1)} %pad_maximum_fusion.6), channel_id=1, source_target_pairs={{2,0},{4,2},{6,4},{0,6},{3,1},{5,3},{7,5},{1,7},{10,8},{12,10},{14... | collective-permute-start | bytes 6152 | tf_op jit(solution)/shard_map/ppermute | solution.py:126
  230.8 1.7 fusion.45
  233.3 3.8 %all-to-all-start.11 = ((f32[16,8,128]{2,1,0:T(8,128)}), f32[16,8,128]{2,1,0:T(8,128)S(1)}, u32[]{:S(2)}, u32[]{:S(2)}) async-start(f32[16,8,128]{2,1,0:T(8,128)} %broadcast_in_dim.43), calls=%async_computation.11 | async-start | bytes 131072 | tf_op jit(solution)/shard_map/all_to_all | solution.py:24
  237.2 7.7 %all-to-all-done.11 = f32[16,8,128]{2,1,0:T(8,128)S(1)} async-done(((f32[16,8,128]{2,1,0:T(8,128)}), f32[16,8,128]{2,1,0:T(8,128)S(1)}, u32[]{:S(2)}, u32[]{:S(2)}) %all-to-all-start.11) | async-done | bytes 65568 | tf_op jit(solution)/shard_map/all_to_all | solution.py:24
  245.6 0.9 fusion.46
  247.3 4.2 %all-to-all-start.12 = ((f32[64,8,128]{2,1,0:T(8,128)}), f32[64,8,128]{2,1,0:T(8,128)S(1)}, u32[]{:S(2)}, u32[]{:S(2)}) async-start(f32[64,8,128]{2,1,0:T(8,128)} %broadcast_in_dim.44), calls=%async_computation.12 | async-start | bytes 524288 | tf_op jit(solution)/shard_map/all_to_all | solution.py:24
  252.4 12.3 %all-to-all-done.12 = f32[64,8,128]{2,1,0:T(8,128)S(1)} async-done(((f32[64,8,128]{2,1,0:T(8,128)}), f32[64,8,128]{2,1,0:T(8,128)S(1)}, u32[]{:S(2)}, u32[]{:S(2)}) %all-to-all-start.12) | async-done | bytes 262176 | tf_op jit(solution)/shard_map/all_to_all | solution.py:24
  266.0 1.4 reshape.98
  (135 shorter events, 20.6 us)
Async XLA Ops:
  0.6 49.8 %copy-start.12 = (f32[32,32]{1,0:T(8,128)S(1)}, f32[32,32]{1,0:T(8,128)}, u32[]{:S(2)}) copy-start(f32[32,32]{1,0:T(8,128)} %param.20) | copy-start | bytes 12292
  2.3 55.9 %collective-permute-start = (f32[3,32,256]{2,1,0:T(8,128)S(1)}, f32[3,32,256]{2,1,0:T(8,128)}, u32[]{:S(2)}, u32[]{:S(2)}) collective-permute-start(f32[3,32,256]{2,1,0:T(8,128)S(1)} %constant_dynamic-update-slice_fusion), channel_id=1, source_target_pairs={{2,0},{4,2},{6,4},{0,6},{3,1},{5,3},{7,5},{1,7},{10,8},{12,10},{14... | collective-permute-start | bytes 294920 | tf_op jit(solution)/shard_map/ppermute | solution.py:126
  7.5 54.0 %collective-permute-start.1 = (f32[3,32,256]{2,1,0:T(8,128)S(1)}, f32[3,32,256]{2,1,0:T(8,128)}, u32[]{:S(2)}, u32[]{:S(2)}) collective-permute-start(f32[3,32,256]{2,1,0:T(8,128)S(1)} %constant_dynamic-update-slice_fusion), channel_id=1, source_target_pairs={{4,0},{6,2},{0,4},{2,6},{5,1},{7,3},{1,5},{3,7},{12,8},{14,10},{8,... | collective-permute-start | bytes 294920 | tf_op jit(solution)/shard_map/ppermute | solution.py:126
  9.9 51.6 %collective-permute-start.2 = (f32[3,32,256]{2,1,0:T(8,128)S(1)}, f32[3,32,256]{2,1,0:T(8,128)}, u32[]{:S(2)}, u32[]{:S(2)}) collective-permute-start(f32[3,32,256]{2,1,0:T(8,128)S(1)} %constant_dynamic-update-slice_fusion), channel_id=1, source_target_pairs={{6,0},{0,2},{2,4},{4,6},{7,1},{1,3},{3,5},{5,7},{14,8},{8,10},{10,... | collective-permute-start | bytes 294920 | tf_op jit(solution)/shard_map/ppermute | solution.py:126
  12.4 73.9 %collective-permute-start.6 = (f32[32,2048]{1,0:T(8,128)}, f32[32,2048]{1,0:T(8,128)S(1)}, u32[]{:S(2)}, u32[]{:S(2)}) collective-permute-start(f32[32,2048]{1,0:T(8,128)} %param.21), channel_id=1, source_target_pairs={{2,0},{4,2},{6,4},{0,6},{3,1},{5,3},{7,5},{1,7},{10,8},{12,10},{14... | collective-permute-start | bytes 786440 | tf_op jit(solution)/shard_map/ppermute | solution.py:126
  16.4 73.2 %collective-permute-start.7 = (f32[32,2048]{1,0:T(8,128)}, f32[32,2048]{1,0:T(8,128)}, u32[]{:S(2)}, u32[]{:S(2)}) collective-permute-start(f32[32,2048]{1,0:T(8,128)} %param.21), channel_id=1, source_target_pairs={{4,0},{6,2},{0,4},{2,6},{5,1},{7,3},{1,5},{3,7},{12,8},{14,10},{8,... | collective-permute-start | bytes 786440 | tf_op jit(solution)/shard_map/ppermute | solution.py:126
  22.8 27.5 %all-to-all-start = ((f32[64,8,128]{2,1,0:T(8,128)}), f32[64,8,128]{2,1,0:T(8,128)S(1)}, u32[]{:S(2)}, u32[]{:S(2)}) async-start(f32[64,8,128]{2,1,0:T(8,128)} %get-tuple-element.29), calls=%async_computation | async-start | bytes 524288 | tf_op jit(solution)/shard_map/all_to_all | solution.py:24
  51.8 6.4 %copy-start.11 = (f32[32,2,32]{2,1,0:T(2,128)S(1)}, f32[32,2,32]{2,1,0:T(2,128)}, u32[]{:S(2)}) copy-start(f32[32,2,32]{2,1,0:T(2,128)} %param.23) | copy-start | bytes 24580
  52.5 18.9 %copy-start = (f32[32,4096]{1,0:T(8,128)S(1)}, f32[32,4096]{1,0:T(8,128)}, u32[]{:S(2)}) copy-start(f32[32,4096]{1,0:T(8,128)} %param.22) | copy-start | bytes 1572868
  53.4 17.9 %all-to-all-start.1 = ((f32[64,8,128]{2,1,0:T(8,128)}), f32[64,8,128]{2,1,0:T(8,128)S(1)}, u32[]{:S(2)}, u32[]{:S(2)}) async-start(f32[64,8,128]{2,1,0:T(8,128)} %copy.65), calls=%async_computation.1 | async-start | bytes 524288 | tf_op jit(solution)/shard_map/all_to_all | solution.py:24
  58.2 31.4 %collective-permute-start.8 = (f32[32,2048]{1,0:T(8,128)}, f32[32,2048]{1,0:T(8,128)}, u32[]{:S(2)}, u32[]{:S(2)}) collective-permute-start(f32[32,2048]{1,0:T(8,128)} %param.21), channel_id=1, source_target_pairs={{6,0},{0,2},{2,4},{4,6},{7,1},{1,3},{3,5},{5,7},{14,8},{8,10},{10,... | collective-permute-start | bytes 786440 | tf_op jit(solution)/shard_map/ppermute | solution.py:126
  73.9 42.3 %all-to-all-start.2 = ((f32[64,8,256]{2,1,0:T(8,128)}), f32[64,8,256]{2,1,0:T(8,128)S(1)}, u32[]{:S(2)}, u32[]{:S(2)}) async-start(f32[64,8,256]{2,1,0:T(8,128)} %copy.70), calls=%async_computation.2 | async-start | bytes 1048576 | tf_op jit(solution)/shard_map/all_to_all | solution.py:24
  78.7 35.7 %collective-permute-start.5 = (f32[32,4224]{1,0:T(8,128)S(1)}, f32[32,4224]{1,0:T(8,128)S(1)}, u32[]{:S(2)}, u32[]{:S(2)}) collective-permute-start(f32[32,4224]{1,0:T(8,128)S(1)} %pad_maximum_fusion.2), channel_id=1, source_target_pairs={{6,0},{0,2},{2,4},{4,6},{7,1},{1,3},{3,5},{5,7},{14,8},{8,10},{10,... | collective-permute-start | bytes 1622024 | tf_op jit(solution)/shard_map/ppermute | solution.py:126
  82.0 31.6 %collective-permute-start.4 = (f32[32,4224]{1,0:T(8,128)S(1)}, f32[32,4224]{1,0:T(8,128)S(1)}, u32[]{:S(2)}, u32[]{:S(2)}) collective-permute-start(f32[32,4224]{1,0:T(8,128)S(1)} %pad_maximum_fusion.2), channel_id=1, source_target_pairs={{4,0},{6,2},{0,4},{2,6},{5,1},{7,3},{1,5},{3,7},{12,8},{14,10},{8,... | collective-permute-start | bytes 1622024 | tf_op jit(solution)/shard_map/ppermute | solution.py:126
  86.3 3.2 %copy-start.9 = (f32[32,2048]{1,0:T(8,128)}, f32[32,2048]{1,0:T(8,128)S(1)}, u32[]{:S(2)}) copy-start(f32[32,2048]{1,0:T(8,128)S(1)} %collective-permute-done.6) | copy-start | bytes 786436
  86.3 26.3 %collective-permute-start.3 = (f32[32,4224]{1,0:T(8,128)S(1)}, f32[32,4224]{1,0:T(8,128)S(1)}, u32[]{:S(2)}, u32[]{:S(2)}) collective-permute-start(f32[32,4224]{1,0:T(8,128)S(1)} %pad_maximum_fusion.2), channel_id=1, source_target_pairs={{2,0},{4,2},{6,4},{0,6},{3,1},{5,3},{7,5},{1,7},{10,8},{12,10},{14... | collective-permute-start | bytes 1622024 | tf_op jit(solution)/shard_map/ppermute | solution.py:126
  112.7 1.8 copy-start.4
  113.6 1.0 copy-start.3
  114.5 0.8 copy-start.2
  116.9 14.0 %all-to-all-start.3 = ((f32[8,8,256]{2,1,0:T(8,128)}), f32[8,8,256]{2,1,0:T(8,128)S(1)}, u32[]{:S(2)}, u32[]{:S(2)}) async-start(f32[8,8,256]{2,1,0:T(8,128)} %broadcast_in_dim.35), calls=%async_computation.3 | async-start | bytes 131072 | tf_op jit(solution)/shard_map/all_to_all | solution.py:24
  123.7 13.6 %slice-start = ((f32[32,4224]{1,0:T(8,128)}), f32[32,128]{1,0:T(8,128)S(1)}, s32[]{:S(2)}) async-start(f32[32,4224]{1,0:T(8,128)} %copy-done.2), calls=%async_computation.13 | async-start | bytes 32768 | tf_op jit(solution)/shard_map/slice | solution.py:188
  123.7 24.8 %slice-start.1 = ((f32[32,4224]{1,0:T(8,128)}), f32[32,128]{1,0:T(8,128)S(1)}, s32[]{:S(2)}) async-start(f32[32,4224]{1,0:T(8,128)} %copy-done.3), calls=%async_computation.14 | async-start | bytes 32768 | tf_op jit(solution)/shard_map/slice | solution.py:188
  123.7 35.8 %slice-start.2 = ((f32[32,4224]{1,0:T(8,128)}), f32[32,128]{1,0:T(8,128)S(1)}, s32[]{:S(2)}) async-start(f32[32,4224]{1,0:T(8,128)} %copy-done.4), calls=%async_computation.15 | async-start | bytes 32768 | tf_op jit(solution)/shard_map/slice | solution.py:188
  125.3 85.1 %copy-start.13 = (s32[2]{0:T(128)S(1)}, s32[2]{0:T(128)}, u32[]{:S(2)}) copy-start(s32[2]{0:T(128)} %parents.1) | copy-start | bytes 28
  131.9 12.3 %all-to-all-start.4 = ((f32[8,4,256]{2,1,0:T(4,128)}), f32[8,4,256]{2,1,0:T(4,128)S(1)}, u32[]{:S(2)}, u32[]{:S(2)}) async-start(f32[8,4,256]{2,1,0:T(4,128)} %broadcast_in_dim.36), calls=%async_computation.4 | async-start | bytes 65536 | tf_op jit(solution)/shard_map/all_to_all | solution.py:24
  145.2 10.1 %all-to-all-start.5 = ((f32[8,4,256]{2,1,0:T(4,128)}), f32[8,4,256]{2,1,0:T(4,128)S(1)}, u32[]{:S(2)}, u32[]{:S(2)}) async-start(f32[8,4,256]{2,1,0:T(4,128)} %broadcast_in_dim.37), calls=%async_computation.5 | async-start | bytes 65536 | tf_op jit(solution)/shard_map/all_to_all | solution.py:24
  156.2 10.1 %all-to-all-start.6 = ((f32[8,4,256]{2,1,0:T(4,128)}), f32[8,4,256]{2,1,0:T(4,128)S(1)}, u32[]{:S(2)}, u32[]{:S(2)}) async-start(f32[8,4,256]{2,1,0:T(4,128)} %broadcast_in_dim.38), calls=%async_computation.6 | async-start | bytes 65536 | tf_op jit(solution)/shard_map/all_to_all | solution.py:24
  167.3 10.1 %all-to-all-start.7 = ((f32[8,4,256]{2,1,0:T(4,128)}), f32[8,4,256]{2,1,0:T(4,128)S(1)}, u32[]{:S(2)}, u32[]{:S(2)}) async-start(f32[8,4,256]{2,1,0:T(4,128)} %broadcast_in_dim.39), calls=%async_computation.7 | async-start | bytes 65536 | tf_op jit(solution)/shard_map/all_to_all | solution.py:24
  197.3 22.3 %all-to-all-start.10 = ((f32[16,8,256]{2,1,0:T(8,128)}), f32[16,8,256]{2,1,0:T(8,128)S(1)}, u32[]{:S(2)}, u32[]{:S(2)}) async-start(f32[16,8,256]{2,1,0:T(8,128)} %broadcast_in_dim.42), calls=%async_computation.10 | async-start | bytes 262144 | tf_op jit(solution)/shard_map/all_to_all | solution.py:24
  219.6 26.0 %copy-start.1 = (f32[128,2048]{1,0:T(8,128)S(1)}, f32[128,2048]{1,0:T(8,128)}, u32[]{:S(2)}) copy-start(f32[128,2048]{1,0:T(8,128)} %pad_maximum_fusion.1) | copy-start | bytes 3145732
  219.9 17.2 %collective-permute-start.11 = (f32[8,64]{1,0:T(8,128)S(1)}, f32[8,64]{1,0:T(8,128)S(1)}, u32[]{:S(2)}, u32[]{:S(2)}) collective-permute-start(f32[8,64]{1,0:T(8,128)S(1)} %pad_maximum_fusion.8), channel_id=1, source_target_pairs={{6,0},{0,2},{2,4},{4,6},{7,1},{1,3},{3,5},{5,7},{14,8},{8,10},{10,... | collective-permute-start | bytes 6152 | tf_op jit(solution)/shard_map/ppermute | solution.py:126
  223.9 13.2 %collective-permute-start.10 = (f32[8,64]{1,0:T(8,128)S(1)}, f32[8,64]{1,0:T(8,128)S(1)}, u32[]{:S(2)}, u32[]{:S(2)}) collective-permute-start(f32[8,64]{1,0:T(8,128)S(1)} %pad_maximum_fusion.7), channel_id=1, source_target_pairs={{4,0},{6,2},{0,4},{2,6},{5,1},{7,3},{1,5},{3,7},{12,8},{14,10},{8,... | collective-permute-start | bytes 6152 | tf_op jit(solution)/shard_map/ppermute | solution.py:126
  227.6 9.5 %collective-permute-start.9 = (f32[8,64]{1,0:T(8,128)S(1)}, f32[8,64]{1,0:T(8,128)S(1)}, u32[]{:S(2)}, u32[]{:S(2)}) collective-permute-start(f32[8,64]{1,0:T(8,128)S(1)} %pad_maximum_fusion.6), channel_id=1, source_target_pairs={{2,0},{4,2},{6,4},{0,6},{3,1},{5,3},{7,5},{1,7},{10,8},{12,10},{14... | collective-permute-start | bytes 6152 | tf_op jit(solution)/shard_map/ppermute | solution.py:126
  233.3 11.6 %all-to-all-start.11 = ((f32[16,8,128]{2,1,0:T(8,128)}), f32[16,8,128]{2,1,0:T(8,128)S(1)}, u32[]{:S(2)}, u32[]{:S(2)}) async-start(f32[16,8,128]{2,1,0:T(8,128)} %broadcast_in_dim.43), calls=%async_computation.11 | async-start | bytes 131072 | tf_op jit(solution)/shard_map/all_to_all | solution.py:24
  247.3 17.4 %all-to-all-start.12 = ((f32[64,8,128]{2,1,0:T(8,128)}), f32[64,8,128]{2,1,0:T(8,128)S(1)}, u32[]{:S(2)}, u32[]{:S(2)}) async-start(f32[64,8,128]{2,1,0:T(8,128)} %broadcast_in_dim.44), calls=%async_computation.12 | async-start | bytes 524288 | tf_op jit(solution)/shard_map/all_to_all | solution.py:24
  252.4 15.0 %copy-start.5 = (f32[2,128,128]{2,1,0:T(8,128)S(1)}, f32[2,128,128]{2,1,0:T(8,128)}, u32[]{:S(2)}) copy-start(f32[2,128,128]{2,1,0:T(8,128)} %front.1) | copy-start | bytes 393220
  252.4 15.0 %copy-start.10 = (f32[32,256]{1,0:T(8,128)S(1)}, f32[32,256]{1,0:T(8,128)}, u32[]{:S(2)}) copy-start(f32[32,256]{1,0:T(8,128)} %get-tuple-element.28) | copy-start | bytes 98308
  265.2 2.7 %copy-start.6 = (f32[2,128,128]{2,1,0:T(8,128)S(1)}, f32[2,128,128]{2,1,0:T(8,128)}, u32[]{:S(2)}) copy-start(f32[2,128,128]{2,1,0:T(8,128)} %inverse.1) | copy-start | bytes 393220
  265.2 3.0 %copy-start.8 = (f32[2,128,128]{2,1,0:T(8,128)S(1)}, f32[2,128,128]{2,1,0:T(8,128)}, u32[]{:S(2)}) copy-start(f32[2,128,128]{2,1,0:T(8,128)} %link.1) | copy-start | bytes 393220
  267.4 1.9 copy-start.7

commit v11 on v10

--- a/solution.py
+++ b/solution.py
@@ -64,6 +64,53 @@
             chunks[spot] = chunks[spot] + made
 
 
+def leaf_backward(parents, targets, live, parts, solved, inverse, link, front, leaf, fronts):
+    rows, width = solved.shape[0], inverse.shape[1]
+    n_z, n_x, _, tall, span = parts.shape
+    share = span // n_x
+    lane = lax.broadcasted_iota(jnp.int32, (n_z * n_x * tall, span), 1)
+    for half in range(2):
+        made = jnp.zeros((n_z * n_x * tall, span), jnp.float32)
+        for piece in range(4):
+            source = half * 2 + piece // 2
+            moved = parts[:, :, piece % 2].reshape(n_z * n_x * tall, span)
+            move = (piece - source) * share % span
+            moved = pltpu.roll(moved, move, 1) if move else moved
+            inside = (lane >= piece * share) & (lane < (piece + 1) * share)
+            made = jnp.where(inside, moved, made)
+        made = made.reshape(n_z, n_x * tall, span)
+        for z in range(n_z):
+            fronts[:, (2 * z + half) * width : (2 * z + half + 1) * width] = made[z]
+    alive = jnp.full((rows, width), live[0], jnp.int32)
+    base = []
+    for block in range(2):
+        spot = pl.multiple_of(targets[block] * width, width)
+        picked = fronts[:, pl.ds(spot, width)]
+        base.append(solved[:, block * width : (block + 1) * width] - mmt(picked, front[block]))
+    second = jnp.where(alive > 1, mmt(base[1], inverse[1]), 0.0)
+    carried = jnp.where(alive > parents[0], mmt(second, link[0]), 0.0)
+    leaf[:, :width] = jnp.where(alive > 0, mmt(base[0] - carried, inverse[0]), 0.0)
+    leaf[:, width:] = second
+
+
+def leaf_end(parents, targets, live, parts, solved, inverse, link, front, front_order):
+    rows, span = solved.shape
+    outs = (
+        jax.ShapeDtypeStruct((rows, span), jnp.float32),
+        jax.ShapeDtypeStruct((rows, front_order), jnp.float32),
+    )
+    scalars, arrays = (parents, targets, live), (parts, solved, inverse, link, front)
+    specs = [whole_block(item, pltpu.SMEM) for item in scalars]
+    specs += [whole_block(item) for item in arrays]
+    return pl.pallas_call(
+        leaf_backward,
+        grid=(1,),
+        in_specs=specs,
+        out_specs=tuple(whole_block(item) for item in outs),
+        out_shape=outs,
+    )(*scalars, *arrays)
+
+
 def whole_block(array, space=None):
     zeros = (0,) * array.ndim
     if space is not None:
@@ -116,7 +163,6 @@
         share = front_inverse.shape[0]
         part = root_inverse.shape[2]
         few = rows // n_near
-        live = live_blocks[0]
         my_dev = lax.axis_index(DEV)
         my_z, my_x, my_core = (lax.axis_index(name) for name in DEV)
         some = rows // n_x
@@ -145,23 +191,20 @@
             chunks = natural.reshape(4, rows // 4, n_dev, share).transpose(2, 1, 0, 3)
             return unfold(jnp.sum(swap(chunks.reshape(n_dev, rows // 4, 4 * share), DEV), 0), 4)
 
-        has_parent = parents[0] < live
         solved, placed = leaf_start(
             parents, front_rows, live_blocks, leaf_right, leaf_inverse, leaf_link, leaf_front, n_dev
         )
-        solved0, solved1 = solved[:, :width], solved[:, width:]
         behind = (n_x - my_x) % n_x
         spots = [my_x * (n_core * share), my_x * some]
         spots += [behind * size for size in (n_core * share, share, some)]
         for step in range(n_x):
             spot = my_z * part + (my_x + n_x - step) % n_x * (n_core * share) + my_core * share
             spots += [spot, spot + front_order]
-        spots += [front_rows[block] * width for block in range(2)]
         spots = tuple(spot.astype(jnp.uint32) for spot in spots)
         start = front_right - unfold(jnp.sum(swap(placed, DEV), 0), 4)
         start, spots = lax.optimization_barrier((start, spots))
         ahead_part, rows_x, back_part, back_share, back_rows = spots[:5]
-        root_spots, leaf_spots = spots[5:-2], spots[-2:]
+        root_spots = spots[5:]
         y_own = dev_sum(mm(start, front_inverse))
         side = jnp.pad(y_own, ((0, 0), (0, width - share)))
         couples = from_all(jnp.concatenate([front_couple, side], 1))
@@ -201,30 +244,20 @@
         rest = spread(rest, LINE, n_line)
         rest = rest.reshape(n_z, n_core, some, n_x, share).transpose(2, 0, 3, 1, 4)
         found = turn(mmt(rest.reshape(some, front_order), inverse), 1, back_share)
-        found = spread(found, DEV, n_dev).reshape(n_z, n_x, n_core, some, n_x, share)
-        front_solution = found.transpose(1, 3, 0, 4, 2, 5).reshape(rows, front_order)
-        root = [
-            jnp.concatenate(
-                [
-                    lax.dynamic_slice_in_dim(whole, spot, share, 1)
-                    for spot in root_spots[2 * step : 2 * step + 2]
-                ],
-                1,
-            )
-            for step in range(n_x)
-        ]
-        root = [root[0]] + [from_right(root[step], step) for step in range(1, n_x)]
+        found = spread(found, DEV, n_dev).reshape(n_z, n_x, n_core, some, n_x * share)
+        root = []
+        early = lax.optimization_barrier(whole)
+        for step in range(n_x):
+            cuts = root_spots[2 * step : 2 * step + 2]
+            cuts = [lax.dynamic_slice_in_dim(early if step in (1, 3) else whole, spot, share, 1) for spot in cuts]
+            cuts = jnp.concatenate(cuts, 1)
+            root.append(from_right(cuts, step) if step else cuts)
         root = turn(jnp.concatenate(root, 0), 0, back_rows).reshape(rows, 2, share)
 
-        def back(solved, block):
-            picked = lax.dynamic_slice_in_dim(front_solution, leaf_spots[block], width, 1)
-            return solved - mmt(picked, leaf_front[block])
-
-        base0, base1 = back(solved0, 0), back(solved1, 1)
-        leaf1 = jnp.where(live > 1, mmt(base1, leaf_inverse[1]), 0.0)
-        carried = jnp.where(has_parent, mmt(leaf1, leaf_link[0]), 0.0)
-        leaf0 = jnp.where(live > 0, mmt(base0 - carried, leaf_inverse[0]), 0.0)
-        leaf_solution = jnp.concatenate([leaf0, leaf1], 1)
+        leaf_solution, front_solution = leaf_end(
+            parents, front_rows, live_blocks, found, solved, leaf_inverse, leaf_link, leaf_front,
+            front_order,
+        )
         return leaf_solution, front_solution, root
 
     return body

time: 271 us -> 269 us (level)
  blocking collectives: 21.2 us -> 42.5 us
  starting transfers between devices: 109 us -> 96.1 us
  waiting for transfers between devices: 98.9 us -> 92.3 us
  local copies, waits for them, and re-layouts: 19.8 us -> 15.9 us
  Pallas kernels: 2.63 us -> 5.91 us
    all_to_all x2 -> x3, blocking collectives: 18.5 us -> 39.9 us  [swap(): return lax.all_to_all(chunks, axes, 0, 0, tiled=True)]
    all_to_all x11 -> x10, starting transfers between devices: 67.3 us -> 54.2 us  [swap(): return lax.all_to_all(chunks, axes, 0, 0, tiled=True)]
    all_to_all x11 -> x10, waiting for transfers between devices: 78.1 us -> 71.5 us  [swap(): return lax.all_to_all(chunks, axes, 0, 0, tiled=True)]
    pallas_call x0 -> x1, Pallas kernels: none -> 3.28 us  [leaf_end(): pl.pallas_call(leaf_backward, grid=(1,), in_specs=specs, out_specs=tuple(...]
  transfers between devices with their start and end apart: 23 -> 22, of which waited for: 11 -> 10; matrix products, arithmetic and copies ran while one was open for 7% -> 6% of each run, Pallas kernels for 1% -> 1%
where the time goes in v11:
time: 269 us; the launch traced here: 267 us
  starting transfers between devices  96.1 us (36%)
  waiting for transfers between devices  92.3 us (34%)
  blocking collectives  42.5 us (16%)
  local copies, waits for them, and re-layouts  15.9 us (6%)
  other arithmetic  6.33 us (2%)
  matrix products  6.16 us (2%)
  Pallas kernels  5.91 us (2%)
    all_to_all x10, waiting for transfers between devices, swap(): return lax.all_to_all(chunks, axes, 0, 0, tiled=True)  71.5 us
    all_to_all x10, starting transfers between devices, swap(): return lax.all_to_all(chunks, axes, 0, 0, tiled=True)  54.2 us
    ppermute x12, starting transfers between devices, from_right(): return lax.ppermute(values, 'x', pairs)  41.9 us
    all_to_all x3, blocking collectives, swap(): return lax.all_to_all(chunks, axes, 0, 0, tiled=True)  39.9 us
    ppermute x12, waiting for transfers between devices, from_right(): return lax.ppermute(values, 'x', pairs)  20.8 us
  transfers between devices with their start and end apart: 22, of which 10 were waited for; matrix products, arithmetic and copies ran while one was open for 6% of the time, Pallas kernels for 1%

profile of v11, /device:TPU:1, one launch (start us, length us, event | category | flops | bytes accessed | tf_op | source)
XLA Modules:
  0.0 267.2 jit_solution(18041590749481127157)
XLA Ops:
  2.3 5.2 %collective-permute-start = (f32[3,32,256]{2,1,0:T(8,128)S(1)}, f32[3,32,256]{2,1,0:T(8,128)}, u32[]{:S(2)}, u32[]{:S(2)}) collective-permute-start(f32[3,32,256]{2,1,0:T(8,128)S(1)} %constant_dynamic-update-slice_fusion), channel_id=1, source_target_pairs={{2,0},{4,2},{6,4},{0,6},{3,1},{5,3},{7,5},{1,7},{10,8},{12,10},{14... | collective-permute-start | bytes 294920 | tf_op jit(solution)/shard_map/ppermute | solution.py:172
  7.5 2.4 collective-permute-start.1
  9.9 2.5 collective-permute-start.2
  12.4 4.0 %collective-permute-start.6 = (f32[32,2048]{1,0:T(8,128)}, f32[32,2048]{1,0:T(8,128)S(1)}, u32[]{:S(2)}, u32[]{:S(2)}) collective-permute-start(f32[32,2048]{1,0:T(8,128)} %param.21), channel_id=1, source_target_pairs={{2,0},{4,2},{6,4},{0,6},{3,1},{5,3},{7,5},{1,7},{10,8},{12,10},{14... | collective-permute-start | bytes 786440 | tf_op jit(solution)/shard_map/ppermute | solution.py:172
  16.4 3.2 %collective-permute-start.7 = (f32[32,2048]{1,0:T(8,128)}, f32[32,2048]{1,0:T(8,128)}, u32[]{:S(2)}, u32[]{:S(2)}) collective-permute-start(f32[32,2048]{1,0:T(8,128)} %param.21), channel_id=1, source_target_pairs={{4,0},{6,2},{0,4},{2,6},{5,1},{7,3},{1,5},{3,7},{12,8},{14,10},{8,... | collective-permute-start | bytes 786440 | tf_op jit(solution)/shard_map/ppermute | solution.py:172
  20.2 2.6 shard_map.148
  22.8 14.4 %all-to-all-start = ((f32[64,8,128]{2,1,0:T(8,128)}), f32[64,8,128]{2,1,0:T(8,128)S(1)}, u32[]{:S(2)}, u32[]{:S(2)}) async-start(f32[64,8,128]{2,1,0:T(8,128)} %get-tuple-element.28), calls=%async_computation | async-start | bytes 524288 | tf_op jit(solution)/shard_map/all_to_all | solution.py:24
  37.6 12.7 %all-to-all-done = f32[64,8,128]{2,1,0:T(8,128)S(1)} async-done(((f32[64,8,128]{2,1,0:T(8,128)}), f32[64,8,128]{2,1,0:T(8,128)S(1)}, u32[]{:S(2)}, u32[]{:S(2)}) %all-to-all-start) | async-done | bytes 262176 | tf_op jit(solution)/shard_map/all_to_all | solution.py:24
  50.5 1.3 fusion.25
  52.5 0.9 copy.62
  53.4 4.8 %all-to-all-start.1 = ((f32[64,8,128]{2,1,0:T(8,128)}), f32[64,8,128]{2,1,0:T(8,128)S(1)}, u32[]{:S(2)}, u32[]{:S(2)}) async-start(f32[64,8,128]{2,1,0:T(8,128)} %copy.62), calls=%async_computation.1 | async-start | bytes 524288 | tf_op jit(solution)/shard_map/all_to_all | solution.py:24
  58.2 3.3 %collective-permute-start.8 = (f32[32,2048]{1,0:T(8,128)}, f32[32,2048]{1,0:T(8,128)}, u32[]{:S(2)}, u32[]{:S(2)}) collective-permute-start(f32[32,2048]{1,0:T(8,128)} %param.21), channel_id=1, source_target_pairs={{6,0},{0,2},{2,4},{4,6},{7,1},{1,3},{3,5},{5,7},{14,8},{8,10},{10,... | collective-permute-start | bytes 786440 | tf_op jit(solution)/shard_map/ppermute | solution.py:172
  61.5 1.0 pad_maximum_fusion.3
  62.5 2.7 all-gather
  65.2 6.0 %all-to-all-done.1 = f32[64,8,128]{2,1,0:T(8,128)S(1)} async-done(((f32[64,8,128]{2,1,0:T(8,128)}), f32[64,8,128]{2,1,0:T(8,128)S(1)}, u32[]{:S(2)}, u32[]{:S(2)}) %all-to-all-start.1) | async-done | bytes 262176 | tf_op jit(solution)/shard_map/all_to_all | solution.py:24
  71.4 0.9 fusion
  72.8 1.1 copy.67
  73.9 4.8 %all-to-all-start.2 = ((f32[64,8,256]{2,1,0:T(8,128)}), f32[64,8,256]{2,1,0:T(8,128)S(1)}, u32[]{:S(2)}, u32[]{:S(2)}) async-start(f32[64,8,256]{2,1,0:T(8,128)} %copy.67), calls=%async_computation.2 | async-start | bytes 1048576 | tf_op jit(solution)/shard_map/all_to_all | solution.py:24
  78.7 3.3 %collective-permute-start.5 = (f32[32,4224]{1,0:T(8,128)S(1)}, f32[32,4224]{1,0:T(8,128)S(1)}, u32[]{:S(2)}, u32[]{:S(2)}) collective-permute-start(f32[32,4224]{1,0:T(8,128)S(1)} %pad_maximum_fusion.2), channel_id=1, source_target_pairs={{6,0},{0,2},{2,4},{4,6},{7,1},{1,3},{3,5},{5,7},{14,8},{8,10},{10,... | collective-permute-start | bytes 1622024 | tf_op jit(solution)/shard_map/ppermute | solution.py:172
  82.0 4.3 %collective-permute-start.4 = (f32[32,4224]{1,0:T(8,128)S(1)}, f32[32,4224]{1,0:T(8,128)S(1)}, u32[]{:S(2)}, u32[]{:S(2)}) collective-permute-start(f32[32,4224]{1,0:T(8,128)S(1)} %pad_maximum_fusion.2), channel_id=1, source_target_pairs={{4,0},{6,2},{0,4},{2,6},{5,1},{7,3},{1,5},{3,7},{12,8},{14,10},{8,... | collective-permute-start | bytes 1622024 | tf_op jit(solution)/shard_map/ppermute | solution.py:172
  86.3 3.1 %collective-permute-start.3 = (f32[32,4224]{1,0:T(8,128)S(1)}, f32[32,4224]{1,0:T(8,128)S(1)}, u32[]{:S(2)}, u32[]{:S(2)}) collective-permute-start(f32[32,4224]{1,0:T(8,128)S(1)} %pad_maximum_fusion.2), channel_id=1, source_target_pairs={{2,0},{4,2},{6,4},{0,6},{3,1},{5,3},{7,5},{1,7},{10,8},{12,10},{14... | collective-permute-start | bytes 1622024 | tf_op jit(solution)/shard_map/ppermute | solution.py:172
  89.6 2.3 pad_maximum_fusion.1
  91.9 20.8 %collective-permute-done.3 = f32[32,4224]{1,0:T(8,128)S(1)} collective-permute-done((f32[32,4224]{1,0:T(8,128)S(1)}, f32[32,4224]{1,0:T(8,128)S(1)}, u32[]{:S(2)}, u32[]{:S(2)}) %collective-permute-start.3) | collective-permute-done | bytes 540704 | tf_op jit(solution)/shard_map/ppermute | solution.py:172
  112.7 0.9 slice.73
  116.9 6.8 %all-to-all-start.3 = ((f32[8,8,256]{2,1,0:T(8,128)}), f32[8,8,256]{2,1,0:T(8,128)S(1)}, u32[]{:S(2)}, u32[]{:S(2)}) async-start(f32[8,8,256]{2,1,0:T(8,128)} %broadcast_in_dim.30), calls=%async_computation.3 | async-start | bytes 131072 | tf_op jit(solution)/shard_map/all_to_all | solution.py:24
  123.7 1.5 pad_maximum_fusion
  125.3 5.7 %all-to-all-done.3 = f32[8,8,256]{2,1,0:T(8,128)S(1)} async-done(((f32[8,8,256]{2,1,0:T(8,128)}), f32[8,8,256]{2,1,0:T(8,128)S(1)}, u32[]{:S(2)}, u32[]{:S(2)}) %all-to-all-start.3) | async-done | bytes 65568 | tf_op jit(solution)/shard_map/all_to_all | solution.py:24
  131.9 5.4 %all-to-all-start.4 = ((f32[8,4,256]{2,1,0:T(4,128)}), f32[8,4,256]{2,1,0:T(4,128)S(1)}, u32[]{:S(2)}, u32[]{:S(2)}) async-start(f32[8,4,256]{2,1,0:T(4,128)} %broadcast_in_dim.31), calls=%async_computation.4 | async-start | bytes 65536 | tf_op jit(solution)/shard_map/all_to_all | solution.py:24
  137.3 6.9 %all-to-all-done.4 = f32[8,4,256]{2,1,0:T(4,128)S(1)} async-done(((f32[8,4,256]{2,1,0:T(4,128)}), f32[8,4,256]{2,1,0:T(4,128)S(1)}, u32[]{:S(2)}, u32[]{:S(2)}) %all-to-all-start.4) | async-done | bytes 32800 | tf_op jit(solution)/shard_map/all_to_all | solution.py:24
  145.1 3.3 %all-to-all-start.5 = ((f32[8,4,256]{2,1,0:T(4,128)}), f32[8,4,256]{2,1,0:T(4,128)S(1)}, u32[]{:S(2)}, u32[]{:S(2)}) async-start(f32[8,4,256]{2,1,0:T(4,128)} %broadcast_in_dim.32), calls=%async_computation.5 | async-start | bytes 65536 | tf_op jit(solution)/shard_map/all_to_all | solution.py:24
  148.5 6.8 %all-to-all-done.5 = f32[8,4,256]{2,1,0:T(4,128)S(1)} async-done(((f32[8,4,256]{2,1,0:T(4,128)}), f32[8,4,256]{2,1,0:T(4,128)S(1)}, u32[]{:S(2)}, u32[]{:S(2)}) %all-to-all-start.5) | async-done | bytes 32800 | tf_op jit(solution)/shard_map/all_to_all | solution.py:24
  156.2 3.3 %all-to-all-start.6 = ((f32[8,4,256]{2,1,0:T(4,128)}), f32[8,4,256]{2,1,0:T(4,128)S(1)}, u32[]{:S(2)}, u32[]{:S(2)}) async-start(f32[8,4,256]{2,1,0:T(4,128)} %broadcast_in_dim.33), calls=%async_computation.6 | async-start | bytes 65536 | tf_op jit(solution)/shard_map/all_to_all | solution.py:24
  159.5 6.8 %all-to-all-done.6 = f32[8,4,256]{2,1,0:T(4,128)S(1)} async-done(((f32[8,4,256]{2,1,0:T(4,128)}), f32[8,4,256]{2,1,0:T(4,128)S(1)}, u32[]{:S(2)}, u32[]{:S(2)}) %all-to-all-start.6) | async-done | bytes 32800 | tf_op jit(solution)/shard_map/all_to_all | solution.py:24
  167.3 3.3 %all-to-all-start.7 = ((f32[8,4,256]{2,1,0:T(4,128)}), f32[8,4,256]{2,1,0:T(4,128)S(1)}, u32[]{:S(2)}, u32[]{:S(2)}) async-start(f32[8,4,256]{2,1,0:T(4,128)} %broadcast_in_dim.34), calls=%async_computation.7 | async-start | bytes 65536 | tf_op jit(solution)/shard_map/all_to_all | solution.py:24
  170.7 6.7 %all-to-all-done.7 = f32[8,4,256]{2,1,0:T(4,128)S(1)} async-done(((f32[8,4,256]{2,1,0:T(4,128)}), f32[8,4,256]{2,1,0:T(4,128)S(1)}, u32[]{:S(2)}, u32[]{:S(2)}) %all-to-all-start.7) | async-done | bytes 32800 | tf_op jit(solution)/shard_map/all_to_all | solution.py:24
  177.7 9.2 %all_to_all.65 = f32[8,4,256]{2,1,0:T(4,128)S(1)} all-to-all(f32[8,4,256]{2,1,0:T(4,128)S(1)} %broadcast_in_dim.35), channel_id=1, replica_groups=mesh['grp'=8,'z'=8,'x'=4,'core'=2] {'z'}, dimensions={0} | all-to-all | bytes 65536 | tf_op jit(solution)/shard_map/all_to_all | solution.py:24
  187.3 9.2 %all_to_all.66 = f32[8,4,256]{2,1,0:T(4,128)S(1)} all-to-all(f32[8,4,256]{2,1,0:T(4,128)S(1)} %broadcast_in_dim.36), channel_id=1, replica_groups=mesh['grp'=8,'z'=8,'x'=4,'core'=2] {'grp'}, dimensions={0} | all-to-all | bytes 65536 | tf_op jit(solution)/shard_map/all_to_all | solution.py:24
  196.6 21.4 %all_to_all.67 = f32[16,8,256]{2,1,0:T(8,128)S(1)} all-to-all(f32[16,8,256]{2,1,0:T(8,128)S(1)} %broadcast_in_dim.37), channel_id=1, replica_groups=mesh['grp'=8,'z'=8,'x'=4,'core'=2] {'z','core'}, dimensions={0} | all-to-all | bytes 262144 | tf_op jit(solution)/shard_map/all_to_all | solution.py:24
  218.4 3.9 %collective-permute-start.11 = (f32[8,64]{1,0:T(8,128)S(1)}, f32[8,64]{1,0:T(8,128)S(1)}, u32[]{:S(2)}, u32[]{:S(2)}) collective-permute-start(f32[8,64]{1,0:T(8,128)S(1)} %pad_maximum_fusion.7), channel_id=1, source_target_pairs={{6,0},{0,2},{2,4},{4,6},{7,1},{1,3},{3,5},{5,7},{14,8},{8,10},{10,... | collective-permute-start | bytes 6152 | tf_op jit(solution)/shard_map/ppermute | solution.py:172
  222.5 3.6 %collective-permute-start.10 = (f32[8,64]{1,0:T(8,128)S(1)}, f32[8,64]{1,0:T(8,128)S(1)}, u32[]{:S(2)}, u32[]{:S(2)}) collective-permute-start(f32[8,64]{1,0:T(8,128)S(1)} %pad_maximum_fusion.6), channel_id=1, source_target_pairs={{4,0},{6,2},{0,4},{2,6},{5,1},{7,3},{1,5},{3,7},{12,8},{14,10},{8,... | collective-permute-start | bytes 6152 | tf_op jit(solution)/shard_map/ppermute | solution.py:172
  226.1 3.2 %collective-permute-start.9 = (f32[8,64]{1,0:T(8,128)S(1)}, f32[8,64]{1,0:T(8,128)S(1)}, u32[]{:S(2)}, u32[]{:S(2)}) collective-permute-start(f32[8,64]{1,0:T(8,128)S(1)} %pad_maximum_fusion.5), channel_id=1, source_target_pairs={{2,0},{4,2},{6,4},{0,6},{3,1},{5,3},{7,5},{1,7},{10,8},{12,10},{14... | collective-permute-start | bytes 6152 | tf_op jit(solution)/shard_map/ppermute | solution.py:172
  229.3 1.7 fusion.29
  231.8 3.8 %all-to-all-start.11 = ((f32[16,8,128]{2,1,0:T(8,128)}), f32[16,8,128]{2,1,0:T(8,128)S(1)}, u32[]{:S(2)}, u32[]{:S(2)}) async-start(f32[16,8,128]{2,1,0:T(8,128)} %broadcast_in_dim.38), calls=%async_computation.11 | async-start | bytes 131072 | tf_op jit(solution)/shard_map/all_to_all | solution.py:24
  235.7 7.7 %all-to-all-done.11 = f32[16,8,128]{2,1,0:T(8,128)S(1)} async-done(((f32[16,8,128]{2,1,0:T(8,128)}), f32[16,8,128]{2,1,0:T(8,128)S(1)}, u32[]{:S(2)}, u32[]{:S(2)}) %all-to-all-start.11) | async-done | bytes 65568 | tf_op jit(solution)/shard_map/all_to_all | solution.py:24
  244.1 0.9 fusion.30
  245.9 4.2 %all-to-all-start.12 = ((f32[64,8,128]{2,1,0:T(8,128)}), f32[64,8,128]{2,1,0:T(8,128)S(1)}, u32[]{:S(2)}, u32[]{:S(2)}) async-start(f32[64,8,128]{2,1,0:T(8,128)} %broadcast_in_dim.39), calls=%async_computation.12 | async-start | bytes 524288 | tf_op jit(solution)/shard_map/all_to_all | solution.py:24
  250.9 12.3 %all-to-all-done.12 = f32[64,8,128]{2,1,0:T(8,128)S(1)} async-done(((f32[64,8,128]{2,1,0:T(8,128)}), f32[64,8,128]{2,1,0:T(8,128)S(1)}, u32[]{:S(2)}, u32[]{:S(2)}) %all-to-all-start.12) | async-done | bytes 262176 | tf_op jit(solution)/shard_map/all_to_all | solution.py:24
  263.9 3.3 %shard_map.149 = (f32[32,256]{1,0:T(8,128)}, f32[32,2048]{1,0:T(8,128)}) custom-call(s32[2]{0:T(128)} %parents.3, s32[2]{0:T(128)} %targets.3, s32[1]{0:T(128)S(6)} %copy.101.live, f32[8,4,2,8,128]{4,3,2,1,0:T(8,128)} %bitcast.79, f32[32,256]{1,0:T(8,128)} %get-tuple-element.41.solved, f32[2,128,128]{2,1,0:T(8,128)} %inverse.3, f32[2,128,128]{2,1,0:T(8,128)} %link.3, ...), custom_call_target="tpu_custom_call" | custom-call | tf_op jit(solution)/shard_map/pallas_call | solution.py:105
  (116 shorter events, 15.9 us)
Async XLA Ops:
  0.6 49.8 %copy-start.8 = (f32[32,32]{1,0:T(8,128)S(1)}, f32[32,32]{1,0:T(8,128)}, u32[]{:S(2)}) copy-start(f32[32,32]{1,0:T(8,128)} %param.20) | copy-start | bytes 12292
  2.3 55.9 %collective-permute-start = (f32[3,32,256]{2,1,0:T(8,128)S(1)}, f32[3,32,256]{2,1,0:T(8,128)}, u32[]{:S(2)}, u32[]{:S(2)}) collective-permute-start(f32[3,32,256]{2,1,0:T(8,128)S(1)} %constant_dynamic-update-slice_fusion), channel_id=1, source_target_pairs={{2,0},{4,2},{6,4},{0,6},{3,1},{5,3},{7,5},{1,7},{10,8},{12,10},{14... | collective-permute-start | bytes 294920 | tf_op jit(solution)/shard_map/ppermute | solution.py:172
  7.5 54.0 %collective-permute-start.1 = (f32[3,32,256]{2,1,0:T(8,128)S(1)}, f32[3,32,256]{2,1,0:T(8,128)}, u32[]{:S(2)}, u32[]{:S(2)}) collective-permute-start(f32[3,32,256]{2,1,0:T(8,128)S(1)} %constant_dynamic-update-slice_fusion), channel_id=1, source_target_pairs={{4,0},{6,2},{0,4},{2,6},{5,1},{7,3},{1,5},{3,7},{12,8},{14,10},{8,... | collective-permute-start | bytes 294920 | tf_op jit(solution)/shard_map/ppermute | solution.py:172
  9.9 51.6 %collective-permute-start.2 = (f32[3,32,256]{2,1,0:T(8,128)S(1)}, f32[3,32,256]{2,1,0:T(8,128)}, u32[]{:S(2)}, u32[]{:S(2)}) collective-permute-start(f32[3,32,256]{2,1,0:T(8,128)S(1)} %constant_dynamic-update-slice_fusion), channel_id=1, source_target_pairs={{6,0},{0,2},{2,4},{4,6},{7,1},{1,3},{3,5},{5,7},{14,8},{8,10},{10,... | collective-permute-start | bytes 294920 | tf_op jit(solution)/shard_map/ppermute | solution.py:172
  12.4 73.9 %collective-permute-start.6 = (f32[32,2048]{1,0:T(8,128)}, f32[32,2048]{1,0:T(8,128)S(1)}, u32[]{:S(2)}, u32[]{:S(2)}) collective-permute-start(f32[32,2048]{1,0:T(8,128)} %param.21), channel_id=1, source_target_pairs={{2,0},{4,2},{6,4},{0,6},{3,1},{5,3},{7,5},{1,7},{10,8},{12,10},{14... | collective-permute-start | bytes 786440 | tf_op jit(solution)/shard_map/ppermute | solution.py:172
  16.4 73.2 %collective-permute-start.7 = (f32[32,2048]{1,0:T(8,128)}, f32[32,2048]{1,0:T(8,128)}, u32[]{:S(2)}, u32[]{:S(2)}) collective-permute-start(f32[32,2048]{1,0:T(8,128)} %param.21), channel_id=1, source_target_pairs={{4,0},{6,2},{0,4},{2,6},{5,1},{7,3},{1,5},{3,7},{12,8},{14,10},{8,... | collective-permute-start | bytes 786440 | tf_op jit(solution)/shard_map/ppermute | solution.py:172
  22.8 27.5 %all-to-all-start = ((f32[64,8,128]{2,1,0:T(8,128)}), f32[64,8,128]{2,1,0:T(8,128)S(1)}, u32[]{:S(2)}, u32[]{:S(2)}) async-start(f32[64,8,128]{2,1,0:T(8,128)} %get-tuple-element.28), calls=%async_computation | async-start | bytes 524288 | tf_op jit(solution)/shard_map/all_to_all | solution.py:24
  51.8 6.4 %copy-start.7 = (f32[32,2,32]{2,1,0:T(2,128)S(1)}, f32[32,2,32]{2,1,0:T(2,128)}, u32[]{:S(2)}) copy-start(f32[32,2,32]{2,1,0:T(2,128)} %param.23) | copy-start | bytes 24580
  52.5 18.9 %copy-start = (f32[32,4096]{1,0:T(8,128)S(1)}, f32[32,4096]{1,0:T(8,128)}, u32[]{:S(2)}) copy-start(f32[32,4096]{1,0:T(8,128)} %param.22) | copy-start | bytes 1572868
  53.4 17.9 %all-to-all-start.1 = ((f32[64,8,128]{2,1,0:T(8,128)}), f32[64,8,128]{2,1,0:T(8,128)S(1)}, u32[]{:S(2)}, u32[]{:S(2)}) async-start(f32[64,8,128]{2,1,0:T(8,128)} %copy.62), calls=%async_computation.1 | async-start | bytes 524288 | tf_op jit(solution)/shard_map/all_to_all | solution.py:24
  58.2 31.4 %collective-permute-start.8 = (f32[32,2048]{1,0:T(8,128)}, f32[32,2048]{1,0:T(8,128)}, u32[]{:S(2)}, u32[]{:S(2)}) collective-permute-start(f32[32,2048]{1,0:T(8,128)} %param.21), channel_id=1, source_target_pairs={{6,0},{0,2},{2,4},{4,6},{7,1},{1,3},{3,5},{5,7},{14,8},{8,10},{10,... | collective-permute-start | bytes 786440 | tf_op jit(solution)/shard_map/ppermute | solution.py:172
  73.9 42.3 %all-to-all-start.2 = ((f32[64,8,256]{2,1,0:T(8,128)}), f32[64,8,256]{2,1,0:T(8,128)S(1)}, u32[]{:S(2)}, u32[]{:S(2)}) async-start(f32[64,8,256]{2,1,0:T(8,128)} %copy.67), calls=%async_computation.2 | async-start | bytes 1048576 | tf_op jit(solution)/shard_map/all_to_all | solution.py:24
  78.7 35.7 %collective-permute-start.5 = (f32[32,4224]{1,0:T(8,128)S(1)}, f32[32,4224]{1,0:T(8,128)S(1)}, u32[]{:S(2)}, u32[]{:S(2)}) collective-permute-start(f32[32,4224]{1,0:T(8,128)S(1)} %pad_maximum_fusion.2), channel_id=1, source_target_pairs={{6,0},{0,2},{2,4},{4,6},{7,1},{1,3},{3,5},{5,7},{14,8},{8,10},{10,... | collective-permute-start | bytes 1622024 | tf_op jit(solution)/shard_map/ppermute | solution.py:172
  82.0 31.6 %collective-permute-start.4 = (f32[32,4224]{1,0:T(8,128)S(1)}, f32[32,4224]{1,0:T(8,128)S(1)}, u32[]{:S(2)}, u32[]{:S(2)}) collective-permute-start(f32[32,4224]{1,0:T(8,128)S(1)} %pad_maximum_fusion.2), channel_id=1, source_target_pairs={{4,0},{6,2},{0,4},{2,6},{5,1},{7,3},{1,5},{3,7},{12,8},{14,10},{8,... | collective-permute-start | bytes 1622024 | tf_op jit(solution)/shard_map/ppermute | solution.py:172
  86.3 3.2 %copy-start.6 = (f32[32,2048]{1,0:T(8,128)}, f32[32,2048]{1,0:T(8,128)S(1)}, u32[]{:S(2)}) copy-start(f32[32,2048]{1,0:T(8,128)S(1)} %collective-permute-done.6) | copy-start | bytes 786436
  86.3 26.3 %collective-permute-start.3 = (f32[32,4224]{1,0:T(8,128)S(1)}, f32[32,4224]{1,0:T(8,128)S(1)}, u32[]{:S(2)}, u32[]{:S(2)}) collective-permute-start(f32[32,4224]{1,0:T(8,128)S(1)} %pad_maximum_fusion.2), channel_id=1, source_target_pairs={{2,0},{4,2},{6,4},{0,6},{3,1},{5,3},{7,5},{1,7},{10,8},{12,10},{14... | collective-permute-start | bytes 1622024 | tf_op jit(solution)/shard_map/ppermute | solution.py:172
  112.7 1.8 copy-start.5
  113.6 1.0 copy-start.4
  114.5 0.8 copy-start.3
  116.9 14.0 %all-to-all-start.3 = ((f32[8,8,256]{2,1,0:T(8,128)}), f32[8,8,256]{2,1,0:T(8,128)S(1)}, u32[]{:S(2)}, u32[]{:S(2)}) async-start(f32[8,8,256]{2,1,0:T(8,128)} %broadcast_in_dim.30), calls=%async_computation.3 | async-start | bytes 131072 | tf_op jit(solution)/shard_map/all_to_all | solution.py:24
  123.7 13.6 %slice-start = ((f32[32,4224]{1,0:T(8,128)}), f32[32,128]{1,0:T(8,128)S(1)}, s32[]{:S(2)}) async-start(f32[32,4224]{1,0:T(8,128)} %copy-done.3), calls=%async_computation.13 | async-start | bytes 32768 | tf_op jit(solution)/shard_map/slice | solution.py:231
  123.7 24.8 %slice-start.1 = ((f32[32,4224]{1,0:T(8,128)}), f32[32,128]{1,0:T(8,128)S(1)}, s32[]{:S(2)}) async-start(f32[32,4224]{1,0:T(8,128)} %copy-done.4), calls=%async_computation.14 | async-start | bytes 32768 | tf_op jit(solution)/shard_map/slice | solution.py:231
  123.7 35.8 %slice-start.2 = ((f32[32,4224]{1,0:T(8,128)}), f32[32,128]{1,0:T(8,128)S(1)}, s32[]{:S(2)}) async-start(f32[32,4224]{1,0:T(8,128)} %copy-done.5), calls=%async_computation.15 | async-start | bytes 32768 | tf_op jit(solution)/shard_map/slice | solution.py:231
  131.9 12.3 %all-to-all-start.4 = ((f32[8,4,256]{2,1,0:T(4,128)}), f32[8,4,256]{2,1,0:T(4,128)S(1)}, u32[]{:S(2)}, u32[]{:S(2)}) async-start(f32[8,4,256]{2,1,0:T(4,128)} %broadcast_in_dim.31), calls=%async_computation.4 | async-start | bytes 65536 | tf_op jit(solution)/shard_map/all_to_all | solution.py:24
  145.1 10.1 %all-to-all-start.5 = ((f32[8,4,256]{2,1,0:T(4,128)}), f32[8,4,256]{2,1,0:T(4,128)S(1)}, u32[]{:S(2)}, u32[]{:S(2)}) async-start(f32[8,4,256]{2,1,0:T(4,128)} %broadcast_in_dim.32), calls=%async_computation.5 | async-start | bytes 65536 | tf_op jit(solution)/shard_map/all_to_all | solution.py:24
  156.2 10.1 %all-to-all-start.6 = ((f32[8,4,256]{2,1,0:T(4,128)}), f32[8,4,256]{2,1,0:T(4,128)S(1)}, u32[]{:S(2)}, u32[]{:S(2)}) async-start(f32[8,4,256]{2,1,0:T(4,128)} %broadcast_in_dim.33), calls=%async_computation.6 | async-start | bytes 65536 | tf_op jit(solution)/shard_map/all_to_all | solution.py:24
  167.3 10.1 %all-to-all-start.7 = ((f32[8,4,256]{2,1,0:T(4,128)}), f32[8,4,256]{2,1,0:T(4,128)S(1)}, u32[]{:S(2)}, u32[]{:S(2)}) async-start(f32[8,4,256]{2,1,0:T(4,128)} %broadcast_in_dim.34), calls=%async_computation.7 | async-start | bytes 65536 | tf_op jit(solution)/shard_map/all_to_all | solution.py:24
  218.1 26.1 %copy-start.1 = (f32[128,2048]{1,0:T(8,128)S(1)}, f32[128,2048]{1,0:T(8,128)}, u32[]{:S(2)}) copy-start(f32[128,2048]{1,0:T(8,128)} %pad_maximum_fusion.1) | copy-start | bytes 3145732
  218.4 17.3 %collective-permute-start.11 = (f32[8,64]{1,0:T(8,128)S(1)}, f32[8,64]{1,0:T(8,128)S(1)}, u32[]{:S(2)}, u32[]{:S(2)}) collective-permute-start(f32[8,64]{1,0:T(8,128)S(1)} %pad_maximum_fusion.7), channel_id=1, source_target_pairs={{6,0},{0,2},{2,4},{4,6},{7,1},{1,3},{3,5},{5,7},{14,8},{8,10},{10,... | collective-permute-start | bytes 6152 | tf_op jit(solution)/shard_map/ppermute | solution.py:172
  222.5 13.2 %collective-permute-start.10 = (f32[8,64]{1,0:T(8,128)S(1)}, f32[8,64]{1,0:T(8,128)S(1)}, u32[]{:S(2)}, u32[]{:S(2)}) collective-permute-start(f32[8,64]{1,0:T(8,128)S(1)} %pad_maximum_fusion.6), channel_id=1, source_target_pairs={{4,0},{6,2},{0,4},{2,6},{5,1},{7,3},{1,5},{3,7},{12,8},{14,10},{8,... | collective-permute-start | bytes 6152 | tf_op jit(solution)/shard_map/ppermute | solution.py:172
  226.1 9.5 %collective-permute-start.9 = (f32[8,64]{1,0:T(8,128)S(1)}, f32[8,64]{1,0:T(8,128)S(1)}, u32[]{:S(2)}, u32[]{:S(2)}) collective-permute-start(f32[8,64]{1,0:T(8,128)S(1)} %pad_maximum_fusion.5), channel_id=1, source_target_pairs={{2,0},{4,2},{6,4},{0,6},{3,1},{5,3},{7,5},{1,7},{10,8},{12,10},{14... | collective-permute-start | bytes 6152 | tf_op jit(solution)/shard_map/ppermute | solution.py:172
  231.8 11.6 %all-to-all-start.11 = ((f32[16,8,128]{2,1,0:T(8,128)}), f32[16,8,128]{2,1,0:T(8,128)S(1)}, u32[]{:S(2)}, u32[]{:S(2)}) async-start(f32[16,8,128]{2,1,0:T(8,128)} %broadcast_in_dim.38), calls=%async_computation.11 | async-start | bytes 131072 | tf_op jit(solution)/shard_map/all_to_all | solution.py:24
  245.9 17.4 %all-to-all-start.12 = ((f32[64,8,128]{2,1,0:T(8,128)}), f32[64,8,128]{2,1,0:T(8,128)S(1)}, u32[]{:S(2)}, u32[]{:S(2)}) async-start(f32[64,8,128]{2,1,0:T(8,128)} %broadcast_in_dim.39), calls=%async_computation.12 | async-start | bytes 524288 | tf_op jit(solution)/shard_map/all_to_all | solution.py:24
  263.2 0.7 copy-start.2
